TPU v7x, 32 devices: a whole 2x2x4 slice. The times are simulated.
32 devices in a mesh: nest: 2 (over core), rows: 8 (over z, x), sub: 2 (over y).
Axes of the slice: x: 2, y: 2, z: 4, core: 2. Of those that a mesh axis runs over, the one named last changes fastest.
Arguments:
- elevation: float32 [2, 1024, 1024], P('nest', ('rows', 'sub')), may hold values from -6 to 6
- momentum_x: float32 [2, 1024, 1024], P('nest', ('rows', 'sub')), may hold values from -6 to 6
- momentum_y: float32 [2, 1024, 1024], P('nest', ('rows', 'sub')), may hold values from -6 to 6
- depth: float32 [2, 1024, 1024], P('nest', ('rows', 'sub')), may hold values from 0.2 to 1
- wet_mask: int32 [2, 1024, 1024], P('nest', ('rows', 'sub')), may hold values 0 or 1
- inverse_x: float32 [2, 8, 128, 128], P('nest'), may hold values from -1 to 2, as said below
- inverse_y: float32 [2, 8, 128, 128], P('nest'), may hold values from -1 to 2, as said below
- nest_map: int32 [2, 2, 1024], replicated, may hold values from 0 to 1023, as said below
Outputs:
- elevation_out: float32 [2, 1024, 1024], P('nest', ('rows', 'sub'))
- momentum_x_out: float32 [2, 1024, 1024], P('nest', ('rows', 'sub'))
- momentum_y_out: float32 [2, 1024, 1024], P('nest', ('rows', 'sub'))
Inputs may be any that keep to these rules, and one draw needn't show every extreme that they name: nest_map[b, 0, j] is the regional row and nest_map[b, 1, j] the regional column for cell j of the near-field's first (b = 0) or last (b = 1) row; the first row is driven by regional row 0 and the last by regional row 1023, and the column is c0 + j // 2 for one offset c0 shared by both rows, with every column below 1024. `inverse_x`: dense blocks, one for each line block of a section. `inverse_y`: dense blocks, one for each line block of a section.
All inputs are finite; a program needn't handle non-finite values. No bound on the sum of `wet_mask` on one device may be relied on, other than what follows from the above.
Results may differ from a plain program's by a relative error of at most 0.00013.
Values sent between devices are 32-bit elements; how exact they have to be, the bound alone decides.
No kernel may reach another device: no remote copies, remote signals or barrier semaphores. Data moves between devices by JAX's collectives and lax.ppermute only.
A program may use at most 64 MiB of HBM per device.

v0:
```python
import jax
import jax.numpy as jnp
from jax import lax
from jax.sharding import PartitionSpec as P

STEPS = 2


step_ratio = 0.5
dispersion = 0.5
nest_blend = 0.5


def from_behind(value, axis, steps):
    count = lax.axis_size(axis)
    leading, last = (max(0, -steps), min(count, count - steps))
    return lax.ppermute(value, axis, [(source, source + steps) for source in range(leading, last)])


def redistribute(blocks):
    return lax.all_to_all(blocks, ("rows", "sub"), split_axis=0, concat_axis=0, tiled=True)


def to_lines(field):
    rows_here, width = field.shape
    count = lax.axis_size(("rows", "sub"))
    blocks = field.reshape(rows_here, count, width // count).transpose(1, 0, 2)
    moved = redistribute(blocks)
    return moved.reshape(count * rows_here, width // count).T


def from_lines(lines):
    line_width, total_rows = lines.shape
    count = lax.axis_size(("rows", "sub"))
    rows_here = total_rows // count
    blocks = lines.T.reshape(count, rows_here, line_width)
    moved = redistribute(blocks)
    return moved.transpose(1, 0, 2).reshape(rows_here, count * line_width)


def operate_last(field, coef):
    right = jnp.pad(field[:, 1:], ((0, 0), (0, 1)))
    left = jnp.pad(field[:, :-1], ((0, 0), (1, 0)))
    coef_left = jnp.pad(coef[:, :-1], ((0, 0), (1, 0)))
    return field + coef * (field - right) + coef_left * (field - left)


def apply_blocks(field, tables):
    leading, length = field.shape
    group = tables.shape[-1]
    split = field.reshape(leading, length // group, group)
    result = jnp.einsum(
        "kij,rkj->rki",
        tables,
        split,
        precision=lax.Precision.HIGHEST,
        preferred_element_type=jnp.float32,
    )
    return result.reshape(leading, length)


def on_device(elevation, momentum_x, momentum_y, depth, wet_mask, inverse_x, inverse_y, nest_map):
    height = elevation[0]
    flow_x = momentum_x[0]
    flow_y = momentum_y[0]
    depth_here = depth[0]
    wetness = wet_mask[0].astype(jnp.float32)
    rows_here, width = height.shape
    total_rows = lax.axis_size(("rows", "sub")) * rows_here
    tables_x = inverse_x[0]
    tables_y = inverse_y[0]
    start = lax.axis_index(("rows", "sub")) * rows_here
    regional = lax.axis_index("nest") == 0
    nearfield = lax.axis_index("nest") == 1
    global_rows = start + lax.iota(jnp.int32, rows_here)
    top_row = jnp.logical_and(nearfield, global_rows == 0)[:, None]
    bottom_row = jnp.logical_and(nearfield, global_rows == total_rows - 1)[:, None]
    face_x = wetness[:, :-1] * wetness[:, 1:] * (0.5 * (depth_here[:, :-1] + depth_here[:, 1:]))
    face_x = jnp.pad(face_x, ((0, 0), (0, 1)))
    coef_x = dispersion * face_x * face_x
    face_y = jnp.zeros_like(height)
    coef_y = jnp.zeros_like(height)
    coef_lines = jnp.zeros_like(height)
    for step in range(STEPS):
        below = from_behind(jnp.stack([height[0], depth_here[0], wetness[0]]), ("rows", "sub"), -1)
        if step == 0:
            depth_next = jnp.concatenate([depth_here[1:], below[1:2]], 0)
            wet_next = jnp.concatenate([wetness[1:], below[2:3]], 0)
            face_y = wetness * wet_next * (0.5 * (depth_here + depth_next))
            coef_y = dispersion * face_y * face_y
            coef_lines = to_lines(coef_y)
        south = jnp.concatenate([height[1:], below[0:1]], 0)
        east = jnp.pad(height[:, 1:], ((0, 0), (0, 1)))
        push_x = flow_x + step_ratio * face_x * (east - height)
        push_y = flow_y + step_ratio * face_y * (south - height)
        first_x = apply_blocks(push_x, tables_x)
        flow_x = first_x + apply_blocks(push_x - operate_last(first_x, coef_x), tables_x)
        lines = to_lines(push_y)
        first_y = apply_blocks(lines, tables_y)
        flow_y = from_lines(
            first_y + apply_blocks(lines - operate_last(first_y, coef_lines), tables_y)
        )
        flux_x = face_x * flow_x
        flux_y = face_y * flow_y
        west = jnp.pad(flux_x[:, :-1], ((0, 0), (1, 0)))
        above = from_behind(flux_y[-1:], ("rows", "sub"), 1)
        north = jnp.concatenate([above, flux_y[:-1]], 0)
        height = height + step_ratio * (flux_x - west + flux_y - north)
        local_rows = nest_map[:, 0, :] - start
        owned = jnp.logical_and(jnp.logical_and(local_rows >= 0, local_rows < rows_here), regional)
        picked = height[jnp.clip(local_rows, 0, rows_here - 1), nest_map[:, 1, :]]
        packet = lax.psum(jnp.where(owned, picked, 0.0), ("nest", "rows", "sub"))
        blended_top = nest_blend * height + (1.0 - nest_blend) * packet[0][None, :]
        blended_bottom = nest_blend * height + (1.0 - nest_blend) * packet[1][None, :]
        height = jnp.where(top_row, blended_top, jnp.where(bottom_row, blended_bottom, height))
    return (height[None], flow_x[None], flow_y[None])


def solution(mesh):
    in_specs = (
        P("nest", ("rows", "sub"), None),
        P("nest", ("rows", "sub"), None),
        P("nest", ("rows", "sub"), None),
        P("nest", ("rows", "sub"), None),
        P("nest", ("rows", "sub"), None),
        P("nest", None, None, None),
        P("nest", None, None, None),
        P(),
    )
    out_specs = (
        P("nest", ("rows", "sub"), None),
        P("nest", ("rows", "sub"), None),
        P("nest", ("rows", "sub"), None),
    )
    return jax.shard_map(
        on_device, mesh=mesh, in_specs=in_specs, out_specs=out_specs, check_vma=False
    )
```

profile of v0, /device:TPU:0, one launch (start us, length us, event | category | flops | bytes accessed | tf_op | source)
XLA Modules:
  0.0 247.4 jit_solution(11802230985280122733)
XLA Ops:
  0.7 1.1 convert_bitcast_fusion
  1.8 1.3 collective-permute-start
  3.1 0.9 slice_bitcast_fusion.3
  4.4 0.9 squeeze.34
  5.5 1.0 concatenate.45
  6.5 0.9 concatenate.48
  7.4 0.9 concatenate.51
  8.5 0.8 slice.195
  9.6 1.6 fusion.2
  11.5 1.0 reshape.253
  12.6 9.6 %all-to-all-start = ((f32[16,1,4096]{2,1,0:T(1,128)}), f32[16,1,4096]{2,1,0:T(1,128)S(1)}, u32[]{:S(2)}, u32[]{:S(2)}) async-start(f32[16,1,4096]{2,1,0:T(1,128)} %reshape.253), calls=%async_computation | async-start | bytes 524288 | tf_op jit(solution)/shard_map/all_to_all | solution.py:21
  23.0 1.1 convolution_bitcast_fusion.5
  24.1 0.9 fusion.58
  25.2 1.0 reshape.255
  26.2 5.5 %all-to-all-done = f32[16,1,4096]{2,1,0:T(1,128)S(1)} async-done(((f32[16,1,4096]{2,1,0:T(1,128)}), f32[16,1,4096]{2,1,0:T(1,128)S(1)}, u32[]{:S(2)}, u32[]{:S(2)}) %all-to-all-start) | async-done | bytes 262176 | tf_op jit(solution)/shard_map/all_to_all | solution.py:21
  31.8 4.2 %all-to-all-start.1 = ((f32[16,1,4096]{2,1,0:T(1,128)}), f32[16,1,4096]{2,1,0:T(1,128)}, u32[]{:S(2)}, u32[]{:S(2)}) async-start(f32[16,1,4096]{2,1,0:T(1,128)} %reshape.255), calls=%async_computation.1 | async-start | bytes 524288 | tf_op jit(solution)/shard_map/all_to_all | solution.py:21
  36.5 1.3 reduce.12
  37.8 1.0 reshape.254
  38.8 1.3 copy.88
  40.1 1.1 convolution_bitcast_fusion.3
  41.3 0.8 fusion.59
  42.0 2.4 all-to-all-done.1
  44.4 2.2 reduce.13
  46.7 1.0 reshape.256
  47.7 1.2 copy.89
  48.9 2.2 convolution_bitcast_fusion.2
  51.2 1.0 copy.191
  52.2 2.1 reshape.257
  54.2 4.6 %all-to-all-start.2 = ((f32[16,1,4096]{2,1,0:T(1,128)}), f32[16,1,4096]{2,1,0:T(1,128)S(1)}, u32[]{:S(2)}, u32[]{:S(2)}) async-start(f32[16,1,4096]{2,1,0:T(1,128)} %reshape.257), calls=%async_computation.2 | async-start | bytes 524288 | tf_op jit(solution)/shard_map/all_to_all | solution.py:21
  58.8 2.2 convolution_bitcast_fusion.4
  61.8 5.5 %all-to-all-done.2 = f32[16,1,4096]{2,1,0:T(1,128)S(1)} async-done(((f32[16,1,4096]{2,1,0:T(1,128)}), f32[16,1,4096]{2,1,0:T(1,128)S(1)}, u32[]{:S(2)}, u32[]{:S(2)}) %all-to-all-start.2) | async-done | bytes 262176 | tf_op jit(solution)/shard_map/all_to_all | solution.py:21
  67.3 1.3 reduce.14
  68.5 1.0 reshape.258
  69.6 1.2 copy.90
  70.8 1.3 fusion.53
  72.1 3.4 %collective-permute-start.1 = (f32[1,1024]{1,0:T(1,128)S(1)}, f32[1,1024]{1,0:T(1,128)S(1)}, u32[]{:S(2)}, u32[]{:S(2)}) collective-permute-start(f32[1,1024]{1,0:T(1,128)S(1)} %slice.208), channel_id=1, source_target_pairs={{0,1},{1,2},{2,3},{3,4},{4,5},{5,6},{6,7},{7,8},{8,9},{9,10},{10,1... | collective-permute-start | bytes 12296 | tf_op jit(solution)/shard_map/ppermute | solution.py:17
  75.5 1.3 collective-permute-done.1
  76.9 16.6 %gather_fusion = f32[2048]{0:T(1024)S(1)} fusion(f32[64,1024]{1,0:T(8,128)S(1)} %fusion.41, s32[2048]{0:T(1024)S(1)} %bitcast.265), kind=kCustom, calls=%fused_computation | custom fusion | bytes 32768 | tf_op jit(solution)/shard_map/gather | solution.py:111
  93.6 41.4 %psum.14 = f32[2,1024]{1,0:T(2,128)S(1)} all-reduce(f32[2,1024]{1,0:T(2,128)S(1)} %bitcast_select_fusion.1), channel_id=1, replica_groups=mesh['nest'=2,'rows'=8,'sub'=2] {'nest','rows','sub'}, use_global_device_ids=true, to_apply=%region_0.1 | all-reduce | flops 2048 | bytes 16384 | tf_op jit(solution)/shard_map/psum | solution.py:112
  135.2 1.3 collective-permute-start.2
  136.7 4.4 %collective-permute-done.2 = f32[3,1024]{1,0:T(4,128)S(1)} collective-permute-done((f32[3,1024]{1,0:T(4,128)S(1)}, f32[3,1024]{1,0:T(4,128)S(1)}, u32[]{:S(2)}, u32[]{:S(2)}) %collective-permute-start.2) | collective-permute-done | bytes 12320 | tf_op jit(solution)/shard_map/ppermute | solution.py:17
  141.2 1.0 fusion.16
  142.1 2.0 copy.91
  144.2 2.1 reshape.259
  146.2 5.7 %all-to-all-start.3 = ((f32[16,1,4096]{2,1,0:T(1,128)}), f32[16,1,4096]{2,1,0:T(1,128)S(1)}, u32[]{:S(2)}, u32[]{:S(2)}) async-start(f32[16,1,4096]{2,1,0:T(1,128)} %reshape.259), calls=%async_computation.3 | async-start | bytes 524288 | tf_op jit(solution)/shard_map/all_to_all | solution.py:21
  151.9 1.1 fusion.11
  153.1 7.3 %all-to-all-done.3 = f32[16,1,4096]{2,1,0:T(1,128)S(1)} async-done(((f32[16,1,4096]{2,1,0:T(1,128)}), f32[16,1,4096]{2,1,0:T(1,128)S(1)}, u32[]{:S(2)}, u32[]{:S(2)}) %all-to-all-start.3) | async-done | bytes 262176 | tf_op jit(solution)/shard_map/all_to_all | solution.py:21
  160.4 1.3 reduce.15
  161.6 1.0 reshape.260
  162.6 2.1 copy.79
  164.8 1.2 reshape.217
  166.0 1.1 convolution_bitcast_fusion.1
  167.3 1.2 convolution_bitcast_fusion
  168.8 1.0 reshape.261
  169.8 3.5 %all-to-all-start.4 = ((f32[16,1,4096]{2,1,0:T(1,128)}), f32[16,1,4096]{2,1,0:T(1,128)S(1)}, u32[]{:S(2)}, u32[]{:S(2)}) async-start(f32[16,1,4096]{2,1,0:T(1,128)} %reshape.261), calls=%async_computation.4 | async-start | bytes 524288 | tf_op jit(solution)/shard_map/all_to_all | solution.py:21
  173.5 0.8 copy-done.5
  174.3 1.9 bitcast_add_fusion.4
  176.2 5.6 %all-to-all-done.4 = f32[16,1,4096]{2,1,0:T(1,128)S(1)} async-done(((f32[16,1,4096]{2,1,0:T(1,128)}), f32[16,1,4096]{2,1,0:T(1,128)S(1)}, u32[]{:S(2)}, u32[]{:S(2)}) %all-to-all-start.4) | async-done | bytes 262176 | tf_op jit(solution)/shard_map/all_to_all | solution.py:21
  181.9 1.3 reduce.16
  183.6 3.5 %collective-permute-start.3 = (f32[1,1024]{1,0:T(1,128)S(1)}, f32[1,1024]{1,0:T(1,128)S(1)}, u32[]{:S(2)}, u32[]{:S(2)}) collective-permute-start(f32[1,1024]{1,0:T(1,128)S(1)} %slice.221), channel_id=1, source_target_pairs={{0,1},{1,2},{2,3},{3,4},{4,5},{5,6},{6,7},{7,8},{8,9},{9,10},{10,1... | collective-permute-start | bytes 12296 | tf_op jit(solution)/shard_map/ppermute | solution.py:17
  188.1 0.9 copy.93
  189.2 16.6 %gather_fusion.1 = f32[2048]{0:T(1024)S(1)} fusion(f32[64,1024]{1,0:T(8,128)S(1)} %fusion.45, s32[2048]{0:T(1024)S(1)} %bitcast.266), kind=kCustom, calls=%fused_computation.1 | custom fusion | bytes 32768 | tf_op jit(solution)/shard_map/gather | solution.py:111
  205.9 40.7 %psum.15 = f32[2,1024]{1,0:T(2,128)S(1)} all-reduce(f32[2,1024]{1,0:T(2,128)S(1)} %bitcast_select_fusion), channel_id=1, replica_groups=mesh['nest'=2,'rows'=8,'sub'=2] {'nest','rows','sub'}, use_global_device_ids=true, to_apply=%region_1.2 | all-reduce | flops 2048 | bytes 16384 | tf_op jit(solution)/shard_map/psum | solution.py:112
  246.5 0.9 select_bitcast_fusion
  (85 shorter events, 6.6 us)
Async XLA Ops:
  0.6 22.3 %copy-start = (f32[1,8,128,128]{3,2,1,0:T(8,128)S(1)}, f32[1,8,128,128]{3,2,1,0:T(8,128)}, u32[]{:S(2)}) copy-start(f32[1,8,128,128]{3,2,1,0:T(8,128)} %param.13) | copy-start | bytes 1572868
  0.6 1.1 copy-start.3
  0.7 1.2 copy-start.2
  1.8 7.5 %collective-permute-start = (f32[3,1024]{1,0:T(4,128)S(1)}, f32[3,1024]{1,0:T(4,128)S(1)}, u32[]{:S(2)}, u32[]{:S(2)}) collective-permute-start(f32[3,1024]{1,0:T(4,128)S(1)} %pad_maximum_fusion.1), channel_id=1, source_target_pairs={{1,0},{2,1},{3,2},{4,3},{5,4},{6,5},{7,6},{8,7},{9,8},{10,9},{11,1... | collective-permute-start | bytes 36872 | tf_op jit(solution)/shard_map/ppermute | solution.py:17
  7.4 0.9 copy-start.12
  9.6 1.6 copy-start.9
  12.6 9.6 %copy-start.11 = (f32[64,1023]{1,0:T(8,128)S(1)}, f32[64,1023]{1,0:T(8,128)}, u32[]{:S(2)}) copy-start(f32[64,1023]{1,0:T(8,128)} %slice.195) | copy-start | bytes 785668
  12.6 9.6 %copy-start.13 = (f32[1,64,1024]{2,1,0:T(8,128)S(1)}, f32[1,64,1024]{2,1,0:T(8,128)}, u32[]{:S(2)}) copy-start(f32[1,64,1024]{2,1,0:T(8,128)} %param.9) | copy-start | bytes 786436
  12.6 19.2 %all-to-all-start = ((f32[16,1,4096]{2,1,0:T(1,128)}), f32[16,1,4096]{2,1,0:T(1,128)S(1)}, u32[]{:S(2)}, u32[]{:S(2)}) async-start(f32[16,1,4096]{2,1,0:T(1,128)} %reshape.253), calls=%async_computation | async-start | bytes 524288 | tf_op jit(solution)/shard_map/all_to_all | solution.py:21
  22.3 0.7 copy-start.6
  26.2 9.7 %copy-start.14 = (s32[2,2,1024]{2,1,0:T(2,128)S(1)}, s32[2,2,1024]{2,1,0:T(2,128)}, u32[]{:S(2)}) copy-start(s32[2,2,1024]{2,1,0:T(2,128)} %param.15) | copy-start | bytes 49156
  31.8 12.7 %all-to-all-start.1 = ((f32[16,1,4096]{2,1,0:T(1,128)}), f32[16,1,4096]{2,1,0:T(1,128)}, u32[]{:S(2)}, u32[]{:S(2)}) async-start(f32[16,1,4096]{2,1,0:T(1,128)} %reshape.255), calls=%async_computation.1 | async-start | bytes 524288 | tf_op jit(solution)/shard_map/all_to_all | solution.py:21
  38.8 1.3 copy-start.1
  54.2 4.6 %copy-start.7 = (f32[64,1024]{1,0:T(8,128)S(1)}, f32[64,1024]{1,0:T(8,128)}, u32[]{:S(2)}) copy-start(f32[64,1024]{1,0:T(8,128)} %copy-done.6) | copy-start | bytes 786436
  54.2 13.0 %all-to-all-start.2 = ((f32[16,1,4096]{2,1,0:T(1,128)}), f32[16,1,4096]{2,1,0:T(1,128)S(1)}, u32[]{:S(2)}, u32[]{:S(2)}) async-start(f32[16,1,4096]{2,1,0:T(1,128)} %reshape.257), calls=%async_computation.2 | async-start | bytes 524288 | tf_op jit(solution)/shard_map/all_to_all | solution.py:21
  70.8 6.0 %copy-start.8 = (f32[64,1024]{1,0:T(8,128)S(1)}, f32[64,1024]{1,0:T(8,128)}, u32[]{:S(2)}) copy-start(f32[64,1024]{1,0:T(8,128)} %pad_multiply_fusion) | copy-start | bytes 786436
  72.1 4.7 %collective-permute-start.1 = (f32[1,1024]{1,0:T(1,128)S(1)}, f32[1,1024]{1,0:T(1,128)S(1)}, u32[]{:S(2)}, u32[]{:S(2)}) collective-permute-start(f32[1,1024]{1,0:T(1,128)S(1)} %slice.208), channel_id=1, source_target_pairs={{0,1},{1,2},{2,3},{3,4},{4,5},{5,6},{6,7},{7,8},{8,9},{9,10},{10,1... | collective-permute-start | bytes 12296 | tf_op jit(solution)/shard_map/ppermute | solution.py:17
  135.2 5.9 %collective-permute-start.2 = (f32[3,1024]{1,0:T(4,128)S(1)}, f32[3,1024]{1,0:T(4,128)S(1)}, u32[]{:S(2)}, u32[]{:S(2)}) collective-permute-start(f32[3,1024]{1,0:T(4,128)S(1)} %pad_maximum_fusion), channel_id=1, source_target_pairs={{1,0},{2,1},{3,2},{4,3},{5,4},{6,5},{7,6},{8,7},{9,8},{10,9},{11,1... | collective-permute-start | bytes 36872 | tf_op jit(solution)/shard_map/ppermute | solution.py:17
  142.1 9.8 %copy-start.4 = (f32[64,1024]{1,0:T(8,128)}, f32[64,1024]{1,0:T(8,128)S(1)}, u32[]{:S(2)}) copy-start(f32[64,1024]{1,0:T(8,128)S(1)} %get-tuple-element.12) | copy-start | bytes 786436
  146.2 14.1 %all-to-all-start.3 = ((f32[16,1,4096]{2,1,0:T(1,128)}), f32[16,1,4096]{2,1,0:T(1,128)S(1)}, u32[]{:S(2)}, u32[]{:S(2)}) async-start(f32[16,1,4096]{2,1,0:T(1,128)} %reshape.259), calls=%async_computation.3 | async-start | bytes 524288 | tf_op jit(solution)/shard_map/all_to_all | solution.py:21
  169.8 12.0 %all-to-all-start.4 = ((f32[16,1,4096]{2,1,0:T(1,128)}), f32[16,1,4096]{2,1,0:T(1,128)S(1)}, u32[]{:S(2)}, u32[]{:S(2)}) async-start(f32[16,1,4096]{2,1,0:T(1,128)} %reshape.261), calls=%async_computation.4 | async-start | bytes 524288 | tf_op jit(solution)/shard_map/all_to_all | solution.py:21
  173.4 1.0 copy-start.5
  183.5 3.6 %copy-start.10 = (f32[8,64,128]{2,1,0:T(8,128)S(1)}, f32[8,64,128]{2,1,0:T(8,128)}, u32[]{:S(2)}) copy-start(f32[8,64,128]{2,1,0:T(8,128)} %get-tuple-element.35) | copy-start | bytes 786436
  183.6 5.4 %collective-permute-start.3 = (f32[1,1024]{1,0:T(1,128)S(1)}, f32[1,1024]{1,0:T(1,128)S(1)}, u32[]{:S(2)}, u32[]{:S(2)}) collective-permute-start(f32[1,1024]{1,0:T(1,128)S(1)} %slice.221), channel_id=1, source_target_pairs={{0,1},{1,2},{2,3},{3,4},{4,5},{5,6},{6,7},{7,8},{8,9},{9,10},{10,1... | collective-permute-start | bytes 12296 | tf_op jit(solution)/shard_map/ppermute | solution.py:17
where the time goes:
time: 249 us; the launch traced here: 247 us
  blocking collectives  82.1 us (33%)
  local copies, waits for them, and re-layouts  68.1 us (27%)
  starting transfers between devices  37 us (15%)
  waiting for transfers between devices  32.1 us (13%)
  other arithmetic  15.1 us (6%)
  matrix products  11.9 us (5%)
    psum x2, blocking collectives, on_device(): packet = lax.psum(jnp.where(owned, picked, 0.0), ('nest', 'rows', 'sub'))  82.1 us
    gather x4, local copies, waits for them, and re-layouts, on_device(): picked = height[jnp.clip(local_rows, 0, rows_here - 1), nest_map[:, 1, :]]  33.3 us
    all_to_all x5, starting transfers between devices, redistribute(): lax.all_to_all(blocks, ('rows', 'sub'), split_axis=0, concat_axis=0, tile...  27.5 us
    all_to_all x5, waiting for transfers between devices, redistribute(): lax.all_to_all(blocks, ('rows', 'sub'), split_axis=0, concat_axis=0, tile...  26.3 us
    unnamed x40, local copies, waits for them, and re-layouts  13.1 us
    dot_general x8, matrix products, apply_blocks(): jnp.einsum('kij,rkj->rki', tables, split, precision=lax.Precision.HIGHEST...  11.9 us
    ppermute x4, starting transfers between devices, from_behind(): lax.ppermute(value, axis, [(source, source + steps) for source in range(l...  9.45 us
    all_to_all x5, other arithmetic, redistribute(): lax.all_to_all(blocks, ('rows', 'sub'), split_axis=0, concat_axis=0, tile...  7.24 us
  transfers between devices with their start and end apart: 9, of which 7 were waited for; matrix products, arithmetic and copies ran while one was open for 10% of the time, Pallas kernels for 0%

commit v1 on v0

v1 whole, which is shorter than its diff:
```python
import jax
import jax.numpy as jnp
from jax import lax
from jax.experimental import pallas as pl
from jax.experimental.pallas import tpu as pltpu
from jax.sharding import PartitionSpec as P

LINE = ("rows", "sub")
VM = pl.BlockSpec(memory_space=pltpu.VMEM)
SM = pl.BlockSpec(memory_space=pltpu.SMEM)
F32 = jnp.float32


def moved(value, target):
    blocks = lax.axis_size("rows")
    pairs = []
    for source in range(2 * blocks):
        there = target(source // 2, source % 2)
        if there is not None and 0 <= there[0] < blocks:
            pairs.append((source, 2 * there[0] + there[1]))
    return lax.ppermute(value, LINE, pairs)


def swap_halves(value):
    return lax.ppermute(value, "sub", [(0, 1), (1, 0)])


def swap_nest(value):
    return lax.ppermute(value, "nest", [(0, 1), (1, 0)])


def call(body, outs, ins, scratch=(), flops=0):
    nbytes = sum(x.size * 4 for x in ins) + sum(4 * a * b for a, b in outs)
    return pl.pallas_call(
        body,
        out_shape=[jax.ShapeDtypeStruct(shape, F32) for shape in outs],
        in_specs=[SM if x.dtype == jnp.int32 and x.size < 16 else VM for x in ins],
        out_specs=[VM] * len(outs),
        scratch_shapes=list(scratch),
        cost_estimate=pl.CostEstimate(flops=flops, bytes_accessed=nbytes, transcendentals=0),
        compiler_params=pltpu.CompilerParams(vmem_limit_bytes=32 * 2**20),
    )(*ins)


def face_of(a, b):
    return jnp.where(jnp.logical_and(a > 0.0, b > 0.0), 0.5 * (a + b), 0.0)


def split(a):
    high = a.astype(jnp.bfloat16)
    low = (a - high.astype(F32)).astype(jnp.bfloat16)
    return high, low


def matmul(a, b):
    return jnp.dot(a, b, precision=lax.Precision.HIGHEST, preferred_element_type=F32)


def matmul_t(a, b):
    return lax.dot_general(
        a, b, (((1,), (1,)), ((), ())), precision=lax.Precision.HIGHEST, preferred_element_type=F32
    )


def row_iota(shape):
    return lax.broadcasted_iota(jnp.int32, shape, 0)


def next_row(x, edge):
    n = x.shape[0]
    return jnp.where(row_iota(x.shape) == n - 1, edge, pltpu.roll(x, n - 1, 0))


def prev_row(x, edge):
    return jnp.where(row_iota(x.shape) == 0, edge, pltpu.roll(x, 1, 0))


def prepare_body(h_ref, my_ref, depth_ref, wet_ref, buf_ref, edge_ref):
    n = h_ref.shape[0]
    h = h_ref[...]
    wd = depth_ref[...] * wet_ref[...].astype(F32)
    face = face_of(wd, next_row(wd, 0.0))
    buf_ref[0:n] = my_ref[...] + 0.5 * face * (next_row(h, 0.0) - h)
    buf_ref[n : 2 * n] = wd
    edge = jnp.concatenate([h[0:1], h[n - 1 : n], wd[0:1], wd[n - 1 : n], jnp.zeros((4, h.shape[1]), F32)], 0)
    buf_ref[2 * n : 2 * n + 8] = edge
    edge_ref[...] = edge


def across_body(h_ref, mx_ref, buf_ref, table_ref, flow_ref, hx_ref, push_ref, first_ref):
    n, width = h_ref.shape
    group = table_ref.shape[-1]
    h = h_ref[...]
    wd = buf_ref[n : 2 * n]
    lane = lax.broadcasted_iota(jnp.int32, wd.shape, 1)
    face = face_of(wd, jnp.where(lane == width - 1, 0.0, pltpu.roll(wd, width - 1, 1)))
    coef = 0.5 * face * face
    push = mx_ref[...] + 0.5 * face * (pltpu.roll(h, width - 1, 1) - h)
    push_ref[...] = push
    for b in range(width // group):
        cols = slice(b * group, (b + 1) * group)
        first_ref[:, cols] = matmul_t(push_ref[:, cols], table_ref[b])
    first = first_ref[...]
    operated = (
        first
        + coef * (first - pltpu.roll(first, width - 1, 1))
        + pltpu.roll(coef, 1, 1) * (first - pltpu.roll(first, 1, 1))
    )
    push_ref[...] = push - operated
    for b in range(width // group):
        cols = slice(b * group, (b + 1) * group)
        flow_ref[:, cols] = first_ref[:, cols] + matmul_t(push_ref[:, cols], table_ref[b])
    flux = face * flow_ref[...]
    hx_ref[...] = h + 0.5 * (flux - pltpu.roll(flux, 1, 1))


def solve_lines(push, face, face_above, table):
    coef = 0.5 * face * face
    coef_above = 0.5 * face_above * face_above
    first = matmul(table, push)
    operated = (
        first
        + coef * (first - next_row(first, 0.0))
        + prev_row(coef, coef_above) * (first - prev_row(first, 0.0))
    )
    flow = first + matmul(table, push - operated)
    g = push.shape[0]
    t_up = coef_above * first[0:1]
    u_down = coef[g - 1 : g] * first[g - 1 : g]
    return flow, t_up, u_down


def messages(flow, face, t_up, u_down, table, is_first):
    g = flow.shape[0]
    half_top = 0.5 * face[0:1]
    bottom = face[g - 1 : g]
    side = 0.5 * face[g - 2 : g - 1]
    rows = [
        t_up,
        half_top * flow[0:1],
        half_top * table[0:1, g - 1 : g],
        half_top * table[0:1, 0:1],
        u_down,
        bottom * flow[g - 1 : g],
        bottom * table[g - 1 : g, g - 1 : g],
        bottom * table[g - 1 : g, 0:1],
    ]
    nest_base = jnp.where(is_first, rows[1], -(side * flow[g - 2 : g - 1]))
    nest_coef = jnp.where(is_first, rows[2], -(side * table[g - 2 : g - 1, 0:1]))
    return jnp.concatenate(rows, 0), jnp.concatenate([nest_base, nest_coef], 0)


def lines_body(own_ref, other_ref, cross_ref, along_ref, table_ref, flow_ref, face_ref, msg_ref, nest_ref, aux_ref, push_ref, wd_ref):
    g = table_ref.shape[0]
    n = g // 2
    half = lax.axis_index("sub")
    lower = half == 0
    is_first = lax.axis_index("rows") == 0
    mine = pl.multiple_of(half * n, n)
    theirs = pl.multiple_of((1 - half) * n, n)
    push_ref[pl.ds(mine, n)] = own_ref[0:n]
    push_ref[pl.ds(theirs, n)] = other_ref[0:n]
    wd_ref[pl.ds(mine, n)] = own_ref[n : 2 * n]
    wd_ref[pl.ds(theirs, n)] = other_ref[n : 2 * n]
    own = own_ref[2 * n : 2 * n + 8]
    other = other_ref[2 * n : 2 * n + 8]
    cross = cross_ref[...]
    along = along_ref[...]
    top = jnp.where(lower, own, other)
    bottom = jnp.where(lower, other, own)
    below = jnp.where(lower, along, cross)
    above = jnp.where(lower, cross, along)
    wd = wd_ref[...]
    face = face_of(wd, next_row(wd, below[2:3]))
    face_above = face_of(above[3:4], wd[0:1])
    south = jnp.where(
        row_iota(wd.shape) == n - 1,
        0.5 * face * (bottom[0:1] - top[1:2]),
        jnp.where(row_iota(wd.shape) == g - 1, 0.5 * face * (below[0:1] - bottom[1:2]), 0.0),
    )
    table = table_ref[...]
    flow, t_up, u_down = solve_lines(push_ref[...] + south, face, face_above, table)
    flow_ref[...] = flow
    face_ref[...] = face
    msg_ref[...], nest_rows = messages(flow, face, t_up, u_down, table, is_first)
    nest_ref[0:2] = nest_rows
    nest_ref[2:8] = jnp.zeros((6, face.shape[1]), F32)
    aux_ref[...] = jnp.broadcast_to(face_above, aux_ref.shape)


def upsampled(row, base):
    width = row.shape[1]
    rolled = pltpu.roll(jnp.broadcast_to(row, (8, width)), lax.rem(width - base, width), 1)
    source = lax.broadcasted_iota(jnp.int32, (128, 256), 0)
    target = lax.broadcasted_iota(jnp.int32, (128, 256), 1)
    pick = jnp.where(target // 2 == source, 1.0, 0.0).astype(F32)
    pieces = [matmul(rolled[:, 128 * m : 128 * (m + 1)], pick) for m in range(width // 256)]
    return jnp.concatenate(pieces, 1)[0:1]


def neighbours(even_ref, odd_ref):
    is_even = lax.rem(lax.axis_index("rows"), 2) == 0
    even = even_ref[...]
    odd = odd_ref[...]
    return jnp.where(is_even, odd, even), jnp.where(is_even, even, odd)


def between_body(
    base_ref, flow_ref, face_ref, msg_ref, aux_ref, even_ref, odd_ref, even2_ref, odd2_ref, own_hx_ref, other_hx_ref,
    nest_row_ref, table_ref, h_ref, next_flow_ref, next_msg_ref, next_nest_ref, hx_ref,
):
    g = table_ref.shape[0]
    n = g // 2
    half = lax.axis_index("sub")
    block = lax.axis_index("rows")
    is_first = block == 0
    is_last = block == lax.axis_size("rows") - 1
    nearfield = lax.axis_index("nest") == 1
    mine = pl.multiple_of(half * n, n)
    theirs = pl.multiple_of((1 - half) * n, n)
    hx_ref[pl.ds(mine, n)] = own_hx_ref[...]
    hx_ref[pl.ds(theirs, n)] = other_hx_ref[...]
    own = msg_ref[...]
    above, below = neighbours(even_ref, odd_ref)
    low = lax.rem(block, 4) < 2
    above2 = jnp.where(low, odd2_ref[...], even2_ref[...])
    below2 = jnp.where(low, even2_ref[...], odd2_ref[...])
    table = table_ref[...]
    face = face_ref[...]
    t_row = below[0:1]
    u_row = above[4:5]
    flow = flow_ref[...] + table[:, g - 1 : g] * t_row + table[:, 0:1] * u_row
    flux = face * flow
    flux_above = above[5:6] + above[6:7] * own[0:1] + above[7:8] * above2[4:5]
    h_below = below[1:2] + below[2:3] * below2[0:1] + below[3:4] * own[4:5] - 0.5 * flux[g - 1 : g]
    h = hx_ref[...] + 0.5 * (flux - prev_row(flux, flux_above))
    packet = upsampled(nest_row_ref[0:1], base_ref[0])
    rows = row_iota(h.shape)
    blend = jnp.logical_and(
        nearfield,
        jnp.logical_or(jnp.logical_and(is_first, rows == 0), jnp.logical_and(is_last, rows == g - 1)),
    )
    h = jnp.where(blend, 0.5 * h + 0.5 * packet, h)
    hx_ref[...] = h
    h_ref[...] = hx_ref[pl.ds(mine, n)]
    push = flow + 0.5 * face * (next_row(h, h_below) - h)
    next_flow, t_up, u_down = solve_lines(push, face, aux_ref[0:1], table)
    next_flow_ref[...] = next_flow
    next_msg_ref[...], nest_rows = messages(next_flow, face, t_up, u_down, table, is_first)
    next_nest_ref[0:2] = nest_rows
    next_nest_ref[2:8] = jnp.zeros((6, face.shape[1]), F32)


def finish_body(
    base_ref, flow_ref, face_ref, msg_ref, even_ref, odd_ref, above2_ref, hx_ref, nest_row_ref, table_ref,
    h_ref, my_ref, flux_ref,
):
    g = table_ref.shape[0]
    n = g // 2
    half = lax.axis_index("sub")
    block = lax.axis_index("rows")
    is_first = jnp.logical_and(block == 0, half == 0)
    is_last = jnp.logical_and(block == lax.axis_size("rows") - 1, half == 1)
    nearfield = lax.axis_index("nest") == 1
    mine = pl.multiple_of(half * n, n)
    own = msg_ref[...]
    above, below = neighbours(even_ref, odd_ref)
    table = table_ref[...]
    flow = flow_ref[...] + table[:, g - 1 : g] * below[0:1] + table[:, 0:1] * above[4:5]
    flux = face_ref[...] * flow
    flux_above = above[5:6] + above[6:7] * own[0:1] + above[7:8] * above2_ref[4:5]
    flux_ref[0] = flow
    flux_ref[1] = flux - prev_row(flux, flux_above)
    my_ref[...] = flux_ref[0, pl.ds(mine, n)]
    h = hx_ref[...] + 0.5 * flux_ref[1, pl.ds(mine, n)]
    packet = upsampled(nest_row_ref[0:1], base_ref[0])
    rows = row_iota(h.shape)
    blend = jnp.logical_and(
        nearfield,
        jnp.logical_or(jnp.logical_and(is_first, rows == 0), jnp.logical_and(is_last, rows == n - 1)),
    )
    h_ref[...] = jnp.where(blend, 0.5 * h + 0.5 * packet, h)


def on_device(elevation, momentum_x, momentum_y, depth, wet_mask, inverse_x, inverse_y, nest_map):
    n, width = elevation.shape[1:]
    g = inverse_y.shape[-1]
    assert g == 2 * n and lax.axis_size("sub") == 2
    block = lax.axis_index("rows")
    half = lax.axis_index("sub")
    base = nest_map[0, 1, 0:1]
    height = elevation[0]
    table_x = inverse_x[0]
    table_y = lax.dynamic_index_in_dim(inverse_y[0], block, 0, keepdims=False)
    is_first = block == 0
    solve_flops = 2 * g * g * width * 2

    buf, edge = call(prepare_body, [(2 * n + 8, width), (8, width)], [height, momentum_y[0], depth[0], wet_mask[0]])
    other = swap_halves(buf)
    cross = moved(edge, lambda k, s: (k + 1, 0) if s == 1 else (k - 1, 1))
    along = moved(edge, lambda k, s: (k + 1, 1) if s == 1 else (k - 1, 0))
    flow_x, hx = call(
        across_body, [(n, width)] * 2, [height, momentum_x[0], buf, table_x],
        [pltpu.VMEM((n, width), F32)] * 2, solve_flops,
    )
    hx_edge = jnp.concatenate([hx[0:1], hx[n - 1 : n]], 0)
    other_edge = swap_halves(hx_edge)
    other_hx = swap_halves(hx)
    hx_top = jnp.where(half == 0, hx_edge[0:1], other_edge[0:1])
    hx_bottom = jnp.where(half == 0, other_edge[1:2], hx_edge[1:2])
    flow, face, msg, nest_rows, aux = call(
        lines_body, [(g, width), (g, width), (8, width), (8, width), (8, width)],
        [buf, other, cross, along, table_y], [pltpu.VMEM((g, width), F32)] * 2, solve_flops,
    )
    msg = jnp.concatenate([msg[0:1], msg[1:2] + hx_top, msg[2:]], 0)
    even = moved(msg, lambda k, s: (k ^ 1, s))
    odd = moved(msg, lambda k, s: (((k + 1) ^ 1) - 1, s))
    even2 = moved(msg, lambda k, s: (k ^ 2, s))
    odd2 = moved(msg, lambda k, s: (((k + 2) ^ 2) - 2, s))
    nest_row = nest_rows[0:1] + jnp.where(is_first, hx_top, hx_bottom) + nest_rows[1:2] * jnp.where(is_first, even[0:1], even[4:5])
    nest_row = swap_nest(nest_row)
    height, flow, msg, nest_rows = call(
        between_body, [(n, width), (g, width), (8, width), (8, width)],
        [base, flow, face, msg, aux, even, odd, even2, odd2, hx, other_hx, nest_row, table_y],
        [pltpu.VMEM((g, width), F32)], solve_flops,
    )
    even = moved(msg, lambda k, s: (k ^ 1, s))
    odd = moved(msg, lambda k, s: (((k + 1) ^ 1) - 1, s))
    above2 = moved(msg, lambda k, s: (k + 2, s))
    flow_x, hx = call(
        across_body, [(n, width)] * 2, [height, flow_x, buf, table_x],
        [pltpu.VMEM((n, width), F32)] * 2, solve_flops,
    )
    nest_row = (
        nest_rows[0:1] + jnp.where(half == 0, hx[0:1], hx[n - 1 : n])
        + nest_rows[1:2] * jnp.where(is_first, even[0:1], even[4:5])
    )
    nest_row = swap_nest(nest_row)
    height, flow_y = call(
        finish_body, [(n, width), (n, width)],
        [base, flow, face, msg, even, odd, above2, hx, nest_row, table_y],
        [pltpu.VMEM((2, g, width), F32)],
    )
    return height[None], flow_x[None], flow_y[None]


def solution(mesh):
    fields = P("nest", LINE, None)
    tables = P("nest", None, None, None)
    return jax.shard_map(
        on_device,
        mesh=mesh,
        in_specs=(fields,) * 5 + (tables, tables, P()),
        out_specs=(fields,) * 3,
        check_vma=False,
    )
```

time: 249 us -> 55.1 us (0.22)
  the two profiles are of different devices: /device:TPU:0 before, /device:TPU:9 now
where the time goes in v1:
time: 55.1 us; the launch traced here: 54.4 us
  starting transfers between devices  28.1 us (51%)
  Pallas kernels  11 us (20%)
  local copies, waits for them, and re-layouts  10.6 us (19%)
  waiting for transfers between devices  2.86 us (5%)
  other arithmetic  0.91 us (2%)
  between operations  0.91 us (2%)
    ppermute x9, starting transfers between devices, moved(): return lax.ppermute(value, LINE, pairs)  20.5 us
    pallas_call x6, Pallas kernels, call(): pl.pallas_call(body, out_shape=[jax.ShapeDtypeStruct(shape, F32) for shap...  11 us
    unnamed x36, local copies, waits for them, and re-layouts  9.41 us
    ppermute x2, starting transfers between devices, swap_nest(): return lax.ppermute(value, 'nest', [(0, 1), (1, 0)])  4.64 us
    ppermute x3, starting transfers between devices, swap_halves(): return lax.ppermute(value, 'sub', [(0, 1), (1, 0)])  2.95 us
    ppermute x3, waiting for transfers between devices, swap_halves(): return lax.ppermute(value, 'sub', [(0, 1), (1, 0)])  2.02 us
    slice x1, local copies, waits for them, and re-layouts, on_device(): base = nest_map[0, 1, 0:1]  1.2 us
  transfers between devices with their start and end apart: 14, of which 2 were waited for; matrix products, arithmetic and copies ran while one was open for 4% of the time, Pallas kernels for 12%

profile of v1, /device:TPU:9, one launch (start us, length us, event | category | flops | bytes accessed | tf_op | source)
XLA Modules:
  0.0 54.4 jit_solution(13116675352748123607)
XLA Ops:
  0.6 0.0 copy-start
  0.6 0.0 copy-start.2
  0.7 1.0 %copy-done.2 = f32[1,64,1024]{2,1,0:T(8,128)S(1)} copy-done((f32[1,64,1024]{2,1,0:T(8,128)S(1)}, f32[1,64,1024]{2,1,0:T(8,128)}, u32[]{:S(2)}) %copy-start.2) | copy-done | bytes 262168
  1.7 0.0 copy-start.6
  1.7 0.9 %copy-done.6 = f32[1,64,1024]{2,1,0:T(8,128)S(1)} copy-done((f32[1,64,1024]{2,1,0:T(8,128)S(1)}, f32[1,64,1024]{2,1,0:T(8,128)}, u32[]{:S(2)}) %copy-start.6) | copy-done | bytes 262168
  2.6 0.0 copy-start.7
  2.6 0.9 %copy-done.7 = f32[1,64,1024]{2,1,0:T(8,128)S(1)} copy-done((f32[1,64,1024]{2,1,0:T(8,128)S(1)}, f32[1,64,1024]{2,1,0:T(8,128)}, u32[]{:S(2)}) %copy-start.7) | copy-done | bytes 262168
  3.6 0.9 %copy-done.8 = s32[1,64,1024]{2,1,0:T(8,128)S(1)} copy-done((s32[1,64,1024]{2,1,0:T(8,128)S(1)}, s32[1,64,1024]{2,1,0:T(8,128)}, u32[]{:S(2)}) %copy-start.8) | copy-done | bytes 262168
  4.5 0.2 shard_map.103
  4.7 1.3 %collective-permute-start = (f32[136,1024]{1,0:T(8,128)S(1)}, f32[136,1024]{1,0:T(8,128)S(1)}, u32[]{:S(2)}, u32[]{:S(2)}) collective-permute-start(f32[136,1024]{1,0:T(8,128)S(1)} %get-tuple-element.20.own_ref.buf_ref), channel_id=1, source_target_pairs={{0,1},{1,0},{2,3},{3,2},{4,5},{5,4},{6,7},{7,6},{8,9},{9,8},{10,11... | collective-permute-start | bytes 1671176 | tf_op jit(solution)/shard_map/ppermute | solution.py:25
  6.0 3.0 %collective-permute-start.2 = (f32[8,1024]{1,0:T(8,128)S(1)}, f32[8,1024]{1,0:T(8,128)S(1)}, u32[]{:S(2)}, u32[]{:S(2)}) collective-permute-start(f32[8,1024]{1,0:T(8,128)S(1)} %get-tuple-element.21), channel_id=1, source_target_pairs={{1,3},{2,0},{3,5},{4,2},{5,7},{6,4},{7,9},{8,6},{9,11},{10,8},{11,... | collective-permute-start | bytes 98312 | tf_op jit(solution)/shard_map/ppermute | solution.py:21
  9.0 3.1 %collective-permute-start.1 = (f32[8,1024]{1,0:T(8,128)S(1)}, f32[8,1024]{1,0:T(8,128)S(1)}, u32[]{:S(2)}, u32[]{:S(2)}) collective-permute-start(f32[8,1024]{1,0:T(8,128)S(1)} %get-tuple-element.21), channel_id=1, source_target_pairs={{1,2},{2,1},{3,4},{4,3},{5,6},{6,5},{7,8},{8,7},{9,10},{10,9},{11,... | collective-permute-start | bytes 98312 | tf_op jit(solution)/shard_map/ppermute | solution.py:21
  12.1 0.0 copy-done.1
  12.1 0.0 copy-done.3
  12.1 2.4 %shard_map.105 = (f32[64,1024]{1,0:T(8,128)S(1)}, f32[64,1024]{1,0:T(8,128)S(1)}) custom-call(f32[64,1024]{1,0:T(8,128)S(1)} %bitcast.15, f32[64,1024]{1,0:T(8,128)S(1)} %bitcast.16, f32[136,1024]{1,0:T(8,128)S(1)} %get-tuple-element.20.own_ref.buf_ref, f32[8,128,128]{2,1,0:T(8,128)S(1)} %bitcast.12), custom_call_target="tpu_custom_call" | custom-call | flops 67108864 | bytes 2129920 | tf_op jit(solution)/shard_map/pallas_call | solution.py:34
  14.5 0.0 copy-start.4
  14.5 0.7 %copy-done.4 = f32[64,1024]{1,0:T(8,128)} copy-done((f32[64,1024]{1,0:T(8,128)}, f32[64,1024]{1,0:T(8,128)S(1)}, u32[]{:S(2)}) %copy-start.4) | copy-done | bytes 262168
  15.3 0.4 collective-permute-start.3
  15.7 0.0 copy-done
  15.7 0.0 collective-permute-done.2.along_ref
  15.7 0.0 copy-start.13
  15.7 0.6 %copy-done.13 = f32[8,1024]{1,0:T(8,128)} copy-done((f32[8,1024]{1,0:T(8,128)}, f32[8,1024]{1,0:T(8,128)S(1)}, u32[]{:S(2)}) %copy-start.13) | copy-done | bytes 32792
  16.3 0.0 collective-permute-done.1.cross_ref
  16.3 0.6 %copy-done.15 = f32[8,1024]{1,0:T(8,128)} copy-done((f32[8,1024]{1,0:T(8,128)}, f32[8,1024]{1,0:T(8,128)S(1)}, u32[]{:S(2)}) %copy-start.15) | copy-done | bytes 32792
  16.9 2.0 %collective-permute-done.other_ref = f32[136,1024]{1,0:T(8,128)S(1)} collective-permute-done((f32[136,1024]{1,0:T(8,128)S(1)}, f32[136,1024]{1,0:T(8,128)S(1)}, u32[]{:S(2)}, u32[]{:S(2)}) %collective-permute-start) | collective-permute-done | bytes 557088 | tf_op jit(solution)/shard_map/ppermute | solution.py:25
  18.9 0.8 %copy-done.14 = f32[8,1024]{1,0:T(8,128)S(1)} copy-done((f32[8,1024]{1,0:T(8,128)S(1)}, f32[8,1024]{1,0:T(8,128)}, u32[]{:S(2)}) %copy-start.14) | copy-done | bytes 32792
  19.7 0.8 %copy-done.16 = f32[8,1024]{1,0:T(8,128)S(1)} copy-done((f32[8,1024]{1,0:T(8,128)S(1)}, f32[8,1024]{1,0:T(8,128)}, u32[]{:S(2)}) %copy-start.16) | copy-done | bytes 32792
  20.5 1.3 %shard_map.104 = (f32[128,1024]{1,0:T(8,128)S(1)}, f32[128,1024]{1,0:T(8,128)S(1)}, f32[8,1024]{1,0:T(8,128)S(1)}, f32[8,1024]{1,0:T(8,128)S(1)}, f32[8,1024]{1,0:T(8,128)S(1)}) custom-call(f32[136,1024]{1,0:T(8,128)S(1)} %get-tuple-element.20.own_ref.buf_ref, f32[136,1024]{1,0:T(8,128)S(1)} %collective-permute-done.other_ref, f32[8,1024]{1,0:T(8,128)S(1)} %copy-done.16, ...), custom_call_target="tpu_custom_call" | custom-call | flops 67108864 | bytes 2392064 | tf_op jit(solution)/shard_map/pallas_call | solution.py:34
  21.8 0.0 copy-start.11
  21.8 0.0 copy-start.17
  21.8 0.6 %copy-done.11 = f32[8,1024]{1,0:T(8,128)} copy-done((f32[8,1024]{1,0:T(8,128)}, f32[8,1024]{1,0:T(8,128)S(1)}, u32[]{:S(2)}) %copy-start.11) | copy-done | bytes 32792
  22.4 0.0 copy-done.17
  22.4 0.0 collective-permute-done.3
  22.4 1.3 %collective-permute-start.4 = (f32[8,1024]{1,0:T(8,128)S(1)}, f32[8,1024]{1,0:T(8,128)S(1)}, u32[]{:S(2)}, u32[]{:S(2)}) collective-permute-start(f32[8,1024]{1,0:T(8,128)S(1)} %pad_maximum_fusion.msg_ref), channel_id=1, source_target_pairs={{0,2},{1,3},{2,0},{3,1},{4,6},{5,7},{6,4},{7,5},{8,10},{9,11},{10,... | collective-permute-start | bytes 98312 | tf_op jit(solution)/shard_map/ppermute | solution.py:21
  23.7 1.2 %collective-permute-start.8 = (f32[64,1024]{1,0:T(8,128)S(1)}, f32[64,1024]{1,0:T(8,128)S(1)}, u32[]{:S(2)}, u32[]{:S(2)}) collective-permute-start(f32[64,1024]{1,0:T(8,128)S(1)} %get-tuple-element.25.own_hx_ref), channel_id=1, source_target_pairs={{0,1},{1,0},{2,3},{3,2},{4,5},{5,4},{6,7},{7,6},{8,9},{9,8},{10,11... | collective-permute-start | bytes 786440 | tf_op jit(solution)/shard_map/ppermute | solution.py:25
  24.9 3.2 %collective-permute-start.7 = (f32[8,1024]{1,0:T(8,128)S(1)}, f32[8,1024]{1,0:T(8,128)S(1)}, u32[]{:S(2)}, u32[]{:S(2)}) collective-permute-start(f32[8,1024]{1,0:T(8,128)S(1)} %pad_maximum_fusion.msg_ref), channel_id=1, source_target_pairs={{4,8},{5,9},{6,10},{7,11},{8,4},{9,5},{10,6},{11,7},{20,24},{21,25... | collective-permute-start | bytes 98312 | tf_op jit(solution)/shard_map/ppermute | solution.py:21
  28.1 0.1 collective-permute-start.6
  28.2 3.3 %collective-permute-start.5 = (f32[8,1024]{1,0:T(8,128)S(1)}, f32[8,1024]{1,0:T(8,128)S(1)}, u32[]{:S(2)}, u32[]{:S(2)}) collective-permute-start(f32[8,1024]{1,0:T(8,128)S(1)} %pad_maximum_fusion.msg_ref), channel_id=1, source_target_pairs={{2,4},{3,5},{4,2},{5,3},{6,8},{7,9},{8,6},{9,7},{10,12},{11,13},{1... | collective-permute-start | bytes 98312 | tf_op jit(solution)/shard_map/ppermute | solution.py:21
  31.5 0.0 collective-permute-done.4.even_ref
  31.6 0.0 copy-start.9
  31.6 0.9 %fusion.3 = f32[1,1024]{1,0:T(1,128)S(1)} fusion(pred[]{:T(512)S(6)} %eq.8, pred[]{:T(512)S(6)} %eq.9, f32[8,1024]{1,0:T(8,128)S(1)} %collective-permute-done.4.even_ref, f32[2,1024]{1,0:T(2,128)S(1)} %collective-permute-done.3, f32[8,1024]{1,0:T(8,128)} %copy-done.17, f32[64,1024]{1,0:T(8,128)S(1)} %get-tuple-element.25.own_hx_ref), kind=kLoop, calls=%fused_computation.12 | loop fusion | flops 7168 | bytes 36866 | tf_op jit(solution)/shard_map/add | solution.py:320
  32.4 3.1 %collective-permute-start.9 = (f32[1,1024]{1,0:T(1,128)S(1)}, f32[1,1024]{1,0:T(1,128)S(1)}, u32[]{:S(2)}, u32[]{:S(2)}) collective-permute-start(f32[1,1024]{1,0:T(1,128)S(1)} %fusion.3), channel_id=1, source_target_pairs={{0,16},{16,0},{1,17},{17,1},{2,18},{18,2},{3,19},{19,3},{4,20},{20... | collective-permute-start | bytes 12296 | tf_op jit(solution)/shard_map/ppermute | solution.py:29
  35.5 1.2 %slice.54 = s32[1,1,1]{2,1,0:T(1,128)} slice(s32[2,2,1024]{2,1,0:T(2,128)} %param.15), slice={[0:1], [1:2], [0:1]} | slice | bytes 8 | tf_op jit(solution)/shard_map/slice | solution.py:291
  36.7 0.0 collective-permute-done.8.other_hx_ref
  36.7 0.0 collective-permute-done.7.odd2_ref
  36.7 0.0 collective-permute-done.6.even2_ref
  36.7 0.0 collective-permute-done.5.odd_ref
  36.8 0.0 collective-permute-done.9.nest_row_ref
  36.8 0.0 copy-done.9
  36.8 0.0 copy-start.10
  36.8 0.7 %copy-done.10 = f32[8,1024]{1,0:T(8,128)S(1)} copy-done((f32[8,1024]{1,0:T(8,128)S(1)}, f32[8,1024]{1,0:T(8,128)}, u32[]{:S(2)}) %copy-start.10) | copy-done | bytes 32792
  37.5 0.8 %copy-done.12 = f32[8,1024]{1,0:T(8,128)S(1)} copy-done((f32[8,1024]{1,0:T(8,128)S(1)}, f32[8,1024]{1,0:T(8,128)}, u32[]{:S(2)}) %copy-start.12) | copy-done | bytes 32792
  38.3 2.3 %shard_map.106 = (f32[64,1024]{1,0:T(8,128)S(1)}, f32[128,1024]{1,0:T(8,128)S(1)}, f32[8,1024]{1,0:T(8,128)S(1)}, f32[8,1024]{1,0:T(8,128)S(1)}) custom-call(s32[1]{0:T(128)} %bitcast.base_ref, f32[128,1024]{1,0:T(8,128)S(1)} %get-tuple-element.22.flow_ref, f32[128,1024]{1,0:T(8,128)S(1)} %get-tuple-element.23.face_ref, ...), custom_call_target="tpu_custom_call" | custom-call | flops 67108864 | bytes 2691076 | tf_op jit(solution)/shard_map/pallas_call | solution.py:34
  40.6 0.1 collective-permute-start.10
  40.6 3.3 %collective-permute-start.12 = (f32[8,1024]{1,0:T(8,128)S(1)}, f32[8,1024]{1,0:T(8,128)S(1)}, u32[]{:S(2)}, u32[]{:S(2)}) collective-permute-start(f32[8,1024]{1,0:T(8,128)S(1)} %get-tuple-element.29.msg_ref), channel_id=1, source_target_pairs={{0,4},{1,5},{2,6},{3,7},{4,8},{5,9},{6,10},{7,11},{8,12},{9,13},{1... | collective-permute-start | bytes 98312 | tf_op jit(solution)/shard_map/ppermute | solution.py:21
  43.9 3.2 %collective-permute-start.11 = (f32[8,1024]{1,0:T(8,128)S(1)}, f32[8,1024]{1,0:T(8,128)S(1)}, u32[]{:S(2)}, u32[]{:S(2)}) collective-permute-start(f32[8,1024]{1,0:T(8,128)S(1)} %get-tuple-element.29.msg_ref), channel_id=1, source_target_pairs={{2,4},{3,5},{4,2},{5,3},{6,8},{7,9},{8,6},{9,7},{10,12},{11,13},{1... | collective-permute-start | bytes 98312 | tf_op jit(solution)/shard_map/ppermute | solution.py:21
  47.1 0.0 copy-done.5
  47.1 3.0 %shard_map.107 = (f32[64,1024]{1,0:T(8,128)}, f32[64,1024]{1,0:T(8,128)S(1)}) custom-call(f32[64,1024]{1,0:T(8,128)S(1)} %get-tuple-element.30.h_ref, f32[64,1024]{1,0:T(8,128)S(1)} %copy-done.5, f32[136,1024]{1,0:T(8,128)S(1)} %get-tuple-element.20.own_ref.buf_ref, f32[8,128,128]{2,1,0:T(8,128)S(1)} %bitcast.13), custom_call_target="tpu_custom_call" | custom-call | flops 67108864 | bytes 2129920 | tf_op jit(solution)/shard_map/pallas_call | solution.py:34
  50.1 0.0 collective-permute-done.10.even_ref
  50.1 1.5 %collective-permute-start.13 = (f32[1,1024]{1,0:T(1,128)S(1)}, f32[1,1024]{1,0:T(1,128)S(1)}, u32[]{:S(2)}, u32[]{:S(2)}) collective-permute-start(f32[1,1024]{1,0:T(1,128)S(1)} %fusion.1), channel_id=1, source_target_pairs={{0,16},{16,0},{1,17},{17,1},{2,18},{18,2},{3,19},{19,3},{4,20},{20... | collective-permute-start | bytes 12296 | tf_op jit(solution)/shard_map/ppermute | solution.py:29
  51.7 0.0 collective-permute-done.12.above2_ref
  51.7 0.0 collective-permute-done.11.odd_ref
  51.7 0.8 %collective-permute-done.13.nest_row_ref = f32[1,1024]{1,0:T(1,128)S(1)} collective-permute-done((f32[1,1024]{1,0:T(1,128)S(1)}, f32[1,1024]{1,0:T(1,128)S(1)}, u32[]{:S(2)}, u32[]{:S(2)}) %collective-permute-start.13) | collective-permute-done | bytes 4128 | tf_op jit(solution)/shard_map/ppermute | solution.py:29
  52.5 1.9 %shard_map.108 = (f32[64,1024]{1,0:T(8,128)}, f32[64,1024]{1,0:T(8,128)}) custom-call(s32[1]{0:T(128)} %bitcast.base_ref, f32[128,1024]{1,0:T(8,128)S(1)} %get-tuple-element.28.flow_ref, f32[128,1024]{1,0:T(8,128)S(1)} %get-tuple-element.23.face_ref, f32[8,1024]{1,0:T(8,128)S(1)} %get-tuple-element.29.msg_ref, ...), custom_call_target="tpu_custom_call" | custom-call | bytes 2035716 | tf_op jit(solution)/shard_map/pallas_call | solution.py:34
  (15 shorter events, 0.1 us)
Async XLA Ops:
  0.6 15.0 %copy-start = (f32[1,8,128,128]{3,2,1,0:T(8,128)S(1)}, f32[1,8,128,128]{3,2,1,0:T(8,128)}, u32[]{:S(2)}) copy-start(f32[1,8,128,128]{3,2,1,0:T(8,128)} %param.14) | copy-start | bytes 1572868
  0.6 1.0 %copy-start.2 = (f32[1,64,1024]{2,1,0:T(8,128)S(1)}, f32[1,64,1024]{2,1,0:T(8,128)}, u32[]{:S(2)}) copy-start(f32[1,64,1024]{2,1,0:T(8,128)} %param.8) | copy-start | bytes 786436
  1.7 0.9 %copy-start.6 = (f32[1,64,1024]{2,1,0:T(8,128)S(1)}, f32[1,64,1024]{2,1,0:T(8,128)}, u32[]{:S(2)}) copy-start(f32[1,64,1024]{2,1,0:T(8,128)} %param.10) | copy-start | bytes 786436
  2.6 0.9 %copy-start.7 = (f32[1,64,1024]{2,1,0:T(8,128)S(1)}, f32[1,64,1024]{2,1,0:T(8,128)}, u32[]{:S(2)}) copy-start(f32[1,64,1024]{2,1,0:T(8,128)} %param.11) | copy-start | bytes 786436
  3.6 0.9 %copy-start.8 = (s32[1,64,1024]{2,1,0:T(8,128)S(1)}, s32[1,64,1024]{2,1,0:T(8,128)}, u32[]{:S(2)}) copy-start(s32[1,64,1024]{2,1,0:T(8,128)} %param.12) | copy-start | bytes 786436
  4.5 7.6 %copy-start.1 = (f32[1,8,128,128]{3,2,1,0:T(8,128)S(1)}, f32[1,8,128,128]{3,2,1,0:T(8,128)}, u32[]{:S(2)}) copy-start(f32[1,8,128,128]{3,2,1,0:T(8,128)} %param.13) | copy-start | bytes 1572868
  4.5 7.6 %copy-start.3 = (f32[1,64,1024]{2,1,0:T(8,128)S(1)}, f32[1,64,1024]{2,1,0:T(8,128)}, u32[]{:S(2)}) copy-start(f32[1,64,1024]{2,1,0:T(8,128)} %param.9) | copy-start | bytes 786436
  4.7 14.3 %collective-permute-start = (f32[136,1024]{1,0:T(8,128)S(1)}, f32[136,1024]{1,0:T(8,128)S(1)}, u32[]{:S(2)}, u32[]{:S(2)}) collective-permute-start(f32[136,1024]{1,0:T(8,128)S(1)} %get-tuple-element.20.own_ref.buf_ref), channel_id=1, source_target_pairs={{0,1},{1,0},{2,3},{3,2},{4,5},{5,4},{6,7},{7,6},{8,9},{9,8},{10,11... | collective-permute-start | bytes 1671176 | tf_op jit(solution)/shard_map/ppermute | solution.py:25
  6.0 9.7 %collective-permute-start.2 = (f32[8,1024]{1,0:T(8,128)S(1)}, f32[8,1024]{1,0:T(8,128)S(1)}, u32[]{:S(2)}, u32[]{:S(2)}) collective-permute-start(f32[8,1024]{1,0:T(8,128)S(1)} %get-tuple-element.21), channel_id=1, source_target_pairs={{1,3},{2,0},{3,5},{4,2},{5,7},{6,4},{7,9},{8,6},{9,11},{10,8},{11,... | collective-permute-start | bytes 98312 | tf_op jit(solution)/shard_map/ppermute | solution.py:21
  9.0 7.3 %collective-permute-start.1 = (f32[8,1024]{1,0:T(8,128)S(1)}, f32[8,1024]{1,0:T(8,128)S(1)}, u32[]{:S(2)}, u32[]{:S(2)}) collective-permute-start(f32[8,1024]{1,0:T(8,128)S(1)} %get-tuple-element.21), channel_id=1, source_target_pairs={{1,2},{2,1},{3,4},{4,3},{5,6},{6,5},{7,8},{8,7},{9,10},{10,9},{11,... | collective-permute-start | bytes 98312 | tf_op jit(solution)/shard_map/ppermute | solution.py:21
  14.5 0.7 %copy-start.4 = (f32[64,1024]{1,0:T(8,128)}, f32[64,1024]{1,0:T(8,128)S(1)}, u32[]{:S(2)}) copy-start(f32[64,1024]{1,0:T(8,128)S(1)} %get-tuple-element.31.mx_ref) | copy-start | bytes 786436
  15.3 7.1 %collective-permute-start.3 = (f32[2,1024]{1,0:T(2,128)S(1)}, f32[2,1024]{1,0:T(2,128)S(1)}, u32[]{:S(2)}, u32[]{:S(2)}) collective-permute-start(f32[2,1024]{1,0:T(2,128)S(1)} %pad_maximum_fusion.1), channel_id=1, source_target_pairs={{0,1},{1,0},{2,3},{3,2},{4,5},{5,4},{6,7},{7,6},{8,9},{9,8},{10,11... | collective-permute-start | bytes 24584 | tf_op jit(solution)/shard_map/ppermute | solution.py:25
  15.7 0.6 %copy-start.13 = (f32[8,1024]{1,0:T(8,128)}, f32[8,1024]{1,0:T(8,128)S(1)}, u32[]{:S(2)}) copy-start(f32[8,1024]{1,0:T(8,128)S(1)} %collective-permute-done.2.along_ref) | copy-start | bytes 98308
  16.3 0.6 %copy-start.15 = (f32[8,1024]{1,0:T(8,128)}, f32[8,1024]{1,0:T(8,128)S(1)}, u32[]{:S(2)}) copy-start(f32[8,1024]{1,0:T(8,128)S(1)} %collective-permute-done.1.cross_ref) | copy-start | bytes 98308
  18.9 0.8 %copy-start.14 = (f32[8,1024]{1,0:T(8,128)S(1)}, f32[8,1024]{1,0:T(8,128)}, u32[]{:S(2)}) copy-start(f32[8,1024]{1,0:T(8,128)} %copy-done.13) | copy-start | bytes 98308
  19.7 0.8 %copy-start.16 = (f32[8,1024]{1,0:T(8,128)S(1)}, f32[8,1024]{1,0:T(8,128)}, u32[]{:S(2)}) copy-start(f32[8,1024]{1,0:T(8,128)} %copy-done.15) | copy-start | bytes 98308
  21.8 0.6 %copy-start.11 = (f32[8,1024]{1,0:T(8,128)}, f32[8,1024]{1,0:T(8,128)S(1)}, u32[]{:S(2)}) copy-start(f32[8,1024]{1,0:T(8,128)S(1)} %get-tuple-element.26.aux_ref) | copy-start | bytes 98308
  21.8 0.6 %copy-start.17 = (f32[8,1024]{1,0:T(8,128)}, f32[8,1024]{1,0:T(8,128)S(1)}, u32[]{:S(2)}) copy-start(f32[8,1024]{1,0:T(8,128)S(1)} %get-tuple-element.27) | copy-start | bytes 98308
  22.4 9.1 %collective-permute-start.4 = (f32[8,1024]{1,0:T(8,128)S(1)}, f32[8,1024]{1,0:T(8,128)S(1)}, u32[]{:S(2)}, u32[]{:S(2)}) collective-permute-start(f32[8,1024]{1,0:T(8,128)S(1)} %pad_maximum_fusion.msg_ref), channel_id=1, source_target_pairs={{0,2},{1,3},{2,0},{3,1},{4,6},{5,7},{6,4},{7,5},{8,10},{9,11},{10,... | collective-permute-start | bytes 98312 | tf_op jit(solution)/shard_map/ppermute | solution.py:21
  23.7 13.0 %collective-permute-start.8 = (f32[64,1024]{1,0:T(8,128)S(1)}, f32[64,1024]{1,0:T(8,128)S(1)}, u32[]{:S(2)}, u32[]{:S(2)}) collective-permute-start(f32[64,1024]{1,0:T(8,128)S(1)} %get-tuple-element.25.own_hx_ref), channel_id=1, source_target_pairs={{0,1},{1,0},{2,3},{3,2},{4,5},{5,4},{6,7},{7,6},{8,9},{9,8},{10,11... | collective-permute-start | bytes 786440 | tf_op jit(solution)/shard_map/ppermute | solution.py:25
  24.9 11.8 %collective-permute-start.7 = (f32[8,1024]{1,0:T(8,128)S(1)}, f32[8,1024]{1,0:T(8,128)S(1)}, u32[]{:S(2)}, u32[]{:S(2)}) collective-permute-start(f32[8,1024]{1,0:T(8,128)S(1)} %pad_maximum_fusion.msg_ref), channel_id=1, source_target_pairs={{4,8},{5,9},{6,10},{7,11},{8,4},{9,5},{10,6},{11,7},{20,24},{21,25... | collective-permute-start | bytes 98312 | tf_op jit(solution)/shard_map/ppermute | solution.py:21
  28.1 8.6 %collective-permute-start.6 = (f32[8,1024]{1,0:T(8,128)S(1)}, f32[8,1024]{1,0:T(8,128)S(1)}, u32[]{:S(2)}, u32[]{:S(2)}) collective-permute-start(f32[8,1024]{1,0:T(8,128)S(1)} %pad_maximum_fusion.msg_ref), channel_id=1, source_target_pairs={{0,4},{1,5},{2,6},{3,7},{4,0},{5,1},{6,2},{7,3},{8,12},{9,13},{10,... | collective-permute-start | bytes 98312 | tf_op jit(solution)/shard_map/ppermute | solution.py:21
  28.2 8.5 %collective-permute-start.5 = (f32[8,1024]{1,0:T(8,128)S(1)}, f32[8,1024]{1,0:T(8,128)S(1)}, u32[]{:S(2)}, u32[]{:S(2)}) collective-permute-start(f32[8,1024]{1,0:T(8,128)S(1)} %pad_maximum_fusion.msg_ref), channel_id=1, source_target_pairs={{2,4},{3,5},{4,2},{5,3},{6,8},{7,9},{8,6},{9,7},{10,12},{11,13},{1... | collective-permute-start | bytes 98312 | tf_op jit(solution)/shard_map/ppermute | solution.py:21
  31.6 5.2 %copy-start.9 = (f32[8,1024]{1,0:T(8,128)}, f32[8,1024]{1,0:T(8,128)S(1)}, u32[]{:S(2)}) copy-start(f32[8,1024]{1,0:T(8,128)S(1)} %collective-permute-done.4.even_ref) | copy-start | bytes 98308
  32.4 4.3 %collective-permute-start.9 = (f32[1,1024]{1,0:T(1,128)S(1)}, f32[1,1024]{1,0:T(1,128)S(1)}, u32[]{:S(2)}, u32[]{:S(2)}) collective-permute-start(f32[1,1024]{1,0:T(1,128)S(1)} %fusion.3), channel_id=1, source_target_pairs={{0,16},{16,0},{1,17},{17,1},{2,18},{18,2},{3,19},{19,3},{4,20},{20... | collective-permute-start | bytes 12296 | tf_op jit(solution)/shard_map/ppermute | solution.py:29
  36.8 0.8 %copy-start.10 = (f32[8,1024]{1,0:T(8,128)S(1)}, f32[8,1024]{1,0:T(8,128)}, u32[]{:S(2)}) copy-start(f32[8,1024]{1,0:T(8,128)} %copy-done.9) | copy-start | bytes 98308
  37.5 0.8 %copy-start.12 = (f32[8,1024]{1,0:T(8,128)S(1)}, f32[8,1024]{1,0:T(8,128)}, u32[]{:S(2)}) copy-start(f32[8,1024]{1,0:T(8,128)} %copy-done.11) | copy-start | bytes 98308
  38.3 8.8 %copy-start.5 = (f32[64,1024]{1,0:T(8,128)S(1)}, f32[64,1024]{1,0:T(8,128)}, u32[]{:S(2)}) copy-start(f32[64,1024]{1,0:T(8,128)} %copy-done.4) | copy-start | bytes 786436
  40.6 9.6 %collective-permute-start.10 = (f32[8,1024]{1,0:T(8,128)S(1)}, f32[8,1024]{1,0:T(8,128)S(1)}, u32[]{:S(2)}, u32[]{:S(2)}) collective-permute-start(f32[8,1024]{1,0:T(8,128)S(1)} %get-tuple-element.29.msg_ref), channel_id=1, source_target_pairs={{0,2},{1,3},{2,0},{3,1},{4,6},{5,7},{6,4},{7,5},{8,10},{9,11},{10,... | collective-permute-start | bytes 98312 | tf_op jit(solution)/shard_map/ppermute | solution.py:21
  40.6 11.0 %collective-permute-start.12 = (f32[8,1024]{1,0:T(8,128)S(1)}, f32[8,1024]{1,0:T(8,128)S(1)}, u32[]{:S(2)}, u32[]{:S(2)}) collective-permute-start(f32[8,1024]{1,0:T(8,128)S(1)} %get-tuple-element.29.msg_ref), channel_id=1, source_target_pairs={{0,4},{1,5},{2,6},{3,7},{4,8},{5,9},{6,10},{7,11},{8,12},{9,13},{1... | collective-permute-start | bytes 98312 | tf_op jit(solution)/shard_map/ppermute | solution.py:21
  43.9 7.8 %collective-permute-start.11 = (f32[8,1024]{1,0:T(8,128)S(1)}, f32[8,1024]{1,0:T(8,128)S(1)}, u32[]{:S(2)}, u32[]{:S(2)}) collective-permute-start(f32[8,1024]{1,0:T(8,128)S(1)} %get-tuple-element.29.msg_ref), channel_id=1, source_target_pairs={{2,4},{3,5},{4,2},{5,3},{6,8},{7,9},{8,6},{9,7},{10,12},{11,13},{1... | collective-permute-start | bytes 98312 | tf_op jit(solution)/shard_map/ppermute | solution.py:21
  50.1 2.4 %collective-permute-start.13 = (f32[1,1024]{1,0:T(1,128)S(1)}, f32[1,1024]{1,0:T(1,128)S(1)}, u32[]{:S(2)}, u32[]{:S(2)}) collective-permute-start(f32[1,1024]{1,0:T(1,128)S(1)} %fusion.1), channel_id=1, source_target_pairs={{0,16},{16,0},{1,17},{17,1},{2,18},{18,2},{3,19},{19,3},{4,20},{20... | collective-permute-start | bytes 12296 | tf_op jit(solution)/shard_map/ppermute | solution.py:29

commit v2 on v1

--- a/solution.py
+++ b/solution.py
@@ -8,6 +8,7 @@
 LINE = ("rows", "sub")
 VM = pl.BlockSpec(memory_space=pltpu.VMEM)
 SM = pl.BlockSpec(memory_space=pltpu.SMEM)
+FAR = pl.BlockSpec(memory_space=pltpu.HBM)
 F32 = jnp.float32
 
 
@@ -29,16 +30,23 @@
     return lax.ppermute(value, "nest", [(0, 1), (1, 0)])
 
 
-def call(body, outs, ins, scratch=(), flops=0):
-    nbytes = sum(x.size * 4 for x in ins) + sum(4 * a * b for a, b in outs)
+def call(body, outs, ins, scratch=(), flops=0, far=(), far_outs=(), vmem=8):
+    shapes = [o if isinstance(o, jax.ShapeDtypeStruct) else jax.ShapeDtypeStruct(o, F32) for o in outs]
+    nbytes = sum(4 * x.size for i, x in enumerate(ins) if i not in far) + sum(4 * x.size for x in shapes)
+
+    def spec(i, x, others):
+        if i in others:
+            return FAR
+        return SM if x.dtype == jnp.int32 and x.size < 16 else VM
+
     return pl.pallas_call(
         body,
-        out_shape=[jax.ShapeDtypeStruct(shape, F32) for shape in outs],
-        in_specs=[SM if x.dtype == jnp.int32 and x.size < 16 else VM for x in ins],
-        out_specs=[VM] * len(outs),
+        out_shape=shapes,
+        in_specs=[spec(i, x, far) for i, x in enumerate(ins)],
+        out_specs=[spec(i, x, far_outs) for i, x in enumerate(shapes)],
         scratch_shapes=list(scratch),
         cost_estimate=pl.CostEstimate(flops=flops, bytes_accessed=nbytes, transcendentals=0),
-        compiler_params=pltpu.CompilerParams(vmem_limit_bytes=32 * 2**20),
+        compiler_params=pltpu.CompilerParams(vmem_limit_bytes=vmem * 2**20),
     )(*ins)
 
 
@@ -53,12 +61,23 @@
 
 
 def matmul(a, b):
-    return jnp.dot(a, b, precision=lax.Precision.HIGHEST, preferred_element_type=F32)
+    a_high, a_low = split(a)
+    b_high, b_low = split(b)
+    return jnp.dot(
+        jnp.concatenate([a_high, a_high, a_low], 1),
+        jnp.concatenate([b_high, b_low, b_high], 0),
+        preferred_element_type=F32,
+    )
 
 
 def matmul_t(a, b):
+    a_high, a_low = split(a)
+    b_high, b_low = split(b)
     return lax.dot_general(
-        a, b, (((1,), (1,)), ((), ())), precision=lax.Precision.HIGHEST, preferred_element_type=F32
+        jnp.concatenate([a_high, a_high, a_low], 1),
+        jnp.concatenate([b_high, b_low, b_high], 1),
+        (((1,), (1,)), ((), ())),
+        preferred_element_type=F32,
     )
 
 
@@ -75,19 +94,31 @@
     return jnp.where(row_iota(x.shape) == 0, edge, pltpu.roll(x, 1, 0))
 
 
-def prepare_body(h_ref, my_ref, depth_ref, wet_ref, buf_ref, edge_ref):
+def prepare_body(h_far, my_far, depth_far, wet_far, buf_ref, edge_ref, h_ref, my_ref, depth_ref, wet_ref, sems):
+    copies = [
+        pltpu.make_async_copy(depth_far, depth_ref, sems.at[0]),
+        pltpu.make_async_copy(wet_far, wet_ref, sems.at[1]),
+        pltpu.make_async_copy(h_far, h_ref, sems.at[2]),
+        pltpu.make_async_copy(my_far, my_ref, sems.at[3]),
+    ]
+    for copy in copies:
+        copy.start()
     n = h_ref.shape[0]
+    copies[0].wait()
+    copies[1].wait()
+    wd = depth_ref[...] * wet_ref[...].astype(F32)
+    buf_ref[n : 2 * n] = wd
+    face = face_of(wd, next_row(wd, 0.0))
+    copies[2].wait()
     h = h_ref[...]
-    wd = depth_ref[...] * wet_ref[...].astype(F32)
-    face = face_of(wd, next_row(wd, 0.0))
-    buf_ref[0:n] = my_ref[...] + 0.5 * face * (next_row(h, 0.0) - h)
-    buf_ref[n : 2 * n] = wd
     edge = jnp.concatenate([h[0:1], h[n - 1 : n], wd[0:1], wd[n - 1 : n], jnp.zeros((4, h.shape[1]), F32)], 0)
     buf_ref[2 * n : 2 * n + 8] = edge
     edge_ref[...] = edge
-
-
-def across_body(h_ref, mx_ref, buf_ref, table_ref, flow_ref, hx_ref, push_ref, first_ref):
+    copies[3].wait()
+    buf_ref[0:n] = my_ref[...] + 0.5 * face * (next_row(h, 0.0) - h)
+
+
+def across(h_ref, mx_ref, buf_ref, table_ref, flow_ref, hx_ref, push_ref, first_ref):
     n, width = h_ref.shape
     group = table_ref.shape[-1]
     h = h_ref[...]
@@ -112,6 +143,42 @@
         flow_ref[:, cols] = first_ref[:, cols] + matmul_t(push_ref[:, cols], table_ref[b])
     flux = face * flow_ref[...]
     hx_ref[...] = h + 0.5 * (flux - pltpu.roll(flux, 1, 1))
+
+
+def across_first_body(
+    h_ref, mx_ref, buf_ref, table_ref, tables_far, map_far, along_ref,
+    flow_ref, hx_ref, hx_edge_ref, line_table_ref, base_ref, push_ref, first_ref, map_ref, sems,
+):
+    n = h_ref.shape[0]
+    fetch_table = pltpu.make_async_copy(tables_far.at[lax.axis_index("rows")], line_table_ref, sems.at[0])
+    fetch_map = pltpu.make_async_copy(map_far.at[0, :, pl.ds(0, 128)], map_ref, sems.at[1])
+    fetch_table.start()
+    fetch_map.start()
+    across(h_ref, mx_ref, buf_ref, table_ref, flow_ref, hx_ref, push_ref, first_ref)
+    hx_edge_ref[0:1] = hx_ref[0:1]
+    hx_edge_ref[1:2] = hx_ref[n - 1 : n]
+    hx_edge_ref[2:8] = jnp.zeros((6, h_ref.shape[1]), F32)
+    fetch_map.wait()
+    base_ref[0] = map_ref[1, 0]
+    fetch_table.wait()
+
+
+def across_last_body(
+    h_ref, mx_ref, buf_ref, table_ref, nest_ref, even_ref, flow_far, hx_ref, nest_row_ref, flow_ref, push_ref, first_ref, sem
+):
+    n = h_ref.shape[0]
+    across(h_ref, mx_ref, buf_ref, table_ref, flow_ref, hx_ref, push_ref, first_ref)
+    out = pltpu.make_async_copy(flow_ref, flow_far, sem)
+    out.start()
+    edge = jnp.where(lax.axis_index("sub") == 0, hx_ref[0:1], hx_ref[n - 1 : n])
+    even = even_ref[...]
+    row = nest_ref[0:1] + edge + nest_ref[1:2] * nest_factor(even)
+    nest_row_ref[...] = jnp.broadcast_to(row, nest_row_ref.shape)
+    out.wait()
+
+
+def nest_factor(even):
+    return jnp.where(lax.axis_index("rows") == 0, even[0:1], even[4:5])
 
 
 def solve_lines(push, face, face_above, table):
@@ -150,7 +217,10 @@
     return jnp.concatenate(rows, 0), jnp.concatenate([nest_base, nest_coef], 0)
 
 
-def lines_body(own_ref, other_ref, cross_ref, along_ref, table_ref, flow_ref, face_ref, msg_ref, nest_ref, aux_ref, push_ref, wd_ref):
+def lines_body(
+    own_ref, other_ref, cross_ref, along_ref, hx_ref, other_hx_ref, table_ref,
+    flow_ref, face_ref, msg_ref, nest_ref, push_ref, wd_ref,
+):
     g = table_ref.shape[0]
     n = g // 2
     half = lax.axis_index("sub")
@@ -182,20 +252,36 @@
     flow, t_up, u_down = solve_lines(push_ref[...] + south, face, face_above, table)
     flow_ref[...] = flow
     face_ref[...] = face
-    msg_ref[...], nest_rows = messages(flow, face, t_up, u_down, table, is_first)
-    nest_ref[0:2] = nest_rows
-    nest_ref[2:8] = jnp.zeros((6, face.shape[1]), F32)
-    aux_ref[...] = jnp.broadcast_to(face_above, aux_ref.shape)
+    hx_top = jnp.where(lower, hx_ref[0:1], other_hx_ref[0:1])
+    hx_bottom = jnp.where(lower, other_hx_ref[1:2], hx_ref[1:2])
+    rows, nest_rows = messages(flow, face, t_up, u_down, table, is_first)
+    msg_ref[...] = rows
+    msg_ref[1:2] = rows[1:2] + hx_top
+    nest_ref[0:1] = nest_rows[0:1] + jnp.where(is_first, hx_top, hx_bottom)
+    nest_ref[1:2] = nest_rows[1:2]
+    nest_ref[2:3] = face_above
+    nest_ref[3:8] = jnp.zeros((5, face.shape[1]), F32)
 
 
 def upsampled(row, base):
     width = row.shape[1]
     rolled = pltpu.roll(jnp.broadcast_to(row, (8, width)), lax.rem(width - base, width), 1)
+    high = rolled.astype(jnp.bfloat16)
+    middle, low = split(rolled - high.astype(F32))
+    part = lax.broadcasted_iota(jnp.int32, rolled.shape, 0)
+    parts = jnp.where(
+        part == 0,
+        high.astype(F32),
+        jnp.where(part == 1, middle.astype(F32), jnp.where(part == 2, low.astype(F32), 0.0)),
+    ).astype(jnp.bfloat16)
     source = lax.broadcasted_iota(jnp.int32, (128, 256), 0)
     target = lax.broadcasted_iota(jnp.int32, (128, 256), 1)
-    pick = jnp.where(target // 2 == source, 1.0, 0.0).astype(F32)
-    pieces = [matmul(rolled[:, 128 * m : 128 * (m + 1)], pick) for m in range(width // 256)]
-    return jnp.concatenate(pieces, 1)[0:1]
+    pick = jnp.where(target // 2 == source, 1.0, 0.0).astype(jnp.bfloat16)
+    pieces = [
+        jnp.dot(parts[:, 128 * m : 128 * (m + 1)], pick, preferred_element_type=F32) for m in range(width // 256)
+    ]
+    picked = jnp.concatenate(pieces, 1)
+    return picked[0:1] + picked[1:2] + picked[2:3]
 
 
 def neighbours(even_ref, odd_ref):
@@ -206,8 +292,8 @@
 
 
 def between_body(
-    base_ref, flow_ref, face_ref, msg_ref, aux_ref, even_ref, odd_ref, even2_ref, odd2_ref, own_hx_ref, other_hx_ref,
-    nest_row_ref, table_ref, h_ref, next_flow_ref, next_msg_ref, next_nest_ref, hx_ref,
+    base_ref, flow_ref, face_ref, msg_ref, nest_ref, even_ref, even2_ref, odd2_ref, odd_ref, own_hx_ref, other_hx_ref,
+    nest_there_ref, even_there_ref, table_ref, h_ref, next_flow_ref, next_msg_ref, next_nest_ref, hx_ref,
 ):
     g = table_ref.shape[0]
     n = g // 2
@@ -234,7 +320,7 @@
     flux_above = above[5:6] + above[6:7] * own[0:1] + above[7:8] * above2[4:5]
     h_below = below[1:2] + below[2:3] * below2[0:1] + below[3:4] * own[4:5] - 0.5 * flux[g - 1 : g]
     h = hx_ref[...] + 0.5 * (flux - prev_row(flux, flux_above))
-    packet = upsampled(nest_row_ref[0:1], base_ref[0])
+    packet = upsampled(nest_there_ref[0:1] + nest_there_ref[1:2] * nest_factor(even_there_ref[...]), base_ref[0])
     rows = row_iota(h.shape)
     blend = jnp.logical_and(
         nearfield,
@@ -244,7 +330,7 @@
     hx_ref[...] = h
     h_ref[...] = hx_ref[pl.ds(mine, n)]
     push = flow + 0.5 * face * (next_row(h, h_below) - h)
-    next_flow, t_up, u_down = solve_lines(push, face, aux_ref[0:1], table)
+    next_flow, t_up, u_down = solve_lines(push, face, nest_ref[2:3], table)
     next_flow_ref[...] = next_flow
     next_msg_ref[...], nest_rows = messages(next_flow, face, t_up, u_down, table, is_first)
     next_nest_ref[0:2] = nest_rows
@@ -252,8 +338,8 @@
 
 
 def finish_body(
-    base_ref, flow_ref, face_ref, msg_ref, even_ref, odd_ref, above2_ref, hx_ref, nest_row_ref, table_ref,
-    h_ref, my_ref, flux_ref,
+    base_ref, flow_ref, face_ref, msg_ref, even_ref, above2_ref, odd_ref, hx_ref, nest_row_ref, table_ref,
+    h_far, my_far, h_ref, my_ref, sems,
 ):
     g = table_ref.shape[0]
     n = g // 2
@@ -262,17 +348,21 @@
     is_first = jnp.logical_and(block == 0, half == 0)
     is_last = jnp.logical_and(block == lax.axis_size("rows") - 1, half == 1)
     nearfield = lax.axis_index("nest") == 1
-    mine = pl.multiple_of(half * n, n)
+    mine = pl.ds(pl.multiple_of(half * n, n), n)
     own = msg_ref[...]
     above, below = neighbours(even_ref, odd_ref)
-    table = table_ref[...]
-    flow = flow_ref[...] + table[:, g - 1 : g] * below[0:1] + table[:, 0:1] * above[4:5]
-    flux = face_ref[...] * flow
+    t_row = below[0:1]
+    u_row = above[4:5]
+    table = table_ref[mine]
+    flow = flow_ref[mine] + table[:, g - 1 : g] * t_row + table[:, 0:1] * u_row
+    my_ref[...] = flow
+    copy_my = pltpu.make_async_copy(my_ref, my_far, sems.at[0])
+    copy_my.start()
     flux_above = above[5:6] + above[6:7] * own[0:1] + above[7:8] * above2_ref[4:5]
-    flux_ref[0] = flow
-    flux_ref[1] = flux - prev_row(flux, flux_above)
-    my_ref[...] = flux_ref[0, pl.ds(mine, n)]
-    h = hx_ref[...] + 0.5 * flux_ref[1, pl.ds(mine, n)]
+    flow_mid = flow_ref[n - 1 : n] + table_ref[n - 1 : n, g - 1 : g] * t_row + table_ref[n - 1 : n, 0:1] * u_row
+    before = jnp.where(half == 0, flux_above, face_ref[n - 1 : n] * flow_mid)
+    flux = face_ref[mine] * flow
+    h = hx_ref[...] + 0.5 * (flux - prev_row(flux, before))
     packet = upsampled(nest_row_ref[0:1], base_ref[0])
     rows = row_iota(h.shape)
     blend = jnp.logical_and(
@@ -280,66 +370,65 @@
         jnp.logical_or(jnp.logical_and(is_first, rows == 0), jnp.logical_and(is_last, rows == n - 1)),
     )
     h_ref[...] = jnp.where(blend, 0.5 * h + 0.5 * packet, h)
+    copy_h = pltpu.make_async_copy(h_ref, h_far, sems.at[1])
+    copy_h.start()
+    copy_my.wait()
+    copy_h.wait()
 
 
 def on_device(elevation, momentum_x, momentum_y, depth, wet_mask, inverse_x, inverse_y, nest_map):
     n, width = elevation.shape[1:]
     g = inverse_y.shape[-1]
     assert g == 2 * n and lax.axis_size("sub") == 2
-    block = lax.axis_index("rows")
-    half = lax.axis_index("sub")
-    base = nest_map[0, 1, 0:1]
     height = elevation[0]
     table_x = inverse_x[0]
-    table_y = lax.dynamic_index_in_dim(inverse_y[0], block, 0, keepdims=False)
-    is_first = block == 0
     solve_flops = 2 * g * g * width * 2
-
-    buf, edge = call(prepare_body, [(2 * n + 8, width), (8, width)], [height, momentum_y[0], depth[0], wet_mask[0]])
+    part = pltpu.VMEM((n, width), F32)
+    dma = pltpu.SemaphoreType.DMA
+
+    buf, edge = call(
+        prepare_body, [(2 * n + 8, width), (8, width)], [height, momentum_y[0], depth[0], wet_mask[0]],
+        [part, part, part, pltpu.VMEM((n, width), jnp.int32), dma((4,))], far=(0, 1, 2, 3), vmem=60,
+    )
     other = swap_halves(buf)
     cross = moved(edge, lambda k, s: (k + 1, 0) if s == 1 else (k - 1, 1))
     along = moved(edge, lambda k, s: (k + 1, 1) if s == 1 else (k - 1, 0))
-    flow_x, hx = call(
-        across_body, [(n, width)] * 2, [height, momentum_x[0], buf, table_x],
-        [pltpu.VMEM((n, width), F32)] * 2, solve_flops,
-    )
-    hx_edge = jnp.concatenate([hx[0:1], hx[n - 1 : n]], 0)
+    flow_x, hx, hx_edge, table_y, base = call(
+        across_first_body, [(n, width), (n, width), (8, width), (g, g), jax.ShapeDtypeStruct((1,), jnp.int32)],
+        [height, momentum_x[0], buf, table_x, inverse_y[0], nest_map, along],
+        [part, part, pltpu.SMEM((2, 128), jnp.int32), dma((2,))], solve_flops, far=(4, 5),
+    )
     other_edge = swap_halves(hx_edge)
+    flow, face, msg, nest = call(
+        lines_body, [(g, width), (g, width), (8, width), (8, width)],
+        [buf, other, cross, along, hx_edge, other_edge, table_y], [pltpu.VMEM((g, width), F32)] * 2, solve_flops,
+    )
+    hx, msg = lax.optimization_barrier((hx, msg))
     other_hx = swap_halves(hx)
-    hx_top = jnp.where(half == 0, hx_edge[0:1], other_edge[0:1])
-    hx_bottom = jnp.where(half == 0, other_edge[1:2], hx_edge[1:2])
-    flow, face, msg, nest_rows, aux = call(
-        lines_body, [(g, width), (g, width), (8, width), (8, width), (8, width)],
-        [buf, other, cross, along, table_y], [pltpu.VMEM((g, width), F32)] * 2, solve_flops,
-    )
-    msg = jnp.concatenate([msg[0:1], msg[1:2] + hx_top, msg[2:]], 0)
+    odd = moved(msg, lambda k, s: (((k + 1) ^ 1) - 1, s))
     even = moved(msg, lambda k, s: (k ^ 1, s))
+    odd2 = moved(msg, lambda k, s: (((k + 2) ^ 2) - 2, s))
+    even2 = moved(msg, lambda k, s: (k ^ 2, s))
+    nest_there = swap_nest(nest)
+    even_there = swap_nest(even)
+    height, flow, msg, next_nest = call(
+        between_body, [(n, width), (g, width), (8, width), (8, width)],
+        [base, flow, face, msg, nest, even, even2, odd2, odd, hx, other_hx, nest_there, even_there, table_y],
+        [pltpu.VMEM((g, width), F32)], solve_flops,
+    )
     odd = moved(msg, lambda k, s: (((k + 1) ^ 1) - 1, s))
-    even2 = moved(msg, lambda k, s: (k ^ 2, s))
-    odd2 = moved(msg, lambda k, s: (((k + 2) ^ 2) - 2, s))
-    nest_row = nest_rows[0:1] + jnp.where(is_first, hx_top, hx_bottom) + nest_rows[1:2] * jnp.where(is_first, even[0:1], even[4:5])
-    nest_row = swap_nest(nest_row)
-    height, flow, msg, nest_rows = call(
-        between_body, [(n, width), (g, width), (8, width), (8, width)],
-        [base, flow, face, msg, aux, even, odd, even2, odd2, hx, other_hx, nest_row, table_y],
-        [pltpu.VMEM((g, width), F32)], solve_flops,
-    )
     even = moved(msg, lambda k, s: (k ^ 1, s))
-    odd = moved(msg, lambda k, s: (((k + 1) ^ 1) - 1, s))
     above2 = moved(msg, lambda k, s: (k + 2, s))
-    flow_x, hx = call(
-        across_body, [(n, width)] * 2, [height, flow_x, buf, table_x],
-        [pltpu.VMEM((n, width), F32)] * 2, solve_flops,
-    )
-    nest_row = (
-        nest_rows[0:1] + jnp.where(half == 0, hx[0:1], hx[n - 1 : n])
-        + nest_rows[1:2] * jnp.where(is_first, even[0:1], even[4:5])
+    flow_x, hx, nest_row = call(
+        across_last_body, [(n, width), (n, width), (8, width)],
+        [height, flow_x, buf, table_x, next_nest, even],
+        [part, part, part, dma], solve_flops, far_outs=(0,),
     )
     nest_row = swap_nest(nest_row)
     height, flow_y = call(
         finish_body, [(n, width), (n, width)],
-        [base, flow, face, msg, even, odd, above2, hx, nest_row, table_y],
-        [pltpu.VMEM((2, g, width), F32)],
+        [base, flow, face, msg, even, above2, odd, hx, nest_row, table_y],
+        [part, part, dma((2,))], far_outs=(0, 1),
     )
     return height[None], flow_x[None], flow_y[None]
 

time: 55.1 us -> 49.2 us (0.89)
  the two profiles are of different devices: /device:TPU:9 before, /device:TPU:0 now
where the time goes in v2:
time: 49.2 us; the launch traced here: 48.9 us
  starting transfers between devices  26.7 us (54%)
  Pallas kernels  10.1 us (21%)
  waiting for transfers between devices  9.2 us (19%)
  local copies, waits for them, and re-layouts  2.11 us (4%)
  between operations  0.82 us (2%)
    ppermute x9, starting transfers between devices, moved(): return lax.ppermute(value, LINE, pairs)  19.4 us
    pallas_call x6, Pallas kernels, call(): pl.pallas_call(body, out_shape=shapes, in_specs=[spec(i, x, far) for i, x...  10.1 us
    ppermute x3, starting transfers between devices, swap_halves(): return lax.ppermute(value, 'sub', [(0, 1), (1, 0)])  6.66 us
    ppermute x9, waiting for transfers between devices, moved(): return lax.ppermute(value, LINE, pairs)  5.44 us
    ppermute x3, waiting for transfers between devices, swap_halves(): return lax.ppermute(value, 'sub', [(0, 1), (1, 0)])  2.58 us
    unnamed x14, local copies, waits for them, and re-layouts  2.11 us
    ppermute x3, waiting for transfers between devices, swap_nest(): return lax.ppermute(value, 'nest', [(0, 1), (1, 0)])  1.18 us
  transfers between devices with their start and end apart: 15, of which 4 were waited for; matrix products, arithmetic and copies ran while one was open for 0% of the time, Pallas kernels for 7%

profile of v2, /device:TPU:0, one launch (start us, length us, event | category | flops | bytes accessed | tf_op | source)
XLA Modules:
  0.0 48.9 jit_solution(13131262317440431288)
XLA Ops:
  0.6 0.0 copy-start.6
  0.6 0.0 copy-start.2
  0.7 0.0 copy-start.3
  0.7 0.0 copy-start.5
  0.7 2.2 %shard_map.103 = (f32[136,1024]{1,0:T(8,128)}, f32[8,1024]{1,0:T(8,128)}) custom-call(f32[64,1024]{1,0:T(8,128)} %bitcast.12, f32[64,1024]{1,0:T(8,128)} %bitcast.16, f32[64,1024]{1,0:T(8,128)} %bitcast.17, s32[64,1024]{1,0:T(8,128)} %bitcast.18), custom_call_target="tpu_custom_call" | custom-call | bytes 589824 | tf_op jit(solution)/shard_map/pallas_call | solution.py:42
  2.9 3.0 %collective-permute-start.1 = (f32[136,1024]{1,0:T(8,128)}, f32[136,1024]{1,0:T(8,128)S(1)}, u32[]{:S(2)}, u32[]{:S(2)}) collective-permute-start(f32[136,1024]{1,0:T(8,128)} %get-tuple-element.25.buf_ref.own_ref), channel_id=1, source_target_pairs={{0,1},{1,0},{2,3},{3,2},{4,5},{5,4},{6,7},{7,6},{8,9},{9,8},{10,11... | collective-permute-start | bytes 1671176 | tf_op jit(solution)/shard_map/ppermute | solution.py:26
  5.9 1.3 %collective-permute-start = (f32[8,1024]{1,0:T(8,128)}, f32[8,1024]{1,0:T(8,128)S(1)}, u32[]{:S(2)}, u32[]{:S(2)}) collective-permute-start(f32[8,1024]{1,0:T(8,128)} %get-tuple-element.26), channel_id=1, source_target_pairs={{1,3},{2,0},{3,5},{4,2},{5,7},{6,4},{7,9},{8,6},{9,11},{10,8},{11,... | collective-permute-start | bytes 98312 | tf_op jit(solution)/shard_map/ppermute | solution.py:22
  7.2 0.7 %collective-permute-start.2 = (f32[8,1024]{1,0:T(8,128)}, f32[8,1024]{1,0:T(8,128)S(1)}, u32[]{:S(2)}, u32[]{:S(2)}) collective-permute-start(f32[8,1024]{1,0:T(8,128)} %get-tuple-element.26), channel_id=1, source_target_pairs={{1,2},{2,1},{3,4},{4,3},{5,6},{6,5},{7,8},{8,7},{9,10},{10,9},{11,... | collective-permute-start | bytes 98312 | tf_op jit(solution)/shard_map/ppermute | solution.py:22
  7.9 4.0 %collective-permute-done.along_ref = f32[8,1024]{1,0:T(8,128)S(1)} collective-permute-done((f32[8,1024]{1,0:T(8,128)}, f32[8,1024]{1,0:T(8,128)S(1)}, u32[]{:S(2)}, u32[]{:S(2)}) %collective-permute-start) | collective-permute-done | bytes 32800 | tf_op jit(solution)/shard_map/ppermute | solution.py:22
  11.9 0.0 copy-done.6
  11.9 0.0 copy-done.2
  11.9 0.0 copy-done.3
  11.9 0.0 copy-done.5
  11.9 0.0 copy-start
  11.9 1.0 %copy-done = f32[136,1024]{1,0:T(8,128)S(1)} copy-done((f32[136,1024]{1,0:T(8,128)S(1)}, f32[136,1024]{1,0:T(8,128)}, u32[]{:S(2)}) %copy-start) | copy-done | bytes 557080
  13.0 0.0 copy-start.4
  13.0 1.0 %copy-done.4 = f32[1,8,128,128]{3,2,1,0:T(8,128)S(1)} copy-done((f32[1,8,128,128]{3,2,1,0:T(8,128)S(1)}, f32[1,8,128,128]{3,2,1,0:T(8,128)}, u32[]{:S(2)}) %copy-start.4) | copy-done | bytes 524312
  14.0 0.0 copy-start.1
  14.0 1.7 %shard_map.104 = (f32[64,1024]{1,0:T(8,128)S(1)}, f32[64,1024]{1,0:T(8,128)S(1)}, f32[8,1024]{1,0:T(8,128)S(1)}, f32[128,128]{1,0:T(8,128)S(1)}, s32[1]{0:T(128)}) custom-call(f32[64,1024]{1,0:T(8,128)S(1)} %bitcast.13, f32[64,1024]{1,0:T(8,128)S(1)} %bitcast.15, f32[136,1024]{1,0:T(8,128)S(1)} %copy-done, f32[8,128,128]{2,1,0:T(8,128)S(1)} %bitcast.10, ...), custom_call_target="tpu_custom_call" | custom-call | flops 67108864 | bytes 2260996 | tf_op jit(solution)/shard_map/pallas_call | solution.py:42
  15.7 1.4 %collective-permute-start.3 = (f32[8,1024]{1,0:T(8,128)S(1)}, f32[8,1024]{1,0:T(8,128)S(1)}, u32[]{:S(2)}, u32[]{:S(2)}) collective-permute-start(f32[8,1024]{1,0:T(8,128)S(1)} %get-tuple-element.28.hx_ref), channel_id=1, source_target_pairs={{0,1},{1,0},{2,3},{3,2},{4,5},{5,4},{6,7},{7,6},{8,9},{9,8},{10,11... | collective-permute-start | bytes 98312 | tf_op jit(solution)/shard_map/ppermute | solution.py:26
  17.1 0.0 collective-permute-done.2.cross_ref
  17.1 2.6 %collective-permute-done.3.other_hx_ref = f32[8,1024]{1,0:T(8,128)S(1)} collective-permute-done((f32[8,1024]{1,0:T(8,128)S(1)}, f32[8,1024]{1,0:T(8,128)S(1)}, u32[]{:S(2)}, u32[]{:S(2)}) %collective-permute-start.3) | collective-permute-done | bytes 32800 | tf_op jit(solution)/shard_map/ppermute | solution.py:26
  19.7 0.0 collective-permute-done.1.other_ref
  19.7 0.0 copy-done.1
  19.7 1.0 %shard_map.105 = (f32[128,1024]{1,0:T(8,128)S(1)}, f32[128,1024]{1,0:T(8,128)S(1)}, f32[8,1024]{1,0:T(8,128)S(1)}, f32[8,1024]{1,0:T(8,128)S(1)}) custom-call(f32[136,1024]{1,0:T(8,128)S(1)} %copy-done.1, f32[136,1024]{1,0:T(8,128)S(1)} %collective-permute-done.1.other_ref, f32[8,1024]{1,0:T(8,128)S(1)} %collective-permute-done.2.cross_ref, ...), custom_call_target="tpu_custom_call" | custom-call | flops 67108864 | bytes 2424832 | tf_op jit(solution)/shard_map/pallas_call | solution.py:42
  20.7 2.2 %collective-permute-start.8 = (f32[64,1024]{1,0:T(8,128)S(1)}, f32[64,1024]{1,0:T(8,128)S(1)}, u32[]{:S(2)}, u32[]{:S(2)}) collective-permute-start(f32[64,1024]{1,0:T(8,128)S(1)} %get-tuple-element.36.own_hx_ref), channel_id=1, source_target_pairs={{0,1},{1,0},{2,3},{3,2},{4,5},{5,4},{6,7},{7,6},{8,9},{9,8},{10,11... | collective-permute-start | bytes 786440 | tf_op jit(solution)/shard_map/ppermute | solution.py:26
  23.0 0.7 %collective-permute-start.7 = (f32[8,1024]{1,0:T(8,128)S(1)}, f32[8,1024]{1,0:T(8,128)S(1)}, u32[]{:S(2)}, u32[]{:S(2)}) collective-permute-start(f32[8,1024]{1,0:T(8,128)S(1)} %get-tuple-element.34.msg_ref), channel_id=1, source_target_pairs={{2,4},{3,5},{4,2},{5,3},{6,8},{7,9},{8,6},{9,7},{10,12},{11,13},{1... | collective-permute-start | bytes 98312 | tf_op jit(solution)/shard_map/ppermute | solution.py:22
  23.6 4.4 %collective-permute-start.4 = (f32[8,1024]{1,0:T(8,128)S(1)}, f32[8,1024]{1,0:T(8,128)S(1)}, u32[]{:S(2)}, u32[]{:S(2)}) collective-permute-start(f32[8,1024]{1,0:T(8,128)S(1)} %get-tuple-element.34.msg_ref), channel_id=1, source_target_pairs={{0,2},{1,3},{2,0},{3,1},{4,6},{5,7},{6,4},{7,5},{8,10},{9,11},{10,... | collective-permute-start | bytes 98312 | tf_op jit(solution)/shard_map/ppermute | solution.py:22
  28.0 0.7 %collective-permute-start.6 = (f32[8,1024]{1,0:T(8,128)S(1)}, f32[8,1024]{1,0:T(8,128)S(1)}, u32[]{:S(2)}, u32[]{:S(2)}) collective-permute-start(f32[8,1024]{1,0:T(8,128)S(1)} %get-tuple-element.34.msg_ref), channel_id=1, source_target_pairs={{4,8},{5,9},{6,10},{7,11},{8,4},{9,5},{10,6},{11,7},{20,24},{21,25... | collective-permute-start | bytes 98312 | tf_op jit(solution)/shard_map/ppermute | solution.py:22
  28.6 4.5 %collective-permute-start.5 = (f32[8,1024]{1,0:T(8,128)S(1)}, f32[8,1024]{1,0:T(8,128)S(1)}, u32[]{:S(2)}, u32[]{:S(2)}) collective-permute-start(f32[8,1024]{1,0:T(8,128)S(1)} %get-tuple-element.34.msg_ref), channel_id=1, source_target_pairs={{0,4},{1,5},{2,6},{3,7},{4,0},{5,1},{6,2},{7,3},{8,12},{9,13},{10,... | collective-permute-start | bytes 98312 | tf_op jit(solution)/shard_map/ppermute | solution.py:22
  33.1 0.0 collective-permute-done.7.odd_ref
  33.1 0.0 collective-permute-start.9
  33.1 0.0 collective-permute-done.4.even_ref
  33.1 0.5 %collective-permute-start.10 = (f32[8,1024]{1,0:T(8,128)S(1)}, f32[8,1024]{1,0:T(8,128)S(1)}, u32[]{:S(2)}, u32[]{:S(2)}) collective-permute-start(f32[8,1024]{1,0:T(8,128)S(1)} %collective-permute-done.4.even_ref), channel_id=1, source_target_pairs={{0,16},{16,0},{1,17},{17,1},{2,18},{18,2},{3,19},{19,3},{4,20},{20... | collective-permute-start | bytes 98312 | tf_op jit(solution)/shard_map/ppermute | solution.py:30
  33.6 0.0 collective-permute-done.6.odd2_ref
  33.6 1.4 %collective-permute-done.5.even2_ref = f32[8,1024]{1,0:T(8,128)S(1)} collective-permute-done((f32[8,1024]{1,0:T(8,128)S(1)}, f32[8,1024]{1,0:T(8,128)S(1)}, u32[]{:S(2)}, u32[]{:S(2)}) %collective-permute-start.5) | collective-permute-done | bytes 32800 | tf_op jit(solution)/shard_map/ppermute | solution.py:22
  35.0 0.0 collective-permute-done.9.nest_there_ref
  35.0 0.0 collective-permute-done.10.even_there_ref
  35.0 0.0 collective-permute-done.8.other_hx_ref
  35.0 1.9 %shard_map.106 = (f32[64,1024]{1,0:T(8,128)S(1)}, f32[128,1024]{1,0:T(8,128)S(1)}, f32[8,1024]{1,0:T(8,128)S(1)}, f32[8,1024]{1,0:T(8,128)S(1)}) custom-call(s32[1]{0:T(128)} %get-tuple-element.27.base_ref, f32[128,1024]{1,0:T(8,128)S(1)} %get-tuple-element.30.flow_ref, f32[128,1024]{1,0:T(8,128)S(1)} %get-tuple-element.31.face_ref, ...), custom_call_target="tpu_custom_call" | custom-call | flops 67108864 | bytes 2752516 | tf_op jit(solution)/shard_map/pallas_call | solution.py:42
  36.9 0.5 collective-permute-start.11
  37.4 0.7 %collective-permute-start.13 = (f32[8,1024]{1,0:T(8,128)S(1)}, f32[8,1024]{1,0:T(8,128)S(1)}, u32[]{:S(2)}, u32[]{:S(2)}) collective-permute-start(f32[8,1024]{1,0:T(8,128)S(1)} %get-tuple-element.38.msg_ref), channel_id=1, source_target_pairs={{2,4},{3,5},{4,2},{5,3},{6,8},{7,9},{8,6},{9,7},{10,12},{11,13},{1... | collective-permute-start | bytes 98312 | tf_op jit(solution)/shard_map/ppermute | solution.py:22
  38.0 6.2 %collective-permute-start.12 = (f32[8,1024]{1,0:T(8,128)S(1)}, f32[8,1024]{1,0:T(8,128)S(1)}, u32[]{:S(2)}, u32[]{:S(2)}) collective-permute-start(f32[8,1024]{1,0:T(8,128)S(1)} %get-tuple-element.38.msg_ref), channel_id=1, source_target_pairs={{0,4},{1,5},{2,6},{3,7},{4,8},{5,9},{6,10},{7,11},{8,12},{9,13},{1... | collective-permute-start | bytes 98312 | tf_op jit(solution)/shard_map/ppermute | solution.py:22
  44.3 0.0 collective-permute-done.11.even_ref
  44.3 1.7 %shard_map.107 = (f32[64,1024]{1,0:T(8,128)}, f32[64,1024]{1,0:T(8,128)S(1)}, f32[8,1024]{1,0:T(8,128)S(1)}) custom-call(f32[64,1024]{1,0:T(8,128)S(1)} %get-tuple-element.39.h_ref, f32[64,1024]{1,0:T(8,128)S(1)} %get-tuple-element.40.mx_ref, f32[136,1024]{1,0:T(8,128)S(1)} %copy-done.1, f32[8,128,128]{2,1,0:T(8,128)S(1)} %bitcast.11, ...), custom_call_target="tpu_custom_call" | custom-call | flops 67108864 | bytes 2228224 | tf_op jit(solution)/shard_map/pallas_call | solution.py:42
  46.0 0.1 collective-permute-start.14
  46.1 0.0 collective-permute-done.13.odd_ref
  46.1 0.0 collective-permute-done.12.above2_ref
  46.1 1.2 %collective-permute-done.14.nest_row_ref = f32[8,1024]{1,0:T(8,128)S(1)} collective-permute-done((f32[8,1024]{1,0:T(8,128)S(1)}, f32[8,1024]{1,0:T(8,128)S(1)}, u32[]{:S(2)}, u32[]{:S(2)}) %collective-permute-start.14) | collective-permute-done | bytes 32800 | tf_op jit(solution)/shard_map/ppermute | solution.py:30
  47.3 1.6 %shard_map.108 = (f32[64,1024]{1,0:T(8,128)}, f32[64,1024]{1,0:T(8,128)}) custom-call(s32[1]{0:T(128)} %get-tuple-element.27.base_ref, f32[128,1024]{1,0:T(8,128)S(1)} %get-tuple-element.37.flow_ref, f32[128,1024]{1,0:T(8,128)S(1)} %get-tuple-element.31.face_ref, f32[8,1024]{1,0:T(8,128)S(1)} %get-tuple-element.38.msg_ref, ...), custom_call_target="tpu_custom_call" | custom-call | bytes 2064388 | tf_op jit(solution)/shard_map/pallas_call | solution.py:42
Async XLA Ops:
  0.6 11.3 %copy-start.6 = (s32[2,2,1024]{2,1,0:T(2,128)S(1)}, s32[2,2,1024]{2,1,0:T(2,128)}, u32[]{:S(2)}) copy-start(s32[2,2,1024]{2,1,0:T(2,128)} %map_far.1) | copy-start | bytes 49156
  0.6 11.3 %copy-start.2 = (f32[1,8,128,128]{3,2,1,0:T(8,128)S(1)}, f32[1,8,128,128]{3,2,1,0:T(8,128)}, u32[]{:S(2)}) copy-start(f32[1,8,128,128]{3,2,1,0:T(8,128)} %param.13) | copy-start | bytes 1572868
  0.7 11.3 %copy-start.3 = (f32[1,64,1024]{2,1,0:T(8,128)S(1)}, f32[1,64,1024]{2,1,0:T(8,128)}, u32[]{:S(2)}) copy-start(f32[1,64,1024]{2,1,0:T(8,128)} %param.8) | copy-start | bytes 786436
  0.7 11.3 %copy-start.5 = (f32[1,64,1024]{2,1,0:T(8,128)S(1)}, f32[1,64,1024]{2,1,0:T(8,128)}, u32[]{:S(2)}) copy-start(f32[1,64,1024]{2,1,0:T(8,128)} %param.9) | copy-start | bytes 786436
  2.9 16.8 %collective-permute-start.1 = (f32[136,1024]{1,0:T(8,128)}, f32[136,1024]{1,0:T(8,128)S(1)}, u32[]{:S(2)}, u32[]{:S(2)}) collective-permute-start(f32[136,1024]{1,0:T(8,128)} %get-tuple-element.25.buf_ref.own_ref), channel_id=1, source_target_pairs={{0,1},{1,0},{2,3},{3,2},{4,5},{5,4},{6,7},{7,6},{8,9},{9,8},{10,11... | collective-permute-start | bytes 1671176 | tf_op jit(solution)/shard_map/ppermute | solution.py:26
  5.9 6.0 %collective-permute-start = (f32[8,1024]{1,0:T(8,128)}, f32[8,1024]{1,0:T(8,128)S(1)}, u32[]{:S(2)}, u32[]{:S(2)}) collective-permute-start(f32[8,1024]{1,0:T(8,128)} %get-tuple-element.26), channel_id=1, source_target_pairs={{1,3},{2,0},{3,5},{4,2},{5,7},{6,4},{7,9},{8,6},{9,11},{10,8},{11,... | collective-permute-start | bytes 98312 | tf_op jit(solution)/shard_map/ppermute | solution.py:22
  7.2 9.9 %collective-permute-start.2 = (f32[8,1024]{1,0:T(8,128)}, f32[8,1024]{1,0:T(8,128)S(1)}, u32[]{:S(2)}, u32[]{:S(2)}) collective-permute-start(f32[8,1024]{1,0:T(8,128)} %get-tuple-element.26), channel_id=1, source_target_pairs={{1,2},{2,1},{3,4},{4,3},{5,6},{6,5},{7,8},{8,7},{9,10},{10,9},{11,... | collective-permute-start | bytes 98312 | tf_op jit(solution)/shard_map/ppermute | solution.py:22
  11.9 1.1 %copy-start = (f32[136,1024]{1,0:T(8,128)S(1)}, f32[136,1024]{1,0:T(8,128)}, u32[]{:S(2)}) copy-start(f32[136,1024]{1,0:T(8,128)} %get-tuple-element.25.buf_ref.own_ref) | copy-start | bytes 1671172
  13.0 1.0 %copy-start.4 = (f32[1,8,128,128]{3,2,1,0:T(8,128)S(1)}, f32[1,8,128,128]{3,2,1,0:T(8,128)}, u32[]{:S(2)}) copy-start(f32[1,8,128,128]{3,2,1,0:T(8,128)} %param.14) | copy-start | bytes 1572868
  14.0 5.7 %copy-start.1 = (f32[136,1024]{1,0:T(8,128)S(1)}, f32[136,1024]{1,0:T(8,128)}, u32[]{:S(2)}) copy-start(f32[136,1024]{1,0:T(8,128)} %get-tuple-element.25.buf_ref.own_ref) | copy-start | bytes 1671172
  15.7 4.0 %collective-permute-start.3 = (f32[8,1024]{1,0:T(8,128)S(1)}, f32[8,1024]{1,0:T(8,128)S(1)}, u32[]{:S(2)}, u32[]{:S(2)}) collective-permute-start(f32[8,1024]{1,0:T(8,128)S(1)} %get-tuple-element.28.hx_ref), channel_id=1, source_target_pairs={{0,1},{1,0},{2,3},{3,2},{4,5},{5,4},{6,7},{7,6},{8,9},{9,8},{10,11... | collective-permute-start | bytes 98312 | tf_op jit(solution)/shard_map/ppermute | solution.py:26
  20.7 14.3 %collective-permute-start.8 = (f32[64,1024]{1,0:T(8,128)S(1)}, f32[64,1024]{1,0:T(8,128)S(1)}, u32[]{:S(2)}, u32[]{:S(2)}) collective-permute-start(f32[64,1024]{1,0:T(8,128)S(1)} %get-tuple-element.36.own_hx_ref), channel_id=1, source_target_pairs={{0,1},{1,0},{2,3},{3,2},{4,5},{5,4},{6,7},{7,6},{8,9},{9,8},{10,11... | collective-permute-start | bytes 786440 | tf_op jit(solution)/shard_map/ppermute | solution.py:26
  23.0 10.1 %collective-permute-start.7 = (f32[8,1024]{1,0:T(8,128)S(1)}, f32[8,1024]{1,0:T(8,128)S(1)}, u32[]{:S(2)}, u32[]{:S(2)}) collective-permute-start(f32[8,1024]{1,0:T(8,128)S(1)} %get-tuple-element.34.msg_ref), channel_id=1, source_target_pairs={{2,4},{3,5},{4,2},{5,3},{6,8},{7,9},{8,6},{9,7},{10,12},{11,13},{1... | collective-permute-start | bytes 98312 | tf_op jit(solution)/shard_map/ppermute | solution.py:22
  23.6 9.5 %collective-permute-start.4 = (f32[8,1024]{1,0:T(8,128)S(1)}, f32[8,1024]{1,0:T(8,128)S(1)}, u32[]{:S(2)}, u32[]{:S(2)}) collective-permute-start(f32[8,1024]{1,0:T(8,128)S(1)} %get-tuple-element.34.msg_ref), channel_id=1, source_target_pairs={{0,2},{1,3},{2,0},{3,1},{4,6},{5,7},{6,4},{7,5},{8,10},{9,11},{10,... | collective-permute-start | bytes 98312 | tf_op jit(solution)/shard_map/ppermute | solution.py:22
  28.0 5.6 %collective-permute-start.6 = (f32[8,1024]{1,0:T(8,128)S(1)}, f32[8,1024]{1,0:T(8,128)S(1)}, u32[]{:S(2)}, u32[]{:S(2)}) collective-permute-start(f32[8,1024]{1,0:T(8,128)S(1)} %get-tuple-element.34.msg_ref), channel_id=1, source_target_pairs={{4,8},{5,9},{6,10},{7,11},{8,4},{9,5},{10,6},{11,7},{20,24},{21,25... | collective-permute-start | bytes 98312 | tf_op jit(solution)/shard_map/ppermute | solution.py:22
  28.6 6.4 %collective-permute-start.5 = (f32[8,1024]{1,0:T(8,128)S(1)}, f32[8,1024]{1,0:T(8,128)S(1)}, u32[]{:S(2)}, u32[]{:S(2)}) collective-permute-start(f32[8,1024]{1,0:T(8,128)S(1)} %get-tuple-element.34.msg_ref), channel_id=1, source_target_pairs={{0,4},{1,5},{2,6},{3,7},{4,0},{5,1},{6,2},{7,3},{8,12},{9,13},{10,... | collective-permute-start | bytes 98312 | tf_op jit(solution)/shard_map/ppermute | solution.py:22
  33.1 1.9 %collective-permute-start.9 = (f32[8,1024]{1,0:T(8,128)S(1)}, f32[8,1024]{1,0:T(8,128)S(1)}, u32[]{:S(2)}, u32[]{:S(2)}) collective-permute-start(f32[8,1024]{1,0:T(8,128)S(1)} %get-tuple-element.35.nest_ref), channel_id=1, source_target_pairs={{0,16},{16,0},{1,17},{17,1},{2,18},{18,2},{3,19},{19,3},{4,20},{20... | collective-permute-start | bytes 98312 | tf_op jit(solution)/shard_map/ppermute | solution.py:30
  33.1 1.9 %collective-permute-start.10 = (f32[8,1024]{1,0:T(8,128)S(1)}, f32[8,1024]{1,0:T(8,128)S(1)}, u32[]{:S(2)}, u32[]{:S(2)}) collective-permute-start(f32[8,1024]{1,0:T(8,128)S(1)} %collective-permute-done.4.even_ref), channel_id=1, source_target_pairs={{0,16},{16,0},{1,17},{17,1},{2,18},{18,2},{3,19},{19,3},{4,20},{20... | collective-permute-start | bytes 98312 | tf_op jit(solution)/shard_map/ppermute | solution.py:30
  36.9 7.4 %collective-permute-start.11 = (f32[8,1024]{1,0:T(8,128)S(1)}, f32[8,1024]{1,0:T(8,128)S(1)}, u32[]{:S(2)}, u32[]{:S(2)}) collective-permute-start(f32[8,1024]{1,0:T(8,128)S(1)} %get-tuple-element.38.msg_ref), channel_id=1, source_target_pairs={{0,2},{1,3},{2,0},{3,1},{4,6},{5,7},{6,4},{7,5},{8,10},{9,11},{10,... | collective-permute-start | bytes 98312 | tf_op jit(solution)/shard_map/ppermute | solution.py:22
  37.4 8.7 %collective-permute-start.13 = (f32[8,1024]{1,0:T(8,128)S(1)}, f32[8,1024]{1,0:T(8,128)S(1)}, u32[]{:S(2)}, u32[]{:S(2)}) collective-permute-start(f32[8,1024]{1,0:T(8,128)S(1)} %get-tuple-element.38.msg_ref), channel_id=1, source_target_pairs={{2,4},{3,5},{4,2},{5,3},{6,8},{7,9},{8,6},{9,7},{10,12},{11,13},{1... | collective-permute-start | bytes 98312 | tf_op jit(solution)/shard_map/ppermute | solution.py:22
  38.0 8.1 %collective-permute-start.12 = (f32[8,1024]{1,0:T(8,128)S(1)}, f32[8,1024]{1,0:T(8,128)S(1)}, u32[]{:S(2)}, u32[]{:S(2)}) collective-permute-start(f32[8,1024]{1,0:T(8,128)S(1)} %get-tuple-element.38.msg_ref), channel_id=1, source_target_pairs={{0,4},{1,5},{2,6},{3,7},{4,8},{5,9},{6,10},{7,11},{8,12},{9,13},{1... | collective-permute-start | bytes 98312 | tf_op jit(solution)/shard_map/ppermute | solution.py:22
  46.0 1.3 %collective-permute-start.14 = (f32[8,1024]{1,0:T(8,128)S(1)}, f32[8,1024]{1,0:T(8,128)S(1)}, u32[]{:S(2)}, u32[]{:S(2)}) collective-permute-start(f32[8,1024]{1,0:T(8,128)S(1)} %get-tuple-element.43), channel_id=1, source_target_pairs={{0,16},{16,0},{1,17},{17,1},{2,18},{18,2},{3,19},{19,3},{4,20},{20... | collective-permute-start | bytes 98312 | tf_op jit(solution)/shard_map/ppermute | solution.py:30

commit v3 on v2

--- a/solution.py
+++ b/solution.py
@@ -47,7 +47,7 @@
         scratch_shapes=list(scratch),
         cost_estimate=pl.CostEstimate(flops=flops, bytes_accessed=nbytes, transcendentals=0),
         compiler_params=pltpu.CompilerParams(vmem_limit_bytes=vmem * 2**20),
-    )(*ins)
+    )(*[pltpu.with_memory_space_constraint(x, pltpu.HBM) if i in far else x for i, x in enumerate(ins)])
 
 
 def face_of(a, b):
@@ -94,28 +94,40 @@
     return jnp.where(row_iota(x.shape) == 0, edge, pltpu.roll(x, 1, 0))
 
 
-def prepare_body(h_far, my_far, depth_far, wet_far, buf_ref, edge_ref, h_ref, my_ref, depth_ref, wet_ref, sems):
-    copies = [
-        pltpu.make_async_copy(depth_far, depth_ref, sems.at[0]),
-        pltpu.make_async_copy(wet_far, wet_ref, sems.at[1]),
-        pltpu.make_async_copy(h_far, h_ref, sems.at[2]),
-        pltpu.make_async_copy(my_far, my_ref, sems.at[3]),
-    ]
-    for copy in copies:
-        copy.start()
-    n = h_ref.shape[0]
-    copies[0].wait()
-    copies[1].wait()
+def prepare_body(
+    h_far, my_far, depth_far, wet_far, mx_far, buf_ref, edge_ref, h_ref, mx_ref, my_ref, depth_ref, wet_ref, sems
+):
+    n, width = h_ref.shape
+    parts = 4
+    step = n // parts
+    fetched = []
+    for i, (far, near) in enumerate(
+        [(depth_far, depth_ref), (wet_far, wet_ref), (h_far, h_ref), (my_far, my_ref), (mx_far, mx_ref)]
+    ):
+        copies = [
+            pltpu.make_async_copy(far.at[pl.ds(p * step, step)], near.at[pl.ds(p * step, step)], sems.at[i, p])
+            for p in range(parts)
+        ]
+        for copy in copies:
+            copy.start()
+        fetched.append(copies)
+
+    def wait(i):
+        for copy in fetched[i]:
+            copy.wait()
+
+    wait(0)
+    wait(1)
     wd = depth_ref[...] * wet_ref[...].astype(F32)
     buf_ref[n : 2 * n] = wd
     face = face_of(wd, next_row(wd, 0.0))
-    copies[2].wait()
+    wait(2)
     h = h_ref[...]
-    edge = jnp.concatenate([h[0:1], h[n - 1 : n], wd[0:1], wd[n - 1 : n], jnp.zeros((4, h.shape[1]), F32)], 0)
-    buf_ref[2 * n : 2 * n + 8] = edge
-    edge_ref[...] = edge
-    copies[3].wait()
+    buf_ref[2 * n : 2 * n + 8] = jnp.concatenate([h[0:1], h[n - 1 : n], jnp.zeros((6, width), F32)], 0)
+    wait(3)
     buf_ref[0:n] = my_ref[...] + 0.5 * face * (next_row(h, 0.0) - h)
+    wait(4)
+    edge_ref[...] = jnp.concatenate([h[0:1], wd[0:1], wd[n - 1 : n], mx_ref[0:1]], 0)
 
 
 def across(h_ref, mx_ref, buf_ref, table_ref, flow_ref, hx_ref, push_ref, first_ref):
@@ -146,35 +158,46 @@
 
 
 def across_first_body(
-    h_ref, mx_ref, buf_ref, table_ref, tables_far, map_far, along_ref,
-    flow_ref, hx_ref, hx_edge_ref, line_table_ref, base_ref, push_ref, first_ref, map_ref, sems,
+    h_ref, mx_ref, buf_ref, table_ref, tables_far, along_ref, flow_ref, hx_ref, line_table_ref, push_ref, first_ref, sem
 ):
-    n = h_ref.shape[0]
-    fetch_table = pltpu.make_async_copy(tables_far.at[lax.axis_index("rows")], line_table_ref, sems.at[0])
-    fetch_map = pltpu.make_async_copy(map_far.at[0, :, pl.ds(0, 128)], map_ref, sems.at[1])
+    fetch_table = pltpu.make_async_copy(tables_far.at[lax.axis_index("rows")], line_table_ref, sem)
     fetch_table.start()
-    fetch_map.start()
     across(h_ref, mx_ref, buf_ref, table_ref, flow_ref, hx_ref, push_ref, first_ref)
-    hx_edge_ref[0:1] = hx_ref[0:1]
-    hx_edge_ref[1:2] = hx_ref[n - 1 : n]
-    hx_edge_ref[2:8] = jnp.zeros((6, h_ref.shape[1]), F32)
-    fetch_map.wait()
-    base_ref[0] = map_ref[1, 0]
     fetch_table.wait()
 
 
-def across_last_body(
-    h_ref, mx_ref, buf_ref, table_ref, nest_ref, even_ref, flow_far, hx_ref, nest_row_ref, flow_ref, push_ref, first_ref, sem
-):
-    n = h_ref.shape[0]
+def across_below_body(cross_ref, along_ref, table_ref, hx_ref, h_ref, mx_ref, wd_ref, flow_ref, push_ref, first_ref):
+    below = jnp.where(lax.axis_index("sub") == 0, along_ref[...], cross_ref[...])
+    h_ref[...] = jnp.broadcast_to(below[0:1], h_ref.shape)
+    wd_ref[8:16] = jnp.broadcast_to(below[1:2], h_ref.shape)
+    mx_ref[...] = jnp.broadcast_to(below[3:4], h_ref.shape)
+    across(h_ref, mx_ref, wd_ref, table_ref, flow_ref, hx_ref, push_ref, first_ref)
+
+
+def across_last_body(h_ref, mx_ref, buf_ref, table_ref, flow_far, hx_ref, flow_ref, push_ref, first_ref, sem):
     across(h_ref, mx_ref, buf_ref, table_ref, flow_ref, hx_ref, push_ref, first_ref)
     out = pltpu.make_async_copy(flow_ref, flow_far, sem)
     out.start()
-    edge = jnp.where(lax.axis_index("sub") == 0, hx_ref[0:1], hx_ref[n - 1 : n])
-    even = even_ref[...]
-    row = nest_ref[0:1] + edge + nest_ref[1:2] * nest_factor(even)
-    nest_row_ref[...] = jnp.broadcast_to(row, nest_row_ref.shape)
     out.wait()
+
+
+def relay_body(msg_ref, even_ref, both_ref):
+    both_ref[0:8] = msg_ref[...]
+    both_ref[8:16] = even_ref[...]
+
+
+def packet_body(nest_ref, even_ref, map_ref, hx_ref, *refs):
+    packet_ref = refs[-1]
+    n = hx_ref.shape[0]
+    lower = lax.axis_index("sub") == 0
+    is_first = lax.axis_index("rows") == 0
+    top = hx_ref[0:1]
+    bottom = hx_ref[n - 1 : n]
+    for other_ref in refs[:-1]:
+        top, bottom = jnp.where(lower, top, other_ref[0:1]), jnp.where(lower, other_ref[n - 1 : n], bottom)
+    row = jnp.where(is_first, top, bottom) + nest_ref[0:1] + nest_ref[1:2] * nest_factor(even_ref[...])
+    base = jnp.min(map_ref[0, 1:2, 0:128].astype(F32)).astype(jnp.int32)
+    packet_ref[...] = jnp.broadcast_to(upsampled(row, base), packet_ref.shape)
 
 
 def nest_factor(even):
@@ -218,7 +241,7 @@
 
 
 def lines_body(
-    own_ref, other_ref, cross_ref, along_ref, hx_ref, other_hx_ref, table_ref,
+    own_ref, other_ref, cross_ref, along_ref, table_ref,
     flow_ref, face_ref, msg_ref, nest_ref, push_ref, wd_ref,
 ):
     g = table_ref.shape[0]
@@ -241,8 +264,8 @@
     below = jnp.where(lower, along, cross)
     above = jnp.where(lower, cross, along)
     wd = wd_ref[...]
-    face = face_of(wd, next_row(wd, below[2:3]))
-    face_above = face_of(above[3:4], wd[0:1])
+    face = face_of(wd, next_row(wd, below[1:2]))
+    face_above = face_of(above[2:3], wd[0:1])
     south = jnp.where(
         row_iota(wd.shape) == n - 1,
         0.5 * face * (bottom[0:1] - top[1:2]),
@@ -252,12 +275,9 @@
     flow, t_up, u_down = solve_lines(push_ref[...] + south, face, face_above, table)
     flow_ref[...] = flow
     face_ref[...] = face
-    hx_top = jnp.where(lower, hx_ref[0:1], other_hx_ref[0:1])
-    hx_bottom = jnp.where(lower, other_hx_ref[1:2], hx_ref[1:2])
     rows, nest_rows = messages(flow, face, t_up, u_down, table, is_first)
     msg_ref[...] = rows
-    msg_ref[1:2] = rows[1:2] + hx_top
-    nest_ref[0:1] = nest_rows[0:1] + jnp.where(is_first, hx_top, hx_bottom)
+    nest_ref[0:1] = nest_rows[0:1]
     nest_ref[1:2] = nest_rows[1:2]
     nest_ref[2:3] = face_above
     nest_ref[3:8] = jnp.zeros((5, face.shape[1]), F32)
@@ -284,16 +304,21 @@
     return picked[0:1] + picked[1:2] + picked[2:3]
 
 
-def neighbours(even_ref, odd_ref):
-    is_even = lax.rem(lax.axis_index("rows"), 2) == 0
+def neighbours(even_ref, even2_ref, odd2_ref):
+    block = lax.axis_index("rows")
+    is_even = lax.rem(block, 2) == 0
+    is_low = lax.rem(block, 4) < 2
     even = even_ref[...]
-    odd = odd_ref[...]
-    return jnp.where(is_even, odd, even), jnp.where(is_even, even, odd)
+    even2 = even2_ref[...]
+    odd2 = odd2_ref[...]
+    up = jnp.where(is_low, odd2, even2)
+    down = jnp.where(is_low, even2, odd2)
+    return jnp.where(is_even, up[8:16], even), jnp.where(is_even, even, down[8:16]), up[0:8], down[0:8]
 
 
 def between_body(
-    base_ref, flow_ref, face_ref, msg_ref, nest_ref, even_ref, even2_ref, odd2_ref, odd_ref, own_hx_ref, other_hx_ref,
-    nest_there_ref, even_there_ref, table_ref, h_ref, next_flow_ref, next_msg_ref, next_nest_ref, hx_ref,
+    flow_ref, face_ref, msg_ref, nest_ref, even_ref, even2_ref, odd2_ref, own_hx_ref, other_hx_ref,
+    hx_below_ref, packet_ref, table_ref, h_ref, next_flow_ref, next_msg_ref, next_nest_ref, hx_ref,
 ):
     g = table_ref.shape[0]
     n = g // 2
@@ -307,10 +332,7 @@
     hx_ref[pl.ds(mine, n)] = own_hx_ref[...]
     hx_ref[pl.ds(theirs, n)] = other_hx_ref[...]
     own = msg_ref[...]
-    above, below = neighbours(even_ref, odd_ref)
-    low = lax.rem(block, 4) < 2
-    above2 = jnp.where(low, odd2_ref[...], even2_ref[...])
-    below2 = jnp.where(low, even2_ref[...], odd2_ref[...])
+    above, below, above2, below2 = neighbours(even_ref, even2_ref, odd2_ref)
     table = table_ref[...]
     face = face_ref[...]
     t_row = below[0:1]
@@ -318,9 +340,9 @@
     flow = flow_ref[...] + table[:, g - 1 : g] * t_row + table[:, 0:1] * u_row
     flux = face * flow
     flux_above = above[5:6] + above[6:7] * own[0:1] + above[7:8] * above2[4:5]
-    h_below = below[1:2] + below[2:3] * below2[0:1] + below[3:4] * own[4:5] - 0.5 * flux[g - 1 : g]
+    h_below = hx_below_ref[0:1] + below[1:2] + below[2:3] * below2[0:1] + below[3:4] * own[4:5] - 0.5 * flux[g - 1 : g]
     h = hx_ref[...] + 0.5 * (flux - prev_row(flux, flux_above))
-    packet = upsampled(nest_there_ref[0:1] + nest_there_ref[1:2] * nest_factor(even_there_ref[...]), base_ref[0])
+    packet = packet_ref[0:1]
     rows = row_iota(h.shape)
     blend = jnp.logical_and(
         nearfield,
@@ -338,7 +360,7 @@
 
 
 def finish_body(
-    base_ref, flow_ref, face_ref, msg_ref, even_ref, above2_ref, odd_ref, hx_ref, nest_row_ref, table_ref,
+    flow_ref, face_ref, msg_ref, even_ref, above2_ref, odd_ref, hx_ref, packet_ref, table_ref,
     h_far, my_far, h_ref, my_ref, sems,
 ):
     g = table_ref.shape[0]
@@ -350,7 +372,9 @@
     nearfield = lax.axis_index("nest") == 1
     mine = pl.ds(pl.multiple_of(half * n, n), n)
     own = msg_ref[...]
-    above, below = neighbours(even_ref, odd_ref)
+    is_even = lax.rem(block, 2) == 0
+    above = jnp.where(is_even, odd_ref[...], even_ref[...])
+    below = jnp.where(is_even, even_ref[...], odd_ref[...])
     t_row = below[0:1]
     u_row = above[4:5]
     table = table_ref[mine]
@@ -363,7 +387,7 @@
     before = jnp.where(half == 0, flux_above, face_ref[n - 1 : n] * flow_mid)
     flux = face_ref[mine] * flow
     h = hx_ref[...] + 0.5 * (flux - prev_row(flux, before))
-    packet = upsampled(nest_row_ref[0:1], base_ref[0])
+    packet = packet_ref[0:1]
     rows = row_iota(h.shape)
     blend = jnp.logical_and(
         nearfield,
@@ -380,54 +404,56 @@
     n, width = elevation.shape[1:]
     g = inverse_y.shape[-1]
     assert g == 2 * n and lax.axis_size("sub") == 2
-    height = elevation[0]
     table_x = inverse_x[0]
     solve_flops = 2 * g * g * width * 2
     part = pltpu.VMEM((n, width), F32)
+    slab = pltpu.VMEM((8, width), F32)
     dma = pltpu.SemaphoreType.DMA
 
-    buf, edge = call(
-        prepare_body, [(2 * n + 8, width), (8, width)], [height, momentum_y[0], depth[0], wet_mask[0]],
-        [part, part, part, pltpu.VMEM((n, width), jnp.int32), dma((4,))], far=(0, 1, 2, 3), vmem=60,
+    buf, edge, height, flow_x = call(
+        prepare_body, [(g + 8, width), (4, width), (n, width), (n, width)],
+        [elevation[0], momentum_y[0], depth[0], wet_mask[0], momentum_x[0]],
+        [part, part, pltpu.VMEM((n, width), jnp.int32), dma((5, 4))], far=(0, 1, 2, 3, 4),
     )
     other = swap_halves(buf)
     cross = moved(edge, lambda k, s: (k + 1, 0) if s == 1 else (k - 1, 1))
     along = moved(edge, lambda k, s: (k + 1, 1) if s == 1 else (k - 1, 0))
-    flow_x, hx, hx_edge, table_y, base = call(
-        across_first_body, [(n, width), (n, width), (8, width), (g, g), jax.ShapeDtypeStruct((1,), jnp.int32)],
-        [height, momentum_x[0], buf, table_x, inverse_y[0], nest_map, along],
-        [part, part, pltpu.SMEM((2, 128), jnp.int32), dma((2,))], solve_flops, far=(4, 5),
-    )
-    other_edge = swap_halves(hx_edge)
+    flow_x, hx, table_y = call(
+        across_first_body, [(n, width), (n, width), (g, g)],
+        [height, flow_x, buf, table_x, inverse_y[0], along], [part, part, dma], solve_flops, far=(4,),
+    )
+    other_hx = swap_halves(lax.optimization_barrier((hx, cross))[0])
     flow, face, msg, nest = call(
         lines_body, [(g, width), (g, width), (8, width), (8, width)],
-        [buf, other, cross, along, hx_edge, other_edge, table_y], [pltpu.VMEM((g, width), F32)] * 2, solve_flops,
-    )
-    hx, msg = lax.optimization_barrier((hx, msg))
-    other_hx = swap_halves(hx)
+        [buf, other, cross, along, table_y], [pltpu.VMEM((g, width), F32)] * 2, solve_flops,
+    )
+    even = moved(msg, lambda k, s: (k ^ 1, s))
+    (both,) = call(relay_body, [(16, width)], [msg, even])
+    even2 = moved(both, lambda k, s: (k ^ 2, s))
+    odd2 = moved(both, lambda k, s: (((k + 2) ^ 2) - 2, s))
+    (hx_below,) = call(
+        across_below_body, [(8, width)], [cross, along, table_x], [slab, slab, pltpu.VMEM((16, width), F32)] + [slab] * 3
+    )
+    (packet,) = call(packet_body, [(8, width)], [nest, even, nest_map, hx, other_hx])
+    packet = swap_nest(packet)
+    height, flow, msg, nest = call(
+        between_body, [(n, width), (g, width), (8, width), (8, width)],
+        [flow, face, msg, nest, even, even2, odd2, hx, other_hx, hx_below, packet, table_y],
+        [pltpu.VMEM((g, width), F32)], solve_flops,
+    )
+    even = moved(msg, lambda k, s: (k ^ 1, s))
     odd = moved(msg, lambda k, s: (((k + 1) ^ 1) - 1, s))
-    even = moved(msg, lambda k, s: (k ^ 1, s))
-    odd2 = moved(msg, lambda k, s: (((k + 2) ^ 2) - 2, s))
-    even2 = moved(msg, lambda k, s: (k ^ 2, s))
-    nest_there = swap_nest(nest)
-    even_there = swap_nest(even)
-    height, flow, msg, next_nest = call(
-        between_body, [(n, width), (g, width), (8, width), (8, width)],
-        [base, flow, face, msg, nest, even, even2, odd2, odd, hx, other_hx, nest_there, even_there, table_y],
-        [pltpu.VMEM((g, width), F32)], solve_flops,
-    )
-    odd = moved(msg, lambda k, s: (((k + 1) ^ 1) - 1, s))
-    even = moved(msg, lambda k, s: (k ^ 1, s))
-    above2 = moved(msg, lambda k, s: (k + 2, s))
-    flow_x, hx, nest_row = call(
-        across_last_body, [(n, width), (n, width), (8, width)],
-        [height, flow_x, buf, table_x, next_nest, even],
+    above2 = moved(msg, lambda k, s: (k + 2, s) if s == 0 else None)
+    flow_x, hx = call(
+        across_last_body, [(n, width), (n, width)],
+        [height, flow_x, buf, table_x],
         [part, part, part, dma], solve_flops, far_outs=(0,),
     )
-    nest_row = swap_nest(nest_row)
+    (packet,) = call(packet_body, [(8, width)], [nest, even, nest_map, hx])
+    packet = swap_nest(packet)
     height, flow_y = call(
         finish_body, [(n, width), (n, width)],
-        [base, flow, face, msg, even, above2, odd, hx, nest_row, table_y],
+        [flow, face, msg, even, above2, odd, hx, packet, table_y],
         [part, part, dma((2,))], far_outs=(0, 1),
     )
     return height[None], flow_x[None], flow_y[None]

time: 49.2 us -> 45.2 us (0.919)
  starting transfers between devices: 26.7 us -> 23.6 us
  local copies, waits for them, and re-layouts: 2.11 us -> 0.01 us
  waiting for transfers between devices: 9.2 us -> 10.6 us
    unnamed x14 -> x4, local copies, waits for them, and re-layouts: 2.11 us -> 0.01 us
    ppermute x9 -> x8, starting transfers between devices: 19.4 us -> 17.4 us  [moved(): return lax.ppermute(value, LINE, pairs)]
    ppermute x9 -> x8, waiting for transfers between devices: 5.44 us -> 6.19 us  [moved(): return lax.ppermute(value, LINE, pairs)]
    ppermute x3 -> x2, starting transfers between devices: 6.66 us -> 6.07 us  [swap_halves(): return lax.ppermute(value, 'sub', [(0, 1), (1, 0)])]
    ppermute x3 -> x2, waiting for transfers between devices: 2.58 us -> 2.92 us  [swap_halves(): return lax.ppermute(value, 'sub', [(0, 1), (1, 0)])]
    ppermute x3 -> x2, waiting for transfers between devices: 1.18 us -> 1.45 us  [swap_nest(): return lax.ppermute(value, 'nest', [(0, 1), (1, 0)])]
    pallas_call x6 -> x10, Pallas kernels: 10.1 us -> 9.88 us  [call(): pl.pallas_call(body, out_shape=shapes, in_specs=[spec(i, x, far) for i, x...]
  transfers between devices with their start and end apart: 15 -> 12, of which waited for: 4 -> 6; matrix products, arithmetic and copies ran while one was open for 0% -> 0% of each run, Pallas kernels for 7% -> 14%
where the time goes in v3:
time: 45.2 us; the launch traced here: 44.9 us
  starting transfers between devices  23.6 us (52%)
  waiting for transfers between devices  10.6 us (23%)
  Pallas kernels  9.88 us (22%)
  between operations  0.79 us (2%)
    ppermute x8, starting transfers between devices, moved(): return lax.ppermute(value, LINE, pairs)  17.4 us
    pallas_call x10, Pallas kernels, call(): pl.pallas_call(body, out_shape=shapes, in_specs=[spec(i, x, far) for i, x...  9.88 us
    ppermute x8, waiting for transfers between devices, moved(): return lax.ppermute(value, LINE, pairs)  6.19 us
    ppermute x2, starting transfers between devices, swap_halves(): return lax.ppermute(value, 'sub', [(0, 1), (1, 0)])  6.07 us
    ppermute x2, waiting for transfers between devices, swap_halves(): return lax.ppermute(value, 'sub', [(0, 1), (1, 0)])  2.92 us
    ppermute x2, waiting for transfers between devices, swap_nest(): return lax.ppermute(value, 'nest', [(0, 1), (1, 0)])  1.45 us
  transfers between devices with their start and end apart: 12, of which 6 were waited for; matrix products, arithmetic and copies ran while one was open for 0% of the time, Pallas kernels for 14%

profile of v3, /device:TPU:0, one launch (start us, length us, event | category | flops | bytes accessed | tf_op | source)
XLA Modules:
  0.0 44.9 jit_solution(6905102488404552839)
XLA Ops:
  0.6 0.0 copy-start
  0.6 1.6 %shard_map.103 = (f32[136,1024]{1,0:T(8,128)S(1)}, f32[4,1024]{1,0:T(4,128)S(1)}, f32[64,1024]{1,0:T(8,128)S(1)}, f32[64,1024]{1,0:T(8,128)S(1)}) custom-call(f32[64,1024]{1,0:T(8,128)} %bitcast.14, f32[64,1024]{1,0:T(8,128)} %bitcast.15, f32[64,1024]{1,0:T(8,128)} %bitcast.16, s32[64,1024]{1,0:T(8,128)} %bitcast.17, f32[64,1024]{1,0:T(8,128)} %bitcast.18), custom_call_target="tpu_custom_call" | custom-call | bytes 1097728 | tf_op jit(solution)/shard_map/pallas_call | solution.py:42
  2.2 3.0 %collective-permute-start = (f32[136,1024]{1,0:T(8,128)S(1)}, f32[136,1024]{1,0:T(8,128)S(1)}, u32[]{:S(2)}, u32[]{:S(2)}) collective-permute-start(f32[136,1024]{1,0:T(8,128)S(1)} %get-tuple-element.23.buf_ref.own_ref), channel_id=1, source_target_pairs={{0,1},{1,0},{2,3},{3,2},{4,5},{5,4},{6,7},{7,6},{8,9},{9,8},{10,11... | collective-permute-start | bytes 1671176 | tf_op jit(solution)/shard_map/ppermute | solution.py:26
  5.2 1.3 %collective-permute-start.2 = (f32[4,1024]{1,0:T(4,128)S(1)}, f32[4,1024]{1,0:T(4,128)S(1)}, u32[]{:S(2)}, u32[]{:S(2)}) collective-permute-start(f32[4,1024]{1,0:T(4,128)S(1)} %get-tuple-element.24), channel_id=1, source_target_pairs={{1,3},{2,0},{3,5},{4,2},{5,7},{6,4},{7,9},{8,6},{9,11},{10,8},{11,... | collective-permute-start | bytes 49160 | tf_op jit(solution)/shard_map/ppermute | solution.py:22
  6.5 0.7 %collective-permute-start.1 = (f32[4,1024]{1,0:T(4,128)S(1)}, f32[4,1024]{1,0:T(4,128)S(1)}, u32[]{:S(2)}, u32[]{:S(2)}) collective-permute-start(f32[4,1024]{1,0:T(4,128)S(1)} %get-tuple-element.24), channel_id=1, source_target_pairs={{1,2},{2,1},{3,4},{4,3},{5,6},{6,5},{7,8},{8,7},{9,10},{10,9},{11,... | collective-permute-start | bytes 49160 | tf_op jit(solution)/shard_map/ppermute | solution.py:22
  7.2 3.7 %collective-permute-done.2.along_ref = f32[4,1024]{1,0:T(4,128)S(1)} collective-permute-done((f32[4,1024]{1,0:T(4,128)S(1)}, f32[4,1024]{1,0:T(4,128)S(1)}, u32[]{:S(2)}, u32[]{:S(2)}) %collective-permute-start.2) | collective-permute-done | bytes 16416 | tf_op jit(solution)/shard_map/ppermute | solution.py:22
  10.9 0.0 copy-done
  10.9 1.9 %shard_map.104 = (f32[64,1024]{1,0:T(8,128)S(1)}, f32[64,1024]{1,0:T(8,128)S(1)}, f32[128,128]{1,0:T(8,128)S(1)}) custom-call(f32[64,1024]{1,0:T(8,128)S(1)} %get-tuple-element.25.h_ref, f32[64,1024]{1,0:T(8,128)S(1)} %get-tuple-element.26.mx_ref, f32[136,1024]{1,0:T(8,128)S(1)} %get-tuple-element.23.buf_ref.own_ref, f32[8,128,128]{2,1,0:T(8,128)S(1)} %bitcast.10, ...), custom_call_target="tpu_custom_call" | custom-call | flops 67108864 | bytes 2211840 | tf_op jit(solution)/shard_map/pallas_call | solution.py:42
  12.7 0.0 collective-permute-done.1.cross_ref
  12.7 3.0 %collective-permute-start.6 = (f32[64,1024]{1,0:T(8,128)S(1)}, f32[64,1024]{1,0:T(8,128)S(1)}, u32[]{:S(2)}, u32[]{:S(2)}) collective-permute-start(f32[64,1024]{1,0:T(8,128)S(1)} %get-tuple-element.33.hx_ref.own_hx_ref), channel_id=1, source_target_pairs={{0,1},{1,0},{2,3},{3,2},{4,5},{5,4},{6,7},{7,6},{8,9},{9,8},{10,11... | collective-permute-start | bytes 786440 | tf_op jit(solution)/shard_map/ppermute | solution.py:26
  15.8 2.9 %collective-permute-done.other_ref = f32[136,1024]{1,0:T(8,128)S(1)} collective-permute-done((f32[136,1024]{1,0:T(8,128)S(1)}, f32[136,1024]{1,0:T(8,128)S(1)}, u32[]{:S(2)}, u32[]{:S(2)}) %collective-permute-start) | collective-permute-done | bytes 557088 | tf_op jit(solution)/shard_map/ppermute | solution.py:26
  18.7 1.0 %shard_map.105 = (f32[128,1024]{1,0:T(8,128)S(1)}, f32[128,1024]{1,0:T(8,128)S(1)}, f32[8,1024]{1,0:T(8,128)S(1)}, f32[8,1024]{1,0:T(8,128)S(1)}) custom-call(f32[136,1024]{1,0:T(8,128)S(1)} %get-tuple-element.23.buf_ref.own_ref, f32[136,1024]{1,0:T(8,128)S(1)} %collective-permute-done.other_ref, f32[4,1024]{1,0:T(4,128)S(1)} %collective-permute-done.1.cross_ref, ...), custom_call_target="tpu_custom_call" | custom-call | flops 67108864 | bytes 2326528 | tf_op jit(solution)/shard_map/pallas_call | solution.py:42
  19.7 0.0 copy-start.1
  19.7 2.4 %collective-permute-start.3 = (f32[8,1024]{1,0:T(8,128)S(1)}, f32[8,1024]{1,0:T(8,128)S(1)}, u32[]{:S(2)}, u32[]{:S(2)}) collective-permute-start(f32[8,1024]{1,0:T(8,128)S(1)} %get-tuple-element.30.msg_ref), channel_id=1, source_target_pairs={{0,2},{1,3},{2,0},{3,1},{4,6},{5,7},{6,4},{7,5},{8,10},{9,11},{10,... | collective-permute-start | bytes 98312 | tf_op jit(solution)/shard_map/ppermute | solution.py:22
  22.1 1.9 %collective-permute-done.3.even_ref = f32[8,1024]{1,0:T(8,128)S(1)} collective-permute-done((f32[8,1024]{1,0:T(8,128)S(1)}, f32[8,1024]{1,0:T(8,128)S(1)}, u32[]{:S(2)}, u32[]{:S(2)}) %collective-permute-start.3) | collective-permute-done | bytes 32800 | tf_op jit(solution)/shard_map/ppermute | solution.py:22
  24.0 0.7 %collective-permute-start.5 = (f32[16,1024]{1,0:T(8,128)S(1)}, f32[16,1024]{1,0:T(8,128)S(1)}, u32[]{:S(2)}, u32[]{:S(2)}) collective-permute-start(f32[16,1024]{1,0:T(8,128)S(1)} %shard_map.106), channel_id=1, source_target_pairs={{4,8},{5,9},{6,10},{7,11},{8,4},{9,5},{10,6},{11,7},{20,24},{21,25... | collective-permute-start | bytes 196616 | tf_op jit(solution)/shard_map/ppermute | solution.py:22
  24.7 5.0 %collective-permute-start.4 = (f32[16,1024]{1,0:T(8,128)S(1)}, f32[16,1024]{1,0:T(8,128)S(1)}, u32[]{:S(2)}, u32[]{:S(2)}) collective-permute-start(f32[16,1024]{1,0:T(8,128)S(1)} %shard_map.106), channel_id=1, source_target_pairs={{0,4},{1,5},{2,6},{3,7},{4,0},{5,1},{6,2},{7,3},{8,12},{9,13},{10,... | collective-permute-start | bytes 196616 | tf_op jit(solution)/shard_map/ppermute | solution.py:22
  29.7 0.0 collective-permute-done.6.refs_0_.other_hx_ref
  29.7 0.0 copy-done.1
  29.7 0.3 shard_map.108
  30.0 0.1 collective-permute-start.7
  30.1 0.9 %shard_map.107.hx_below_ref = f32[8,1024]{1,0:T(8,128)S(1)} custom-call(f32[4,1024]{1,0:T(4,128)S(1)} %collective-permute-done.1.cross_ref, f32[4,1024]{1,0:T(4,128)S(1)} %collective-permute-done.2.along_ref, f32[8,128,128]{2,1,0:T(8,128)S(1)} %bitcast.11), custom_call_target="tpu_custom_call" | custom-call | bytes 589824 | tf_op jit(solution)/shard_map/pallas_call | solution.py:42
  31.0 0.3 collective-permute-done.7.packet_ref
  31.3 0.0 collective-permute-done.5.odd2_ref
  31.3 0.6 %collective-permute-done.4.even2_ref = f32[16,1024]{1,0:T(8,128)S(1)} collective-permute-done((f32[16,1024]{1,0:T(8,128)S(1)}, f32[16,1024]{1,0:T(8,128)S(1)}, u32[]{:S(2)}, u32[]{:S(2)}) %collective-permute-start.4) | collective-permute-done | bytes 65568 | tf_op jit(solution)/shard_map/ppermute | solution.py:22
  31.9 1.2 %shard_map.109 = (f32[64,1024]{1,0:T(8,128)S(1)}, f32[128,1024]{1,0:T(8,128)S(1)}, f32[8,1024]{1,0:T(8,128)S(1)}, f32[8,1024]{1,0:T(8,128)S(1)}) custom-call(f32[128,1024]{1,0:T(8,128)S(1)} %get-tuple-element.28.flow_ref, f32[128,1024]{1,0:T(8,128)S(1)} %get-tuple-element.29.face_ref, f32[8,1024]{1,0:T(8,128)S(1)} %get-tuple-element.30.msg_ref, ...), custom_call_target="tpu_custom_call" | custom-call | flops 67108864 | bytes 2785280 | tf_op jit(solution)/shard_map/pallas_call | solution.py:42
  33.1 1.6 %collective-permute-start.8 = (f32[8,1024]{1,0:T(8,128)S(1)}, f32[8,1024]{1,0:T(8,128)S(1)}, u32[]{:S(2)}, u32[]{:S(2)}) collective-permute-start(f32[8,1024]{1,0:T(8,128)S(1)} %get-tuple-element.35.msg_ref), channel_id=1, source_target_pairs={{0,2},{1,3},{2,0},{3,1},{4,6},{5,7},{6,4},{7,5},{8,10},{9,11},{10,... | collective-permute-start | bytes 98312 | tf_op jit(solution)/shard_map/ppermute | solution.py:22
  34.7 0.7 %collective-permute-start.10 = (f32[8,1024]{1,0:T(8,128)S(1)}, f32[8,1024]{1,0:T(8,128)S(1)}, u32[]{:S(2)}, u32[]{:S(2)}) collective-permute-start(f32[8,1024]{1,0:T(8,128)S(1)} %get-tuple-element.35.msg_ref), channel_id=1, source_target_pairs={{2,4},{3,5},{4,2},{5,3},{6,8},{7,9},{8,6},{9,7},{10,12},{11,13},{1... | collective-permute-start | bytes 98312 | tf_op jit(solution)/shard_map/ppermute | solution.py:22
  35.3 5.2 %collective-permute-start.9 = (f32[8,1024]{1,0:T(8,128)S(1)}, f32[8,1024]{1,0:T(8,128)S(1)}, u32[]{:S(2)}, u32[]{:S(2)}) collective-permute-start(f32[8,1024]{1,0:T(8,128)S(1)} %get-tuple-element.35.msg_ref), channel_id=1, source_target_pairs={{0,4},{2,6},{4,8},{6,10},{8,12},{10,14},{16,20},{18,22},{20,24},{2... | collective-permute-start | bytes 98312 | tf_op jit(solution)/shard_map/ppermute | solution.py:22
  40.5 1.7 %shard_map.110 = (f32[64,1024]{1,0:T(8,128)}, f32[64,1024]{1,0:T(8,128)S(1)}) custom-call(f32[64,1024]{1,0:T(8,128)S(1)} %get-tuple-element.36.h_ref, f32[64,1024]{1,0:T(8,128)S(1)} %get-tuple-element.37.mx_ref, f32[136,1024]{1,0:T(8,128)S(1)} %get-tuple-element.23.buf_ref.own_ref, f32[8,128,128]{2,1,0:T(8,128)S(1)} %bitcast.12), custom_call_target="tpu_custom_call" | custom-call | flops 67108864 | bytes 2129920 | tf_op jit(solution)/shard_map/pallas_call | solution.py:42
  42.3 0.0 collective-permute-done.8.even_ref
  42.3 0.3 shard_map.111
  42.6 0.1 collective-permute-start.11
  42.7 0.0 collective-permute-done.10.odd_ref
  42.7 0.0 collective-permute-done.9.above2_ref
  42.7 1.2 %collective-permute-done.11.packet_ref = f32[8,1024]{1,0:T(8,128)S(1)} collective-permute-done((f32[8,1024]{1,0:T(8,128)S(1)}, f32[8,1024]{1,0:T(8,128)S(1)}, u32[]{:S(2)}, u32[]{:S(2)}) %collective-permute-start.11) | collective-permute-done | bytes 32800 | tf_op jit(solution)/shard_map/ppermute | solution.py:30
  43.9 1.0 %shard_map.112 = (f32[64,1024]{1,0:T(8,128)}, f32[64,1024]{1,0:T(8,128)}) custom-call(f32[128,1024]{1,0:T(8,128)S(1)} %get-tuple-element.34.flow_ref, f32[128,1024]{1,0:T(8,128)S(1)} %get-tuple-element.29.face_ref, f32[8,1024]{1,0:T(8,128)S(1)} %get-tuple-element.35.msg_ref, f32[8,1024]{1,0:T(8,128)S(1)} %collective-permute-done.8.even_ref, ...), custom_call_target="tpu_custom_call" | custom-call | bytes 2064384 | tf_op jit(solution)/shard_map/pallas_call | solution.py:42
  (1 shorter events, 0.0 us)
Async XLA Ops:
  0.6 10.2 %copy-start = (f32[1,8,128,128]{3,2,1,0:T(8,128)S(1)}, f32[1,8,128,128]{3,2,1,0:T(8,128)}, u32[]{:S(2)}) copy-start(f32[1,8,128,128]{3,2,1,0:T(8,128)} %param.13) | copy-start | bytes 1572868
  2.2 16.5 %collective-permute-start = (f32[136,1024]{1,0:T(8,128)S(1)}, f32[136,1024]{1,0:T(8,128)S(1)}, u32[]{:S(2)}, u32[]{:S(2)}) collective-permute-start(f32[136,1024]{1,0:T(8,128)S(1)} %get-tuple-element.23.buf_ref.own_ref), channel_id=1, source_target_pairs={{0,1},{1,0},{2,3},{3,2},{4,5},{5,4},{6,7},{7,6},{8,9},{9,8},{10,11... | collective-permute-start | bytes 1671176 | tf_op jit(solution)/shard_map/ppermute | solution.py:26
  5.2 5.6 %collective-permute-start.2 = (f32[4,1024]{1,0:T(4,128)S(1)}, f32[4,1024]{1,0:T(4,128)S(1)}, u32[]{:S(2)}, u32[]{:S(2)}) collective-permute-start(f32[4,1024]{1,0:T(4,128)S(1)} %get-tuple-element.24), channel_id=1, source_target_pairs={{1,3},{2,0},{3,5},{4,2},{5,7},{6,4},{7,9},{8,6},{9,11},{10,8},{11,... | collective-permute-start | bytes 49160 | tf_op jit(solution)/shard_map/ppermute | solution.py:22
  6.5 6.2 %collective-permute-start.1 = (f32[4,1024]{1,0:T(4,128)S(1)}, f32[4,1024]{1,0:T(4,128)S(1)}, u32[]{:S(2)}, u32[]{:S(2)}) collective-permute-start(f32[4,1024]{1,0:T(4,128)S(1)} %get-tuple-element.24), channel_id=1, source_target_pairs={{1,2},{2,1},{3,4},{4,3},{5,6},{6,5},{7,8},{8,7},{9,10},{10,9},{11,... | collective-permute-start | bytes 49160 | tf_op jit(solution)/shard_map/ppermute | solution.py:22
  12.7 16.9 %collective-permute-start.6 = (f32[64,1024]{1,0:T(8,128)S(1)}, f32[64,1024]{1,0:T(8,128)S(1)}, u32[]{:S(2)}, u32[]{:S(2)}) collective-permute-start(f32[64,1024]{1,0:T(8,128)S(1)} %get-tuple-element.33.hx_ref.own_hx_ref), channel_id=1, source_target_pairs={{0,1},{1,0},{2,3},{3,2},{4,5},{5,4},{6,7},{7,6},{8,9},{9,8},{10,11... | collective-permute-start | bytes 786440 | tf_op jit(solution)/shard_map/ppermute | solution.py:26
  19.7 10.0 %copy-start.1 = (s32[2,2,1024]{2,1,0:T(2,128)S(1)}, s32[2,2,1024]{2,1,0:T(2,128)}, u32[]{:S(2)}) copy-start(s32[2,2,1024]{2,1,0:T(2,128)} %map_ref.3) | copy-start | bytes 49156
  19.7 4.3 %collective-permute-start.3 = (f32[8,1024]{1,0:T(8,128)S(1)}, f32[8,1024]{1,0:T(8,128)S(1)}, u32[]{:S(2)}, u32[]{:S(2)}) collective-permute-start(f32[8,1024]{1,0:T(8,128)S(1)} %get-tuple-element.30.msg_ref), channel_id=1, source_target_pairs={{0,2},{1,3},{2,0},{3,1},{4,6},{5,7},{6,4},{7,5},{8,10},{9,11},{10,... | collective-permute-start | bytes 98312 | tf_op jit(solution)/shard_map/ppermute | solution.py:22
  24.0 7.3 %collective-permute-start.5 = (f32[16,1024]{1,0:T(8,128)S(1)}, f32[16,1024]{1,0:T(8,128)S(1)}, u32[]{:S(2)}, u32[]{:S(2)}) collective-permute-start(f32[16,1024]{1,0:T(8,128)S(1)} %shard_map.106), channel_id=1, source_target_pairs={{4,8},{5,9},{6,10},{7,11},{8,4},{9,5},{10,6},{11,7},{20,24},{21,25... | collective-permute-start | bytes 196616 | tf_op jit(solution)/shard_map/ppermute | solution.py:22
  24.7 7.2 %collective-permute-start.4 = (f32[16,1024]{1,0:T(8,128)S(1)}, f32[16,1024]{1,0:T(8,128)S(1)}, u32[]{:S(2)}, u32[]{:S(2)}) collective-permute-start(f32[16,1024]{1,0:T(8,128)S(1)} %shard_map.106), channel_id=1, source_target_pairs={{0,4},{1,5},{2,6},{3,7},{4,0},{5,1},{6,2},{7,3},{8,12},{9,13},{10,... | collective-permute-start | bytes 196616 | tf_op jit(solution)/shard_map/ppermute | solution.py:22
  30.0 1.3 %collective-permute-start.7 = (f32[8,1024]{1,0:T(8,128)S(1)}, f32[8,1024]{1,0:T(8,128)S(1)}, u32[]{:S(2)}, u32[]{:S(2)}) collective-permute-start(f32[8,1024]{1,0:T(8,128)S(1)} %shard_map.108), channel_id=1, source_target_pairs={{0,16},{16,0},{1,17},{17,1},{2,18},{18,2},{3,19},{19,3},{4,20},{20... | collective-permute-start | bytes 98312 | tf_op jit(solution)/shard_map/ppermute | solution.py:30
  33.1 9.1 %collective-permute-start.8 = (f32[8,1024]{1,0:T(8,128)S(1)}, f32[8,1024]{1,0:T(8,128)S(1)}, u32[]{:S(2)}, u32[]{:S(2)}) collective-permute-start(f32[8,1024]{1,0:T(8,128)S(1)} %get-tuple-element.35.msg_ref), channel_id=1, source_target_pairs={{0,2},{1,3},{2,0},{3,1},{4,6},{5,7},{6,4},{7,5},{8,10},{9,11},{10,... | collective-permute-start | bytes 98312 | tf_op jit(solution)/shard_map/ppermute | solution.py:22
  34.7 8.0 %collective-permute-start.10 = (f32[8,1024]{1,0:T(8,128)S(1)}, f32[8,1024]{1,0:T(8,128)S(1)}, u32[]{:S(2)}, u32[]{:S(2)}) collective-permute-start(f32[8,1024]{1,0:T(8,128)S(1)} %get-tuple-element.35.msg_ref), channel_id=1, source_target_pairs={{2,4},{3,5},{4,2},{5,3},{6,8},{7,9},{8,6},{9,7},{10,12},{11,13},{1... | collective-permute-start | bytes 98312 | tf_op jit(solution)/shard_map/ppermute | solution.py:22
  35.3 7.4 %collective-permute-start.9 = (f32[8,1024]{1,0:T(8,128)S(1)}, f32[8,1024]{1,0:T(8,128)S(1)}, u32[]{:S(2)}, u32[]{:S(2)}) collective-permute-start(f32[8,1024]{1,0:T(8,128)S(1)} %get-tuple-element.35.msg_ref), channel_id=1, source_target_pairs={{0,4},{2,6},{4,8},{6,10},{8,12},{10,14},{16,20},{18,22},{20,24},{2... | collective-permute-start | bytes 98312 | tf_op jit(solution)/shard_map/ppermute | solution.py:22
  42.6 1.3 %collective-permute-start.11 = (f32[8,1024]{1,0:T(8,128)S(1)}, f32[8,1024]{1,0:T(8,128)S(1)}, u32[]{:S(2)}, u32[]{:S(2)}) collective-permute-start(f32[8,1024]{1,0:T(8,128)S(1)} %shard_map.111), channel_id=1, source_target_pairs={{0,16},{16,0},{1,17},{17,1},{2,18},{18,2},{3,19},{19,3},{4,20},{20... | collective-permute-start | bytes 98312 | tf_op jit(solution)/shard_map/ppermute | solution.py:30

commit v4 on v3

v4 whole, which is shorter than its diff:
```python
import jax
import jax.numpy as jnp
from jax import lax
from jax.experimental import pallas as pl
from jax.experimental.pallas import tpu as pltpu
from jax.sharding import PartitionSpec as P

LINE = ("rows", "sub")
VM = pl.BlockSpec(memory_space=pltpu.VMEM)
SM = pl.BlockSpec(memory_space=pltpu.SMEM)
FAR = pl.BlockSpec(memory_space=pltpu.HBM)
F32 = jnp.float32


def moved(value, target):
    blocks = lax.axis_size("rows")
    pairs = []
    for source in range(2 * blocks):
        there = target(source // 2, source % 2)
        if there is not None and 0 <= there[0] < blocks:
            pairs.append((source, 2 * there[0] + there[1]))
    return lax.ppermute(value, LINE, pairs)


def swap_halves(value):
    return lax.ppermute(value, "sub", [(0, 1), (1, 0)])


def swap_nest(value):
    return lax.ppermute(value, "nest", [(0, 1), (1, 0)])


def call(body, outs, ins, scratch=(), flops=0, far=(), far_outs=(), vmem=8, aliases=None):
    shapes = [o if isinstance(o, jax.ShapeDtypeStruct) else jax.ShapeDtypeStruct(o, F32) for o in outs]
    nbytes = sum(4 * x.size for i, x in enumerate(ins) if i not in far) + sum(4 * x.size for x in shapes)

    def spec(i, x, others):
        if i in others:
            return FAR
        return SM if x.dtype == jnp.int32 and x.size < 16 else VM

    return pl.pallas_call(
        body,
        out_shape=shapes,
        in_specs=[spec(i, x, far) for i, x in enumerate(ins)],
        out_specs=[spec(i, x, far_outs) for i, x in enumerate(shapes)],
        scratch_shapes=list(scratch),
        input_output_aliases=aliases or {},
        cost_estimate=pl.CostEstimate(flops=flops, bytes_accessed=nbytes, transcendentals=0),
        compiler_params=pltpu.CompilerParams(vmem_limit_bytes=vmem * 2**20),
    )(*[pltpu.with_memory_space_constraint(x, pltpu.HBM) if i in far else x for i, x in enumerate(ins)])


def face_of(a, b):
    return jnp.where(jnp.logical_and(a > 0.0, b > 0.0), 0.5 * (a + b), 0.0)


def split(a):
    high = a.astype(jnp.bfloat16)
    low = (a - high.astype(F32)).astype(jnp.bfloat16)
    return high, low


def matmul(a, b):
    a_high, a_low = split(a)
    b_high, b_low = split(b)
    return jnp.dot(
        jnp.concatenate([a_high, a_high, a_low], 1),
        jnp.concatenate([b_high, b_low, b_high], 0),
        preferred_element_type=F32,
    )


def matmul_t(a, b):
    a_high, a_low = split(a)
    b_high, b_low = split(b)
    return lax.dot_general(
        jnp.concatenate([a_high, a_high, a_low], 1),
        jnp.concatenate([b_high, b_low, b_high], 1),
        (((1,), (1,)), ((), ())),
        preferred_element_type=F32,
    )


def row_iota(shape):
    return lax.broadcasted_iota(jnp.int32, shape, 0)


def next_row(x, edge):
    n = x.shape[0]
    return jnp.where(row_iota(x.shape) == n - 1, edge, pltpu.roll(x, n - 1, 0))


def prev_row(x, edge):
    return jnp.where(row_iota(x.shape) == 0, edge, pltpu.roll(x, 1, 0))


def copies_of(source, target, sems, parts=4):
    step = source.shape[0] // parts
    return [
        pltpu.make_async_copy(source.at[pl.ds(p * step, step)], target.at[pl.ds(p * step, step)], sems.at[p])
        for p in range(parts)
    ]


def depth_body(depth_far, wet_far, wd_ref, depth_ref, wet_ref, sems):
    copies = copies_of(depth_far, depth_ref, sems.at[0]) + copies_of(wet_far, wet_ref, sems.at[1])
    for copy in copies:
        copy.start()
    for copy in copies:
        copy.wait()
    wd_ref[...] = depth_ref[...] * wet_ref[...].astype(F32)


def prepare_body(h_far, my_far, mx_far, wd_ref, buf_ref, edge_ref, h_ref, mx_ref, my_ref, sems):
    n, width = h_ref.shape
    fetched = []
    for i, (far, near) in enumerate([(h_far, h_ref), (my_far, my_ref), (mx_far, mx_ref)]):
        fetched += copies_of(far, near, sems.at[i])
    for copy in fetched:
        copy.start()
    for copy in fetched:
        copy.wait()
    wd = wd_ref[...]
    h = h_ref[...]
    buf_ref[0:n] = my_ref[...] + 0.5 * face_of(wd, next_row(wd, 0.0)) * (next_row(h, 0.0) - h)
    buf_ref[n : n + 8] = jnp.concatenate([h[0:1], h[n - 1 : n], jnp.zeros((6, width), F32)], 0)
    edge_ref[...] = jnp.concatenate([h[0:1], wd[0:1], wd[n - 1 : n], mx_ref[0:1]], 0)


def across(h_ref, mx_ref, wd_ref, table_ref, flow_ref, hx_ref, push_ref, first_ref):
    n, width = h_ref.shape
    group = table_ref.shape[-1]
    h = h_ref[...]
    wd = wd_ref[...]
    lane = lax.broadcasted_iota(jnp.int32, wd.shape, 1)
    face = face_of(wd, jnp.where(lane == width - 1, 0.0, pltpu.roll(wd, width - 1, 1)))
    coef = 0.5 * face * face
    push = mx_ref[...] + 0.5 * face * (pltpu.roll(h, width - 1, 1) - h)
    push_ref[...] = push
    for b in range(width // group):
        cols = slice(b * group, (b + 1) * group)
        first_ref[:, cols] = matmul_t(push_ref[:, cols], table_ref[b])
    first = first_ref[...]
    operated = (
        first
        + coef * (first - pltpu.roll(first, width - 1, 1))
        + pltpu.roll(coef, 1, 1) * (first - pltpu.roll(first, 1, 1))
    )
    push_ref[...] = push - operated
    for b in range(width // group):
        cols = slice(b * group, (b + 1) * group)
        flow_ref[:, cols] = first_ref[:, cols] + matmul_t(push_ref[:, cols], table_ref[b])
    flux = face * flow_ref[...]
    hx_ref[...] = h + 0.5 * (flux - pltpu.roll(flux, 1, 1))


def across_first_body(
    h_ref, mx_ref, wd_ref, table_ref, tables_far, along_ref, flow_ref, hx_ref, line_table_ref, push_ref, first_ref, sem
):
    fetch_table = pltpu.make_async_copy(tables_far.at[lax.axis_index("rows")], line_table_ref, sem)
    fetch_table.start()
    across(h_ref, mx_ref, wd_ref, table_ref, flow_ref, hx_ref, push_ref, first_ref)
    fetch_table.wait()


def across_below_body(cross_ref, along_ref, table_ref, hx_ref, h_ref, mx_ref, wd_ref, flow_ref, push_ref, first_ref):
    below = jnp.where(lax.axis_index("sub") == 0, along_ref[...], cross_ref[...])
    h_ref[...] = jnp.broadcast_to(below[0:1], h_ref.shape)
    wd_ref[...] = jnp.broadcast_to(below[1:2], h_ref.shape)
    mx_ref[...] = jnp.broadcast_to(below[3:4], h_ref.shape)
    across(h_ref, mx_ref, wd_ref, table_ref, flow_ref, hx_ref, push_ref, first_ref)


def relay_body(msg_ref, even_ref, out_ref):
    is_even = lax.rem(lax.axis_index("rows"), 2) == 0
    even = even_ref[...]
    msg = msg_ref[...]
    passed = jnp.where(is_even, even[4:8], even[0:4])
    out_ref[...] = jnp.concatenate([msg[0:1], msg[4:5], passed, jnp.zeros((2, msg.shape[1]), F32)], 0)


def packet_body(nest_ref, even_ref, map_ref, hx_ref, other_ref, packet_ref):
    n = hx_ref.shape[0]
    lower = lax.axis_index("sub") == 0
    is_first = lax.axis_index("rows") == 0
    top = hx_ref[0:1]
    bottom = hx_ref[n - 1 : n]
    if other_ref.shape == hx_ref.shape:
        top, bottom = jnp.where(lower, top, other_ref[0:1]), jnp.where(lower, other_ref[n - 1 : n], bottom)
    row = jnp.where(is_first, top, bottom) + nest_ref[0:1] + nest_ref[1:2] * nest_factor(even_ref)
    base = jnp.min(map_ref[0, 1:2, 0:128].astype(F32)).astype(jnp.int32)
    packet_ref[...] = upsampled(row, base)


def nest_factor(even_ref):
    down = even_ref.shape[0] // 2
    if down == 2:
        down = 1
    return jnp.where(lax.axis_index("rows") == 0, even_ref[0:1], even_ref[down : down + 1])


def solve_lines(push, face, face_above, table):
    coef = 0.5 * face * face
    coef_above = 0.5 * face_above * face_above
    first = matmul(table, push)
    operated = (
        first
        + coef * (first - next_row(first, 0.0))
        + prev_row(coef, coef_above) * (first - prev_row(first, 0.0))
    )
    flow = first + matmul(table, push - operated)
    g = push.shape[0]
    t_up = coef_above * first[0:1]
    u_down = coef[g - 1 : g] * first[g - 1 : g]
    return flow, t_up, u_down


def messages(flow, face, t_up, u_down, table, is_first):
    g = flow.shape[0]
    half_top = 0.5 * face[0:1]
    bottom = face[g - 1 : g]
    side = 0.5 * face[g - 2 : g - 1]
    rows = [
        t_up,
        half_top * flow[0:1],
        half_top * table[0:1, g - 1 : g],
        half_top * table[0:1, 0:1],
        u_down,
        bottom * flow[g - 1 : g],
        bottom * table[g - 1 : g, g - 1 : g],
        bottom * table[g - 1 : g, 0:1],
    ]
    nest_base = jnp.where(is_first, rows[1], -(side * flow[g - 2 : g - 1]))
    nest_coef = jnp.where(is_first, rows[2], -(side * table[g - 2 : g - 1, 0:1]))
    return jnp.concatenate(rows, 0), jnp.concatenate([nest_base, nest_coef], 0)


def faces_body(own_wd_ref, other_wd_ref, face_ref, wd_ref):
    n = own_wd_ref.shape[0]
    half = lax.axis_index("sub")
    wd_ref[pl.ds(pl.multiple_of(half * n, n), n)] = own_wd_ref[...]
    wd_ref[pl.ds(pl.multiple_of((1 - half) * n, n), n)] = other_wd_ref[...]
    wd = wd_ref[...]
    face_ref[...] = face_of(wd, next_row(wd, 0.0))


def lines_body(
    own_ref, own_wd_ref, other_ref, other_wd_ref, cross_ref, along_ref, table_ref, inner_ref,
    flow_ref, face_ref, msg_ref, nest_ref, push_ref,
):
    g = table_ref.shape[0]
    n = g // 2
    half = lax.axis_index("sub")
    lower = half == 0
    is_first = lax.axis_index("rows") == 0
    mine = pl.multiple_of(half * n, n)
    theirs = pl.multiple_of((1 - half) * n, n)
    push_ref[pl.ds(mine, n)] = own_ref[0:n]
    push_ref[pl.ds(theirs, n)] = other_ref[0:n]
    own = own_ref[n : n + 8]
    other = other_ref[n : n + 8]
    cross = cross_ref[...]
    along = along_ref[...]
    top = jnp.where(lower, own, other)
    bottom = jnp.where(lower, other, own)
    below = jnp.where(lower, along, cross)
    above = jnp.where(lower, cross, along)
    face = inner_ref[...]
    wd_last = jnp.where(lower, other_wd_ref[n - 1 : n], own_wd_ref[n - 1 : n])
    face = jnp.where(row_iota(face.shape) == g - 1, face_of(wd_last, below[1:2]), face)
    face_above = face_of(above[2:3], jnp.where(lower, own_wd_ref[0:1], other_wd_ref[0:1]))
    south = jnp.where(
        row_iota(face.shape) == n - 1,
        0.5 * face * (bottom[0:1] - top[1:2]),
        jnp.where(row_iota(face.shape) == g - 1, 0.5 * face * (below[0:1] - bottom[1:2]), 0.0),
    )
    table = table_ref[...]
    flow, t_up, u_down = solve_lines(push_ref[...] + south, face, face_above, table)
    flow_ref[...] = flow
    face_ref[...] = face
    rows, nest_rows = messages(flow, face, t_up, u_down, table, is_first)
    msg_ref[...] = rows
    nest_ref[0:1] = nest_rows[0:1]
    nest_ref[1:2] = nest_rows[1:2]
    nest_ref[2:3] = face_above
    nest_ref[3:8] = jnp.zeros((5, face.shape[1]), F32)


def upsampled(row, base):
    width = row.shape[1]
    rolled = pltpu.roll(jnp.broadcast_to(row, (8, width)), lax.rem(width - base, width), 1)
    high = rolled.astype(jnp.bfloat16)
    middle, low = split(rolled - high.astype(F32))
    part = lax.broadcasted_iota(jnp.int32, rolled.shape, 0)
    parts = jnp.where(
        part == 0,
        high.astype(F32),
        jnp.where(part == 1, middle.astype(F32), jnp.where(part == 2, low.astype(F32), 0.0)),
    ).astype(jnp.bfloat16)
    source = lax.broadcasted_iota(jnp.int32, (128, 256), 0)
    target = lax.broadcasted_iota(jnp.int32, (128, 256), 1)
    pick = jnp.where(target // 2 == source, 1.0, 0.0).astype(jnp.bfloat16)
    pieces = [
        jnp.dot(parts[:, 128 * m : 128 * (m + 1)], pick, preferred_element_type=F32) for m in range(width // 256)
    ]
    picked = jnp.concatenate(pieces, 1)
    return picked[0:1] + picked[1:2] + picked[2:3]


def neighbours(even_ref, even2_ref, odd2_ref):
    block = lax.axis_index("rows")
    is_even = lax.rem(block, 2) == 0
    is_low = lax.rem(block, 4) < 2
    even = even_ref[...]
    even2 = even2_ref[...]
    odd2 = odd2_ref[...]
    up = jnp.where(is_low, odd2, even2)
    down = jnp.where(is_low, even2, odd2)
    return jnp.where(is_even, up[2:6], even[4:8]), jnp.where(is_even, even[0:4], down[2:6]), up[1:2], down[0:1]


def between_body(
    flow_ref, face_ref, msg_ref, nest_ref, even_ref, odd2_ref, even2_ref, own_hx_ref, other_hx_ref,
    hx_below_ref, packet_ref, table_ref, h_ref, next_flow_ref, next_msg_ref, next_nest_ref, gain_ref, u_down_ref, hx_ref,
):
    g = table_ref.shape[0]
    n = g // 2
    half = lax.axis_index("sub")
    block = lax.axis_index("rows")
    is_first = block == 0
    is_last = block == lax.axis_size("rows") - 1
    nearfield = lax.axis_index("nest") == 1
    mine = pl.multiple_of(half * n, n)
    theirs = pl.multiple_of((1 - half) * n, n)
    hx_ref[pl.ds(mine, n)] = own_hx_ref[...]
    hx_ref[pl.ds(theirs, n)] = other_hx_ref[...]
    own = msg_ref[...]
    above, below, u_above2, t_below2 = neighbours(even_ref, even2_ref, odd2_ref)
    table = table_ref[...]
    face = face_ref[...]
    t_row = below[0:1]
    u_row = above[0:1]
    flow = flow_ref[...] + table[:, g - 1 : g] * t_row + table[:, 0:1] * u_row
    flux = face * flow
    flux_above = above[1:2] + above[2:3] * own[0:1] + above[3:4] * u_above2
    h_below = hx_below_ref[0:1] + below[1:2] + below[2:3] * t_below2 + below[3:4] * own[4:5] - 0.5 * flux[g - 1 : g]
    h = hx_ref[...] + 0.5 * (flux - prev_row(flux, flux_above))
    packet = packet_ref[0:1]
    rows = row_iota(h.shape)
    blend = jnp.logical_and(
        nearfield,
        jnp.logical_or(jnp.logical_and(is_first, rows == 0), jnp.logical_and(is_last, rows == g - 1)),
    )
    h = jnp.where(blend, 0.5 * h + 0.5 * packet, h)
    hx_ref[...] = h
    h_ref[...] = hx_ref[pl.ds(mine, n)]
    push = flow + 0.5 * face * (next_row(h, h_below) - h)
    next_flow, t_up, u_down = solve_lines(push, face, nest_ref[2:3], table)
    next_flow_ref[...] = next_flow
    rows, nest_rows = messages(next_flow, face, t_up, u_down, table, is_first)
    next_msg_ref[...] = jnp.concatenate([t_up, u_down, rows[5:6], jnp.zeros_like(t_up)], 0)
    u_down_ref[...] = u_down
    gain_ref[0:2] = above[2:4]
    gain_ref[2:8] = jnp.zeros((6, t_up.shape[1]), F32)
    next_nest_ref[0:2] = nest_rows
    next_nest_ref[2:8] = jnp.zeros((6, face.shape[1]), F32)


def finish_body(
    flow_ref, even_ref, odd_ref, table_ref, face_ref, hx_ref, flow_x_ref,
    my_far, flow_x_far, h_far, edge_ref, before_ref, my_ref, h_ref, sems,
):
    copies = copies_of(flow_x_ref, flow_x_far, sems.at[0])
    for copy in copies:
        copy.start()
    g, width = flow_ref.shape
    n = g // 2
    half = lax.axis_index("sub")
    mine = pl.ds(pl.multiple_of(half * n, n), n)
    is_even = lax.rem(lax.axis_index("rows"), 2) == 0
    above = jnp.where(is_even, odd_ref[...], even_ref[...])
    below = jnp.where(is_even, even_ref[...], odd_ref[...])
    t_row = below[0:1]
    u_row = above[1:2]
    table = table_ref[mine]
    flow = flow_ref[mine] + table[:, g - 1 : g] * t_row + table[:, 0:1] * u_row
    my_ref[...] = flow
    for copy in copies_of(my_ref, my_far, sems.at[1]):
        copy.start()
        copies.append(copy)
    flux = face_ref[mine] * flow
    h_ref[...] = hx_ref[...] + 0.5 * (flux - prev_row(flux, 0.0))
    inner = pl.ds(8, n - 16)
    copies.append(pltpu.make_async_copy(h_ref.at[inner], h_far.at[inner], sems.at[2, 0]))
    copies[-1].start()
    edge_ref[0:8] = h_ref[0:8]
    edge_ref[8:16] = h_ref[n - 8 : n]
    flow_mid = flow_ref[n - 1 : n] + table_ref[n - 1 : n, g - 1 : g] * t_row + table_ref[n - 1 : n, 0:1] * u_row
    before_ref[0:1] = face_ref[n - 1 : n] * flow_mid
    before_ref[1:2] = above[2:3]
    before_ref[2:8] = jnp.zeros((6, width), F32)
    for copy in copies:
        copy.wait()


def finish_edge_body(h_in, edge_ref, before_ref, msg_ref, gain_ref, above2_ref, packet_ref, h_far, rows_ref, sems):
    n = h_far.shape[0]
    half = lax.axis_index("sub")
    block = lax.axis_index("rows")
    nearfield = lax.axis_index("nest") == 1
    is_first = jnp.logical_and(nearfield, jnp.logical_and(block == 0, half == 0))
    is_last = jnp.logical_and(nearfield, jnp.logical_and(block == lax.axis_size("rows") - 1, half == 1))
    flux_above = before_ref[1:2] + gain_ref[0:1] * msg_ref[0:1] + gain_ref[1:2] * above2_ref[...]
    before = jnp.where(half == 0, flux_above, before_ref[0:1])
    packet = packet_ref[...]
    edge = edge_ref[...]
    rows = row_iota(edge.shape)
    edge = jnp.where(rows == 0, edge - 0.5 * before, edge)
    blend = jnp.logical_or(jnp.logical_and(is_first, rows == 0), jnp.logical_and(is_last, rows == 15))
    rows_ref[...] = jnp.where(blend, 0.5 * edge + 0.5 * packet, edge)
    copies = [
        pltpu.make_async_copy(rows_ref.at[pl.ds(0, 8)], h_far.at[pl.ds(0, 8)], sems.at[0]),
        pltpu.make_async_copy(rows_ref.at[pl.ds(8, 8)], h_far.at[pl.ds(n - 8, 8)], sems.at[1]),
    ]
    for copy in copies:
        copy.start()
    for copy in copies:
        copy.wait()


def on_device(elevation, momentum_x, momentum_y, depth, wet_mask, inverse_x, inverse_y, nest_map):
    n, width = elevation.shape[1:]
    g = inverse_y.shape[-1]
    assert g == 2 * n and lax.axis_size("sub") == 2
    table_x = inverse_x[0]
    solve_flops = 2 * g * g * width * 2
    part = pltpu.VMEM((n, width), F32)
    slab = pltpu.VMEM((8, width), F32)
    dma = pltpu.SemaphoreType.DMA

    (wd,) = call(
        depth_body, [(n, width)], [depth[0], wet_mask[0]],
        [part, pltpu.VMEM((n, width), jnp.int32), dma((2, 4))], far=(0, 1),
    )
    other_wd = swap_halves(wd)
    buf, edge, height, flow_x = call(
        prepare_body, [(n + 8, width), (4, width), (n, width), (n, width)],
        [elevation[0], momentum_y[0], momentum_x[0], wd],
        [part, dma((3, 4))], far=(0, 1, 2), flops=int(0),
    )
    other = swap_halves(buf)
    cross = moved(edge, lambda k, s: (k + 1, 0) if s == 1 else (k - 1, 1))
    along = moved(edge, lambda k, s: (k + 1, 1) if s == 1 else (k - 1, 0))
    flow_x, hx, table_y = call(
        across_first_body, [(n, width), (n, width), (g, g)],
        [height, flow_x, wd, table_x, inverse_y[0], along], [part, part, dma], solve_flops, far=(4,),
    )
    (inner,) = call(faces_body, [(g, width)], [wd, other_wd], [pltpu.VMEM((g, width), F32)], flops=int(1e9))
    flow, face, msg, nest = call(
        lines_body, [(g, width), (g, width), (8, width), (8, width)],
        [buf, wd, other, other_wd, cross, along, table_y, inner], [pltpu.VMEM((g, width), F32)], solve_flops,
    )
    other_hx = swap_halves(lax.optimization_barrier((hx, msg))[0])
    even = moved(msg, lambda k, s: (k ^ 1, s))
    (both,) = call(relay_body, [(8, width)], [msg, even], flops=int(3e9))
    even2 = moved(both, lambda k, s: (k ^ 2, s))
    odd2 = moved(both, lambda k, s: (((k + 2) ^ 2) - 2, s))
    (hx_below,) = call(
        across_below_body, [(8, width)], [cross, along, table_x], [slab] * 6
    )
    (packet,) = call(packet_body, [(1, width)], [nest, even, nest_map, hx, other_hx])
    packet = swap_nest(packet)
    height, flow, msg, nest, gain, u_down = call(
        between_body, [(n, width), (g, width), (4, width), (8, width), (8, width), (1, width)],
        [flow, face, msg, nest, even, odd2, even2, hx, other_hx, hx_below, packet, table_y],
        [pltpu.VMEM((g, width), F32)], solve_flops,
    )
    even = moved(msg, lambda k, s: (k ^ 1, s))
    odd = moved(msg, lambda k, s: (((k + 1) ^ 1) - 1, s))
    above2 = moved(u_down, lambda k, s: (k + 2, s) if s == 0 else None)
    flow_x, hx = call(across, [(n, width), (n, width)], [height, flow_x, wd, table_x], [part, part], solve_flops)
    (packet,) = call(packet_body, [(1, width)], [nest, even, nest_map, hx, odd])
    packet = swap_nest(packet)
    flow_y, flow_x, height, edge, before = call(
        finish_body, [(n, width), (n, width), (n, width), (16, width), (8, width)],
        [flow, even, odd, table_y, face, hx, flow_x], [part, part, dma((3, 4))], far_outs=(0, 1, 2),
    )
    (height,) = call(
        finish_edge_body, [(n, width)], [height, edge, before, msg, gain, above2, packet],
        [pltpu.VMEM((16, width), F32), dma((2,))], far=(0,), far_outs=(0,), aliases={0: 0},
    )
    return height[None], flow_x[None], flow_y[None]


def solution(mesh):
    fields = P("nest", LINE, None)
    tables = P("nest", None, None, None)
    return jax.shard_map(
        on_device,
        mesh=mesh,
        in_specs=(fields,) * 5 + (tables, tables, P()),
        out_specs=(fields,) * 3,
        check_vma=False,
    )
```

time: 45.2 us -> 42.6 us (0.942)
  waiting for transfers between devices: 10.6 us -> 7.98 us
  Pallas kernels: 9.88 us -> 11.2 us
  starting transfers between devices: 23.6 us -> 22.3 us
    ppermute x8, waiting for transfers between devices: 6.19 us -> 4.59 us  [moved(): return lax.ppermute(value, LINE, pairs)]
    ppermute x2 -> x3, starting transfers between devices: 6.07 us -> 4.65 us  [swap_halves(): return lax.ppermute(value, 'sub', [(0, 1), (1, 0)])]
    ppermute x2, waiting for transfers between devices: 1.45 us -> 0.1 us  [swap_nest(): return lax.ppermute(value, 'nest', [(0, 1), (1, 0)])]
    pallas_call x10 -> x13, Pallas kernels: 9.88 us -> 11.2 us  [call(): pl.pallas_call(body, out_shape=shapes, in_specs=[spec(i, x, far) for i, x...]
    ppermute x2 -> x3, waiting for transfers between devices: 2.92 us -> 3.3 us  [swap_halves(): return lax.ppermute(value, 'sub', [(0, 1), (1, 0)])]
  transfers between devices with their start and end apart: 12 -> 13, of which waited for: 6 -> 5; matrix products, arithmetic and copies ran while one was open for 0% -> 0% of each run, Pallas kernels for 14% -> 17%
where the time goes in v4:
time: 42.6 us; the launch traced here: 42.3 us
  starting transfers between devices  22.3 us (52%)
  Pallas kernels  11.2 us (26%)
  waiting for transfers between devices  7.98 us (19%)
  between operations  0.8 us (2%)
    ppermute x8, starting transfers between devices, moved(): return lax.ppermute(value, LINE, pairs)  17.5 us
    pallas_call x13, Pallas kernels, call(): pl.pallas_call(body, out_shape=shapes, in_specs=[spec(i, x, far) for i, x...  11.2 us
    ppermute x3, starting transfers between devices, swap_halves(): return lax.ppermute(value, 'sub', [(0, 1), (1, 0)])  4.65 us
    ppermute x8, waiting for transfers between devices, moved(): return lax.ppermute(value, LINE, pairs)  4.59 us
    ppermute x3, waiting for transfers between devices, swap_halves(): return lax.ppermute(value, 'sub', [(0, 1), (1, 0)])  3.3 us
  transfers between devices with their start and end apart: 13, of which 5 were waited for; matrix products, arithmetic and copies ran while one was open for 0% of the time, Pallas kernels for 17%

profile of v4, /device:TPU:0, one launch (start us, length us, event | category | flops | bytes accessed | tf_op | source)
XLA Modules:
  0.0 42.3 jit_solution(13060812299958783621)
XLA Ops:
  0.6 1.2 %shard_map.103.wd_ref.own_wd_ref = f32[64,1024]{1,0:T(8,128)S(1)} custom-call(f32[64,1024]{1,0:T(8,128)} %bitcast.14, s32[64,1024]{1,0:T(8,128)} %bitcast.15), custom_call_target="tpu_custom_call" | custom-call | bytes 262144 | tf_op jit(solution)/shard_map/pallas_call | solution.py:42
  1.8 3.0 %collective-permute-start.1 = (f32[64,1024]{1,0:T(8,128)S(1)}, f32[64,1024]{1,0:T(8,128)S(1)}, u32[]{:S(2)}, u32[]{:S(2)}) collective-permute-start(f32[64,1024]{1,0:T(8,128)S(1)} %shard_map.103.wd_ref.own_wd_ref), channel_id=1, source_target_pairs={{0,1},{1,0},{2,3},{3,2},{4,5},{5,4},{6,7},{7,6},{8,9},{9,8},{10,11... | collective-permute-start | bytes 786440 | tf_op jit(solution)/shard_map/ppermute | solution.py:26
  4.8 0.0 copy-start
  4.8 1.5 %shard_map.104 = (f32[72,1024]{1,0:T(8,128)S(1)}, f32[4,1024]{1,0:T(4,128)S(1)}, f32[64,1024]{1,0:T(8,128)S(1)}, f32[64,1024]{1,0:T(8,128)S(1)}) custom-call(f32[64,1024]{1,0:T(8,128)} %bitcast.16, f32[64,1024]{1,0:T(8,128)} %bitcast.17, f32[64,1024]{1,0:T(8,128)} %bitcast.18, f32[64,1024]{1,0:T(8,128)S(1)} %shard_map.103.wd_ref.own_wd_ref), custom_call_target="tpu_custom_call" | custom-call | bytes 1097728 | tf_op jit(solution)/shard_map/pallas_call | solution.py:42
  6.3 0.1 collective-permute-start
  6.4 1.3 %collective-permute-start.3 = (f32[4,1024]{1,0:T(4,128)S(1)}, f32[4,1024]{1,0:T(4,128)S(1)}, u32[]{:S(2)}, u32[]{:S(2)}) collective-permute-start(f32[4,1024]{1,0:T(4,128)S(1)} %get-tuple-element.29), channel_id=1, source_target_pairs={{1,3},{2,0},{3,5},{4,2},{5,7},{6,4},{7,9},{8,6},{9,11},{10,8},{11,... | collective-permute-start | bytes 49160 | tf_op jit(solution)/shard_map/ppermute | solution.py:22
  7.7 0.7 %collective-permute-start.2 = (f32[4,1024]{1,0:T(4,128)S(1)}, f32[4,1024]{1,0:T(4,128)S(1)}, u32[]{:S(2)}, u32[]{:S(2)}) collective-permute-start(f32[4,1024]{1,0:T(4,128)S(1)} %get-tuple-element.29), channel_id=1, source_target_pairs={{1,2},{2,1},{3,4},{4,3},{5,6},{6,5},{7,8},{8,7},{9,10},{10,9},{11,... | collective-permute-start | bytes 49160 | tf_op jit(solution)/shard_map/ppermute | solution.py:22
  8.3 3.7 %collective-permute-done.3.along_ref = f32[4,1024]{1,0:T(4,128)S(1)} collective-permute-done((f32[4,1024]{1,0:T(4,128)S(1)}, f32[4,1024]{1,0:T(4,128)S(1)}, u32[]{:S(2)}, u32[]{:S(2)}) %collective-permute-start.3) | collective-permute-done | bytes 16416 | tf_op jit(solution)/shard_map/ppermute | solution.py:22
  12.0 0.0 copy-done
  12.0 1.9 %shard_map.105 = (f32[64,1024]{1,0:T(8,128)S(1)}, f32[64,1024]{1,0:T(8,128)S(1)}, f32[128,128]{1,0:T(8,128)S(1)}) custom-call(f32[64,1024]{1,0:T(8,128)S(1)} %get-tuple-element.30.h_ref, f32[64,1024]{1,0:T(8,128)S(1)} %get-tuple-element.31.mx_ref, f32[64,1024]{1,0:T(8,128)S(1)} %shard_map.103.wd_ref.own_wd_ref, f32[8,128,128]{2,1,0:T(8,128)S(1)} %bitcast.10, ...), custom_call_target="tpu_custom_call" | custom-call | flops 67108864 | bytes 1916928 | tf_op jit(solution)/shard_map/pallas_call | solution.py:42
  13.9 0.0 collective-permute-done.1.other_wd_ref
  13.9 0.3 shard_map.106.inner_ref
  14.2 0.0 collective-permute-done.2.cross_ref
  14.2 3.3 %collective-permute-done.other_ref = f32[72,1024]{1,0:T(8,128)S(1)} collective-permute-done((f32[72,1024]{1,0:T(8,128)S(1)}, f32[72,1024]{1,0:T(8,128)S(1)}, u32[]{:S(2)}, u32[]{:S(2)}) %collective-permute-start) | collective-permute-done | bytes 294944 | tf_op jit(solution)/shard_map/ppermute | solution.py:26
  17.5 0.9 %shard_map.107 = (f32[128,1024]{1,0:T(8,128)S(1)}, f32[128,1024]{1,0:T(8,128)S(1)}, f32[8,1024]{1,0:T(8,128)S(1)}, f32[8,1024]{1,0:T(8,128)S(1)}) custom-call(f32[72,1024]{1,0:T(8,128)S(1)} %get-tuple-element.28.own_ref, f32[64,1024]{1,0:T(8,128)S(1)} %shard_map.103.wd_ref.own_wd_ref, f32[72,1024]{1,0:T(8,128)S(1)} %collective-permute-done.other_ref, ...), custom_call_target="tpu_custom_call" | custom-call | flops 67108864 | bytes 2850816 | tf_op jit(solution)/shard_map/pallas_call | solution.py:42
  18.3 2.1 %collective-permute-start.4 = (f32[8,1024]{1,0:T(8,128)S(1)}, f32[8,1024]{1,0:T(8,128)S(1)}, u32[]{:S(2)}, u32[]{:S(2)}) collective-permute-start(f32[8,1024]{1,0:T(8,128)S(1)} %get-tuple-element.35.msg_ref), channel_id=1, source_target_pairs={{0,2},{1,3},{2,0},{3,1},{4,6},{5,7},{6,4},{7,5},{8,10},{9,11},{10,... | collective-permute-start | bytes 98312 | tf_op jit(solution)/shard_map/ppermute | solution.py:22
  20.4 0.0 copy-start.1
  20.5 1.5 %collective-permute-start.7 = (f32[64,1024]{1,0:T(8,128)S(1)}, f32[64,1024]{1,0:T(8,128)S(1)}, u32[]{:S(2)}, u32[]{:S(2)}) collective-permute-start(f32[64,1024]{1,0:T(8,128)S(1)} %get-tuple-element.38.hx_ref.own_hx_ref), channel_id=1, source_target_pairs={{0,1},{1,0},{2,3},{3,2},{4,5},{5,4},{6,7},{7,6},{8,9},{9,8},{10,11... | collective-permute-start | bytes 786440 | tf_op jit(solution)/shard_map/ppermute | solution.py:26
  22.0 0.4 collective-permute-done.4.even_ref
  22.4 0.7 %collective-permute-start.5 = (f32[8,1024]{1,0:T(8,128)S(1)}, f32[8,1024]{1,0:T(8,128)S(1)}, u32[]{:S(2)}, u32[]{:S(2)}) collective-permute-start(f32[8,1024]{1,0:T(8,128)S(1)} %shard_map.108), channel_id=1, source_target_pairs={{4,8},{5,9},{6,10},{7,11},{8,4},{9,5},{10,6},{11,7},{20,24},{21,25... | collective-permute-start | bytes 98312 | tf_op jit(solution)/shard_map/ppermute | solution.py:22
  23.0 5.0 %collective-permute-start.6 = (f32[8,1024]{1,0:T(8,128)S(1)}, f32[8,1024]{1,0:T(8,128)S(1)}, u32[]{:S(2)}, u32[]{:S(2)}) collective-permute-start(f32[8,1024]{1,0:T(8,128)S(1)} %shard_map.108), channel_id=1, source_target_pairs={{0,4},{1,5},{2,6},{3,7},{4,0},{5,1},{6,2},{7,3},{8,12},{9,13},{10,... | collective-permute-start | bytes 98312 | tf_op jit(solution)/shard_map/ppermute | solution.py:22
  28.0 0.0 collective-permute-done.7.other_ref.other_hx_ref
  28.0 0.0 copy-done.1
  28.0 0.3 shard_map.110
  28.4 0.1 collective-permute-start.8
  28.5 0.9 %shard_map.109.hx_below_ref = f32[8,1024]{1,0:T(8,128)S(1)} custom-call(f32[4,1024]{1,0:T(4,128)S(1)} %collective-permute-done.2.cross_ref, f32[4,1024]{1,0:T(4,128)S(1)} %collective-permute-done.3.along_ref, f32[8,128,128]{2,1,0:T(8,128)S(1)} %bitcast.11), custom_call_target="tpu_custom_call" | custom-call | bytes 589824 | tf_op jit(solution)/shard_map/pallas_call | solution.py:42
  29.4 0.0 collective-permute-done.5.odd2_ref
  29.4 0.5 %collective-permute-done.6.even2_ref = f32[8,1024]{1,0:T(8,128)S(1)} collective-permute-done((f32[8,1024]{1,0:T(8,128)S(1)}, f32[8,1024]{1,0:T(8,128)S(1)}, u32[]{:S(2)}, u32[]{:S(2)}) %collective-permute-start.6) | collective-permute-done | bytes 32800 | tf_op jit(solution)/shard_map/ppermute | solution.py:22
  29.9 0.0 collective-permute-done.8.packet_ref
  29.9 1.2 %shard_map.111 = (f32[64,1024]{1,0:T(8,128)S(1)}, f32[128,1024]{1,0:T(8,128)S(1)}, f32[4,1024]{1,0:T(4,128)S(1)}, f32[8,1024]{1,0:T(8,128)S(1)}, f32[8,1024]{1,0:T(8,128)S(1)}, /*index=5*/f32[1,1024]{1,0:T(1,128)S(1)}) custom-call(f32[128,1024]{1,0:T(8,128)S(1)} %get-tuple-element.33.flow_ref, f32[128,1024]{1,0:T(8,128)S(1)} %get-tuple-element.34.face_ref, ...), custom_call_target="tpu_custom_call" | custom-call | flops 67108864 | bytes 2711552 | tf_op jit(solution)/shard_map/pallas_call | solution.py:42
  31.1 0.7 %collective-permute-start.10 = (f32[4,1024]{1,0:T(4,128)S(1)}, f32[4,1024]{1,0:T(4,128)S(1)}, u32[]{:S(2)}, u32[]{:S(2)}) collective-permute-start(f32[4,1024]{1,0:T(4,128)S(1)} %get-tuple-element.40.msg_ref), channel_id=1, source_target_pairs={{2,4},{3,5},{4,2},{5,3},{6,8},{7,9},{8,6},{9,7},{10,12},{11,13},{1... | collective-permute-start | bytes 49160 | tf_op jit(solution)/shard_map/ppermute | solution.py:22
  31.8 4.8 %collective-permute-start.9 = (f32[4,1024]{1,0:T(4,128)S(1)}, f32[4,1024]{1,0:T(4,128)S(1)}, u32[]{:S(2)}, u32[]{:S(2)}) collective-permute-start(f32[4,1024]{1,0:T(4,128)S(1)} %get-tuple-element.40.msg_ref), channel_id=1, source_target_pairs={{0,2},{1,3},{2,0},{3,1},{4,6},{5,7},{6,4},{7,5},{8,10},{9,11},{10,... | collective-permute-start | bytes 49160 | tf_op jit(solution)/shard_map/ppermute | solution.py:22
  36.6 2.3 %collective-permute-start.11 = (f32[1,1024]{1,0:T(1,128)S(1)}, f32[1,1024]{1,0:T(1,128)S(1)}, u32[]{:S(2)}, u32[]{:S(2)}) collective-permute-start(f32[1,1024]{1,0:T(1,128)S(1)} %get-tuple-element.49), channel_id=1, source_target_pairs={{0,4},{2,6},{4,8},{6,10},{8,12},{10,14},{16,20},{18,22},{20,24},{2... | collective-permute-start | bytes 12296 | tf_op jit(solution)/shard_map/ppermute | solution.py:22
  38.9 1.1 %shard_map.112 = (f32[64,1024]{1,0:T(8,128)S(1)}, f32[64,1024]{1,0:T(8,128)S(1)}) custom-call(f32[64,1024]{1,0:T(8,128)S(1)} %get-tuple-element.41.h_ref, f32[64,1024]{1,0:T(8,128)S(1)} %get-tuple-element.42.mx_ref, f32[64,1024]{1,0:T(8,128)S(1)} %shard_map.103.wd_ref.own_wd_ref, f32[8,128,128]{2,1,0:T(8,128)S(1)} %bitcast.12), custom_call_target="tpu_custom_call" | custom-call | flops 67108864 | bytes 1835008 | tf_op jit(solution)/shard_map/pallas_call | solution.py:42
  40.0 0.0 collective-permute-done.10.odd_ref.other_ref
  40.0 0.0 collective-permute-done.9.even_ref
  40.1 0.3 shard_map.114
  40.4 0.1 collective-permute-start.12
  40.5 1.0 %shard_map.113 = (f32[64,1024]{1,0:T(8,128)}, f32[64,1024]{1,0:T(8,128)}, f32[64,1024]{1,0:T(8,128)}, f32[16,1024]{1,0:T(8,128)S(1)}, f32[8,1024]{1,0:T(8,128)S(1)}) custom-call(f32[128,1024]{1,0:T(8,128)S(1)} %get-tuple-element.39.flow_ref, f32[4,1024]{1,0:T(4,128)S(1)} %collective-permute-done.9.even_ref, ...), custom_call_target="tpu_custom_call" | custom-call | bytes 2555904 | tf_op jit(solution)/shard_map/pallas_call | solution.py:42
  41.5 0.0 collective-permute-done.11.above2_ref
  41.5 0.1 collective-permute-done.12.packet_ref
  41.6 0.7 %shard_map.115 = f32[64,1024]{1,0:T(8,128)} custom-call(f32[64,1024]{1,0:T(8,128)} %get-tuple-element.45.h_in, f32[16,1024]{1,0:T(8,128)S(1)} %get-tuple-element.46.edge_ref, f32[8,1024]{1,0:T(8,128)S(1)} %get-tuple-element.47.before_ref, f32[4,1024]{1,0:T(4,128)S(1)} %get-tuple-element.40.msg_ref, ...), custom_call_target="tpu_custom_call", output_to_operand_aliasing={{}: (0, {})} | custom-call | bytes 417792 | tf_op jit(solution)/shard_map/pallas_call | solution.py:42
  (1 shorter events, 0.0 us)
Async XLA Ops:
  1.8 12.1 %collective-permute-start.1 = (f32[64,1024]{1,0:T(8,128)S(1)}, f32[64,1024]{1,0:T(8,128)S(1)}, u32[]{:S(2)}, u32[]{:S(2)}) collective-permute-start(f32[64,1024]{1,0:T(8,128)S(1)} %shard_map.103.wd_ref.own_wd_ref), channel_id=1, source_target_pairs={{0,1},{1,0},{2,3},{3,2},{4,5},{5,4},{6,7},{7,6},{8,9},{9,8},{10,11... | collective-permute-start | bytes 786440 | tf_op jit(solution)/shard_map/ppermute | solution.py:26
  4.8 7.2 %copy-start = (f32[1,8,128,128]{3,2,1,0:T(8,128)S(1)}, f32[1,8,128,128]{3,2,1,0:T(8,128)}, u32[]{:S(2)}) copy-start(f32[1,8,128,128]{3,2,1,0:T(8,128)} %param.13) | copy-start | bytes 1572868
  6.3 11.2 %collective-permute-start = (f32[72,1024]{1,0:T(8,128)S(1)}, f32[72,1024]{1,0:T(8,128)S(1)}, u32[]{:S(2)}, u32[]{:S(2)}) collective-permute-start(f32[72,1024]{1,0:T(8,128)S(1)} %get-tuple-element.28.own_ref), channel_id=1, source_target_pairs={{0,1},{1,0},{2,3},{3,2},{4,5},{5,4},{6,7},{7,6},{8,9},{9,8},{10,11... | collective-permute-start | bytes 884744 | tf_op jit(solution)/shard_map/ppermute | solution.py:26
  6.4 5.6 %collective-permute-start.3 = (f32[4,1024]{1,0:T(4,128)S(1)}, f32[4,1024]{1,0:T(4,128)S(1)}, u32[]{:S(2)}, u32[]{:S(2)}) collective-permute-start(f32[4,1024]{1,0:T(4,128)S(1)} %get-tuple-element.29), channel_id=1, source_target_pairs={{1,3},{2,0},{3,5},{4,2},{5,7},{6,4},{7,9},{8,6},{9,11},{10,8},{11,... | collective-permute-start | bytes 49160 | tf_op jit(solution)/shard_map/ppermute | solution.py:22
  7.7 6.5 %collective-permute-start.2 = (f32[4,1024]{1,0:T(4,128)S(1)}, f32[4,1024]{1,0:T(4,128)S(1)}, u32[]{:S(2)}, u32[]{:S(2)}) collective-permute-start(f32[4,1024]{1,0:T(4,128)S(1)} %get-tuple-element.29), channel_id=1, source_target_pairs={{1,2},{2,1},{3,4},{4,3},{5,6},{6,5},{7,8},{8,7},{9,10},{10,9},{11,... | collective-permute-start | bytes 49160 | tf_op jit(solution)/shard_map/ppermute | solution.py:22
  18.3 4.0 %collective-permute-start.4 = (f32[8,1024]{1,0:T(8,128)S(1)}, f32[8,1024]{1,0:T(8,128)S(1)}, u32[]{:S(2)}, u32[]{:S(2)}) collective-permute-start(f32[8,1024]{1,0:T(8,128)S(1)} %get-tuple-element.35.msg_ref), channel_id=1, source_target_pairs={{0,2},{1,3},{2,0},{3,1},{4,6},{5,7},{6,4},{7,5},{8,10},{9,11},{10,... | collective-permute-start | bytes 98312 | tf_op jit(solution)/shard_map/ppermute | solution.py:22
  20.4 7.6 %copy-start.1 = (s32[2,2,1024]{2,1,0:T(2,128)S(1)}, s32[2,2,1024]{2,1,0:T(2,128)}, u32[]{:S(2)}) copy-start(s32[2,2,1024]{2,1,0:T(2,128)} %map_ref.3) | copy-start | bytes 49156
  20.5 7.6 %collective-permute-start.7 = (f32[64,1024]{1,0:T(8,128)S(1)}, f32[64,1024]{1,0:T(8,128)S(1)}, u32[]{:S(2)}, u32[]{:S(2)}) collective-permute-start(f32[64,1024]{1,0:T(8,128)S(1)} %get-tuple-element.38.hx_ref.own_hx_ref), channel_id=1, source_target_pairs={{0,1},{1,0},{2,3},{3,2},{4,5},{5,4},{6,7},{7,6},{8,9},{9,8},{10,11... | collective-permute-start | bytes 786440 | tf_op jit(solution)/shard_map/ppermute | solution.py:26
  22.4 7.0 %collective-permute-start.5 = (f32[8,1024]{1,0:T(8,128)S(1)}, f32[8,1024]{1,0:T(8,128)S(1)}, u32[]{:S(2)}, u32[]{:S(2)}) collective-permute-start(f32[8,1024]{1,0:T(8,128)S(1)} %shard_map.108), channel_id=1, source_target_pairs={{4,8},{5,9},{6,10},{7,11},{8,4},{9,5},{10,6},{11,7},{20,24},{21,25... | collective-permute-start | bytes 98312 | tf_op jit(solution)/shard_map/ppermute | solution.py:22
  23.0 6.9 %collective-permute-start.6 = (f32[8,1024]{1,0:T(8,128)S(1)}, f32[8,1024]{1,0:T(8,128)S(1)}, u32[]{:S(2)}, u32[]{:S(2)}) collective-permute-start(f32[8,1024]{1,0:T(8,128)S(1)} %shard_map.108), channel_id=1, source_target_pairs={{0,4},{1,5},{2,6},{3,7},{4,0},{5,1},{6,2},{7,3},{8,12},{9,13},{10,... | collective-permute-start | bytes 98312 | tf_op jit(solution)/shard_map/ppermute | solution.py:22
  28.4 1.5 %collective-permute-start.8 = (f32[1,1024]{1,0:T(1,128)S(1)}, f32[1,1024]{1,0:T(1,128)S(1)}, u32[]{:S(2)}, u32[]{:S(2)}) collective-permute-start(f32[1,1024]{1,0:T(1,128)S(1)} %shard_map.110), channel_id=1, source_target_pairs={{0,16},{16,0},{1,17},{17,1},{2,18},{18,2},{3,19},{19,3},{4,20},{20... | collective-permute-start | bytes 12296 | tf_op jit(solution)/shard_map/ppermute | solution.py:30
  31.1 8.9 %collective-permute-start.10 = (f32[4,1024]{1,0:T(4,128)S(1)}, f32[4,1024]{1,0:T(4,128)S(1)}, u32[]{:S(2)}, u32[]{:S(2)}) collective-permute-start(f32[4,1024]{1,0:T(4,128)S(1)} %get-tuple-element.40.msg_ref), channel_id=1, source_target_pairs={{2,4},{3,5},{4,2},{5,3},{6,8},{7,9},{8,6},{9,7},{10,12},{11,13},{1... | collective-permute-start | bytes 49160 | tf_op jit(solution)/shard_map/ppermute | solution.py:22
  31.8 8.2 %collective-permute-start.9 = (f32[4,1024]{1,0:T(4,128)S(1)}, f32[4,1024]{1,0:T(4,128)S(1)}, u32[]{:S(2)}, u32[]{:S(2)}) collective-permute-start(f32[4,1024]{1,0:T(4,128)S(1)} %get-tuple-element.40.msg_ref), channel_id=1, source_target_pairs={{0,2},{1,3},{2,0},{3,1},{4,6},{5,7},{6,4},{7,5},{8,10},{9,11},{10,... | collective-permute-start | bytes 49160 | tf_op jit(solution)/shard_map/ppermute | solution.py:22
  36.6 4.9 %collective-permute-start.11 = (f32[1,1024]{1,0:T(1,128)S(1)}, f32[1,1024]{1,0:T(1,128)S(1)}, u32[]{:S(2)}, u32[]{:S(2)}) collective-permute-start(f32[1,1024]{1,0:T(1,128)S(1)} %get-tuple-element.49), channel_id=1, source_target_pairs={{0,4},{2,6},{4,8},{6,10},{8,12},{10,14},{16,20},{18,22},{20,24},{2... | collective-permute-start | bytes 12296 | tf_op jit(solution)/shard_map/ppermute | solution.py:22
  40.4 1.2 %collective-permute-start.12 = (f32[1,1024]{1,0:T(1,128)S(1)}, f32[1,1024]{1,0:T(1,128)S(1)}, u32[]{:S(2)}, u32[]{:S(2)}) collective-permute-start(f32[1,1024]{1,0:T(1,128)S(1)} %shard_map.114), channel_id=1, source_target_pairs={{0,16},{16,0},{1,17},{17,1},{2,18},{18,2},{3,19},{19,3},{4,20},{20... | collective-permute-start | bytes 12296 | tf_op jit(solution)/shard_map/ppermute | solution.py:30

commit v5 on v4

--- a/solution.py
+++ b/solution.py
@@ -51,6 +51,14 @@
     )(*[pltpu.with_memory_space_constraint(x, pltpu.HBM) if i in far else x for i, x in enumerate(ins)])
 
 
+def by_columns(body, width, step):
+    def run(*refs):
+        for start in range(0, width, step):
+            body(*[ref.at[:, pl.ds(start, step)] if ref.shape[-1] == width else ref for ref in refs])
+
+    return run
+
+
 def face_of(a, b):
     return jnp.where(jnp.logical_and(a > 0.0, b > 0.0), 0.5 * (a + b), 0.0)
 
@@ -61,24 +69,24 @@
     return high, low
 
 
+def stacked(a):
+    high, low = split(a)
+    return jnp.concatenate([jnp.concatenate([high, high], 1), jnp.concatenate([low, jnp.zeros_like(low)], 1)], 0)
+
+
+def folded(product):
+    rows = product.shape[0] // 2
+    return product[:rows] + product[rows:]
+
+
 def matmul(a, b):
-    a_high, a_low = split(a)
-    b_high, b_low = split(b)
-    return jnp.dot(
-        jnp.concatenate([a_high, a_high, a_low], 1),
-        jnp.concatenate([b_high, b_low, b_high], 0),
-        preferred_element_type=F32,
-    )
+    return folded(jnp.dot(stacked(a), jnp.concatenate(split(b), 0), preferred_element_type=F32))
 
 
 def matmul_t(a, b):
-    a_high, a_low = split(a)
-    b_high, b_low = split(b)
-    return lax.dot_general(
-        jnp.concatenate([a_high, a_high, a_low], 1),
-        jnp.concatenate([b_high, b_low, b_high], 1),
-        (((1,), (1,)), ((), ())),
-        preferred_element_type=F32,
+    wide = jnp.concatenate(split(b), 1)
+    return folded(
+        lax.dot_general(stacked(a), wide, (((1,), (1,)), ((), ())), preferred_element_type=F32)
     )
 
 
@@ -125,7 +133,8 @@
     h = h_ref[...]
     buf_ref[0:n] = my_ref[...] + 0.5 * face_of(wd, next_row(wd, 0.0)) * (next_row(h, 0.0) - h)
     buf_ref[n : n + 8] = jnp.concatenate([h[0:1], h[n - 1 : n], jnp.zeros((6, width), F32)], 0)
-    edge_ref[...] = jnp.concatenate([h[0:1], wd[0:1], wd[n - 1 : n], mx_ref[0:1]], 0)
+    outward = jnp.where(lax.axis_index("sub") == 0, wd[0:1], wd[n - 1 : n])
+    edge_ref[...] = jnp.concatenate([h[0:1], outward, mx_ref[0:1], face_of(wd[0:1], wd[1:2])], 0)
 
 
 def across(h_ref, mx_ref, wd_ref, table_ref, flow_ref, hx_ref, push_ref, first_ref):
@@ -156,19 +165,30 @@
 
 
 def across_first_body(
-    h_ref, mx_ref, wd_ref, table_ref, tables_far, along_ref, flow_ref, hx_ref, line_table_ref, push_ref, first_ref, sem
+    h_ref, mx_ref, wd_ref, table_ref, tables_far, along_ref,
+    flow_ref, hx_ref, line_table_ref, near_tables_ref, push_ref, first_ref, sems,
 ):
-    fetch_table = pltpu.make_async_copy(tables_far.at[lax.axis_index("rows")], line_table_ref, sem)
-    fetch_table.start()
+    block = lax.axis_index("rows")
+    group = line_table_ref.shape[0]
+    up = jnp.maximum(block - 1, 0)
+    down = jnp.minimum(block + 1, tables_far.shape[0] - 1)
+    fetches = [
+        pltpu.make_async_copy(tables_far.at[block], line_table_ref, sems.at[0]),
+        pltpu.make_async_copy(tables_far.at[up, pl.ds(group - 8, 8)], near_tables_ref.at[pl.ds(0, 8)], sems.at[1]),
+        pltpu.make_async_copy(tables_far.at[down, pl.ds(0, 8)], near_tables_ref.at[pl.ds(8, 8)], sems.at[2]),
+    ]
+    for fetch in fetches:
+        fetch.start()
     across(h_ref, mx_ref, wd_ref, table_ref, flow_ref, hx_ref, push_ref, first_ref)
-    fetch_table.wait()
+    for fetch in fetches:
+        fetch.wait()
 
 
 def across_below_body(cross_ref, along_ref, table_ref, hx_ref, h_ref, mx_ref, wd_ref, flow_ref, push_ref, first_ref):
     below = jnp.where(lax.axis_index("sub") == 0, along_ref[...], cross_ref[...])
     h_ref[...] = jnp.broadcast_to(below[0:1], h_ref.shape)
     wd_ref[...] = jnp.broadcast_to(below[1:2], h_ref.shape)
-    mx_ref[...] = jnp.broadcast_to(below[3:4], h_ref.shape)
+    mx_ref[...] = jnp.broadcast_to(below[2:3], h_ref.shape)
     across(h_ref, mx_ref, wd_ref, table_ref, flow_ref, hx_ref, push_ref, first_ref)
 
 
@@ -176,8 +196,8 @@
     is_even = lax.rem(lax.axis_index("rows"), 2) == 0
     even = even_ref[...]
     msg = msg_ref[...]
-    passed = jnp.where(is_even, even[4:8], even[0:4])
-    out_ref[...] = jnp.concatenate([msg[0:1], msg[4:5], passed, jnp.zeros((2, msg.shape[1]), F32)], 0)
+    passed = jnp.where(is_even, even[2:4], even[0:2])
+    out_ref[...] = jnp.concatenate([msg[0:1], msg[2:3], passed], 0)
 
 
 def packet_body(nest_ref, even_ref, map_ref, hx_ref, other_ref, packet_ref):
@@ -194,22 +214,15 @@
 
 
 def nest_factor(even_ref):
-    down = even_ref.shape[0] // 2
-    if down == 2:
-        down = 1
-    return jnp.where(lax.axis_index("rows") == 0, even_ref[0:1], even_ref[down : down + 1])
+    return jnp.where(lax.axis_index("rows") == 0, even_ref[0:1], even_ref[2:3])
 
 
 def solve_lines(push, face, face_above, table):
     coef = 0.5 * face * face
     coef_above = 0.5 * face_above * face_above
     first = matmul(table, push)
-    operated = (
-        first
-        + coef * (first - next_row(first, 0.0))
-        + prev_row(coef, coef_above) * (first - prev_row(first, 0.0))
-    )
-    flow = first + matmul(table, push - operated)
+    step = coef * (first - next_row(first, 0.0))
+    flow = first + matmul(table, push - first - step + prev_row(step, -(coef_above * first[0:1])))
     g = push.shape[0]
     t_up = coef_above * first[0:1]
     u_down = coef[g - 1 : g] * first[g - 1 : g]
@@ -219,20 +232,10 @@
 def messages(flow, face, t_up, u_down, table, is_first):
     g = flow.shape[0]
     half_top = 0.5 * face[0:1]
-    bottom = face[g - 1 : g]
     side = 0.5 * face[g - 2 : g - 1]
-    rows = [
-        t_up,
-        half_top * flow[0:1],
-        half_top * table[0:1, g - 1 : g],
-        half_top * table[0:1, 0:1],
-        u_down,
-        bottom * flow[g - 1 : g],
-        bottom * table[g - 1 : g, g - 1 : g],
-        bottom * table[g - 1 : g, 0:1],
-    ]
+    rows = [t_up, half_top * flow[0:1], u_down, face[g - 1 : g] * flow[g - 1 : g]]
     nest_base = jnp.where(is_first, rows[1], -(side * flow[g - 2 : g - 1]))
-    nest_coef = jnp.where(is_first, rows[2], -(side * table[g - 2 : g - 1, 0:1]))
+    nest_coef = jnp.where(is_first, half_top * table[0:1, g - 1 : g], -(side * table[g - 2 : g - 1, 0:1]))
     return jnp.concatenate(rows, 0), jnp.concatenate([nest_base, nest_coef], 0)
 
 
@@ -246,8 +249,8 @@
 
 
 def lines_body(
-    own_ref, own_wd_ref, other_ref, other_wd_ref, cross_ref, along_ref, table_ref, inner_ref,
-    flow_ref, face_ref, msg_ref, nest_ref, push_ref,
+    own_ref, own_wd_ref, other_ref, other_wd_ref, cross_ref, along_ref, table_ref, near_tables_ref, inner_ref,
+    flow_ref, face_ref, msg_ref, nest_ref, gain_ref, push_ref,
 ):
     g = table_ref.shape[0]
     n = g // 2
@@ -266,23 +269,27 @@
     bottom = jnp.where(lower, other, own)
     below = jnp.where(lower, along, cross)
     above = jnp.where(lower, cross, along)
-    face = inner_ref[...]
     wd_last = jnp.where(lower, other_wd_ref[n - 1 : n], own_wd_ref[n - 1 : n])
-    face = jnp.where(row_iota(face.shape) == g - 1, face_of(wd_last, below[1:2]), face)
-    face_above = face_of(above[2:3], jnp.where(lower, own_wd_ref[0:1], other_wd_ref[0:1]))
-    south = jnp.where(
-        row_iota(face.shape) == n - 1,
-        0.5 * face * (bottom[0:1] - top[1:2]),
-        jnp.where(row_iota(face.shape) == g - 1, 0.5 * face * (below[0:1] - bottom[1:2]), 0.0),
-    )
+    face_ref[...] = inner_ref[...]
+    face_ref[g - 1 : g] = face_of(wd_last, below[1:2])
+    face_above = face_of(above[1:2], jnp.where(lower, own_wd_ref[0:1], other_wd_ref[0:1]))
+    push_ref[n - 1 : n] += 0.5 * face_ref[n - 1 : n] * (bottom[0:1] - top[1:2])
+    push_ref[g - 1 : g] += 0.5 * face_ref[g - 1 : g] * (below[0:1] - bottom[1:2])
+    face = face_ref[...]
     table = table_ref[...]
-    flow, t_up, u_down = solve_lines(push_ref[...] + south, face, face_above, table)
+    flow, t_up, u_down = solve_lines(push_ref[...], face, face_above, table)
     flow_ref[...] = flow
-    face_ref[...] = face
     rows, nest_rows = messages(flow, face, t_up, u_down, table, is_first)
     msg_ref[...] = rows
     nest_ref[0:1] = nest_rows[0:1]
     nest_ref[1:2] = nest_rows[1:2]
+    half_below = 0.5 * below[3:4]
+    near = near_tables_ref[...]
+    gain_ref[0:1] = half_below * near[8:9, g - 1 : g]
+    gain_ref[1:2] = half_below * near[8:9, 0:1]
+    gain_ref[2:3] = face_above * near[7:8, g - 1 : g]
+    gain_ref[3:4] = face_above * near[7:8, 0:1]
+    gain_ref[4:8] = jnp.zeros((4, half_below.shape[1]), F32)
     nest_ref[2:3] = face_above
     nest_ref[3:8] = jnp.zeros((5, face.shape[1]), F32)
 
@@ -317,12 +324,12 @@
     odd2 = odd2_ref[...]
     up = jnp.where(is_low, odd2, even2)
     down = jnp.where(is_low, even2, odd2)
-    return jnp.where(is_even, up[2:6], even[4:8]), jnp.where(is_even, even[0:4], down[2:6]), up[1:2], down[0:1]
+    return jnp.where(is_even, up[2:4], even[2:4]), jnp.where(is_even, even[0:2], down[2:4]), up[1:2], down[0:1]
 
 
 def between_body(
-    flow_ref, face_ref, msg_ref, nest_ref, even_ref, odd2_ref, even2_ref, own_hx_ref, other_hx_ref,
-    hx_below_ref, packet_ref, table_ref, h_ref, next_flow_ref, next_msg_ref, next_nest_ref, gain_ref, u_down_ref, hx_ref,
+    flow_ref, face_ref, msg_ref, nest_ref, gain_ref, even_ref, odd2_ref, even2_ref, own_hx_ref, other_hx_ref,
+    hx_below_ref, packet_ref, table_ref, h_ref, next_flow_ref, next_msg_ref, next_nest_ref, u_down_ref, hx_ref,
 ):
     g = table_ref.shape[0]
     n = g // 2
@@ -343,26 +350,23 @@
     u_row = above[0:1]
     flow = flow_ref[...] + table[:, g - 1 : g] * t_row + table[:, 0:1] * u_row
     flux = face * flow
-    flux_above = above[1:2] + above[2:3] * own[0:1] + above[3:4] * u_above2
-    h_below = hx_below_ref[0:1] + below[1:2] + below[2:3] * t_below2 + below[3:4] * own[4:5] - 0.5 * flux[g - 1 : g]
-    h = hx_ref[...] + 0.5 * (flux - prev_row(flux, flux_above))
+    gain = gain_ref[...]
+    flux_above = above[1:2] + gain[2:3] * own[0:1] + gain[3:4] * u_above2
+    h_below = hx_below_ref[0:1] + below[1:2] + gain[0:1] * t_below2 + gain[1:2] * own[2:3] - 0.5 * flux[g - 1 : g]
+    hx_ref[...] = hx_ref[...] + 0.5 * (flux - prev_row(flux, flux_above))
     packet = packet_ref[0:1]
-    rows = row_iota(h.shape)
-    blend = jnp.logical_and(
-        nearfield,
-        jnp.logical_or(jnp.logical_and(is_first, rows == 0), jnp.logical_and(is_last, rows == g - 1)),
-    )
-    h = jnp.where(blend, 0.5 * h + 0.5 * packet, h)
-    hx_ref[...] = h
+    for row, here in ((0, is_first), (g - 1, is_last)):
+        value = hx_ref[row : row + 1]
+        blended = 0.5 * value + 0.5 * packet
+        hx_ref[row : row + 1] = jnp.where(jnp.logical_and(nearfield, here), blended, value)
+    h = hx_ref[...]
     h_ref[...] = hx_ref[pl.ds(mine, n)]
     push = flow + 0.5 * face * (next_row(h, h_below) - h)
     next_flow, t_up, u_down = solve_lines(push, face, nest_ref[2:3], table)
     next_flow_ref[...] = next_flow
     rows, nest_rows = messages(next_flow, face, t_up, u_down, table, is_first)
-    next_msg_ref[...] = jnp.concatenate([t_up, u_down, rows[5:6], jnp.zeros_like(t_up)], 0)
+    next_msg_ref[...] = rows
     u_down_ref[...] = u_down
-    gain_ref[0:2] = above[2:4]
-    gain_ref[2:8] = jnp.zeros((6, t_up.shape[1]), F32)
     next_nest_ref[0:2] = nest_rows
     next_nest_ref[2:8] = jnp.zeros((6, face.shape[1]), F32)
 
@@ -382,7 +386,7 @@
     above = jnp.where(is_even, odd_ref[...], even_ref[...])
     below = jnp.where(is_even, even_ref[...], odd_ref[...])
     t_row = below[0:1]
-    u_row = above[1:2]
+    u_row = above[2:3]
     table = table_ref[mine]
     flow = flow_ref[mine] + table[:, g - 1 : g] * t_row + table[:, 0:1] * u_row
     my_ref[...] = flow
@@ -398,7 +402,7 @@
     edge_ref[8:16] = h_ref[n - 8 : n]
     flow_mid = flow_ref[n - 1 : n] + table_ref[n - 1 : n, g - 1 : g] * t_row + table_ref[n - 1 : n, 0:1] * u_row
     before_ref[0:1] = face_ref[n - 1 : n] * flow_mid
-    before_ref[1:2] = above[2:3]
+    before_ref[1:2] = above[3:4]
     before_ref[2:8] = jnp.zeros((6, width), F32)
     for copy in copies:
         copy.wait()
@@ -411,7 +415,7 @@
     nearfield = lax.axis_index("nest") == 1
     is_first = jnp.logical_and(nearfield, jnp.logical_and(block == 0, half == 0))
     is_last = jnp.logical_and(nearfield, jnp.logical_and(block == lax.axis_size("rows") - 1, half == 1))
-    flux_above = before_ref[1:2] + gain_ref[0:1] * msg_ref[0:1] + gain_ref[1:2] * above2_ref[...]
+    flux_above = before_ref[1:2] + gain_ref[2:3] * msg_ref[0:1] + gain_ref[3:4] * above2_ref[...]
     before = jnp.where(half == 0, flux_above, before_ref[0:1])
     packet = packet_ref[...]
     edge = edge_ref[...]
@@ -452,18 +456,18 @@
     other = swap_halves(buf)
     cross = moved(edge, lambda k, s: (k + 1, 0) if s == 1 else (k - 1, 1))
     along = moved(edge, lambda k, s: (k + 1, 1) if s == 1 else (k - 1, 0))
-    flow_x, hx, table_y = call(
-        across_first_body, [(n, width), (n, width), (g, g)],
-        [height, flow_x, wd, table_x, inverse_y[0], along], [part, part, dma], solve_flops, far=(4,),
+    flow_x, hx, table_y, near_tables = call(
+        across_first_body, [(n, width), (n, width), (g, g), (16, g)],
+        [height, flow_x, wd, table_x, inverse_y[0], along], [part, part, dma((3,))], solve_flops, far=(4,),
     )
     (inner,) = call(faces_body, [(g, width)], [wd, other_wd], [pltpu.VMEM((g, width), F32)], flops=int(1e9))
-    flow, face, msg, nest = call(
-        lines_body, [(g, width), (g, width), (8, width), (8, width)],
-        [buf, wd, other, other_wd, cross, along, table_y, inner], [pltpu.VMEM((g, width), F32)], solve_flops,
+    flow, face, msg, nest, gain = call(
+        by_columns(lines_body, width, 256), [(g, width), (g, width), (4, width), (8, width), (8, width)],
+        [buf, wd, other, other_wd, cross, along, table_y, near_tables, inner], [pltpu.VMEM((g, width), F32)], solve_flops,
     )
     other_hx = swap_halves(lax.optimization_barrier((hx, msg))[0])
     even = moved(msg, lambda k, s: (k ^ 1, s))
-    (both,) = call(relay_body, [(8, width)], [msg, even], flops=int(3e9))
+    (both,) = call(relay_body, [(4, width)], [msg, even], flops=int(3e9))
     even2 = moved(both, lambda k, s: (k ^ 2, s))
     odd2 = moved(both, lambda k, s: (((k + 2) ^ 2) - 2, s))
     (hx_below,) = call(
@@ -471,9 +475,9 @@
     )
     (packet,) = call(packet_body, [(1, width)], [nest, even, nest_map, hx, other_hx])
     packet = swap_nest(packet)
-    height, flow, msg, nest, gain, u_down = call(
-        between_body, [(n, width), (g, width), (4, width), (8, width), (8, width), (1, width)],
-        [flow, face, msg, nest, even, odd2, even2, hx, other_hx, hx_below, packet, table_y],
+    height, flow, msg, nest, u_down = call(
+        by_columns(between_body, width, 256), [(n, width), (g, width), (4, width), (8, width), (1, width)],
+        [flow, face, msg, nest, gain, even, odd2, even2, hx, other_hx, hx_below, packet, table_y],
         [pltpu.VMEM((g, width), F32)], solve_flops,
     )
     even = moved(msg, lambda k, s: (k ^ 1, s))

time: 42.6 us -> 41.9 us (0.984)
  Pallas kernels: 11.2 us -> 10.4 us
    pallas_call x13, Pallas kernels: 11.2 us -> 10.4 us  [call(): pl.pallas_call(body, out_shape=shapes, in_specs=[spec(i, x, far) for i, x...]
  transfers between devices with their start and end apart: 13 -> 13, of which waited for: 5 -> 5; matrix products, arithmetic and copies ran while one was open for 0% -> 0% of each run, Pallas kernels for 17% -> 16%
where the time goes in v5:
time: 41.9 us; the launch traced here: 41.6 us
  starting transfers between devices  22.4 us (53%)
  Pallas kernels  10.4 us (25%)
  waiting for transfers between devices  8.05 us (19%)
  between operations  0.8 us (2%)
    ppermute x8, starting transfers between devices, moved(): return lax.ppermute(value, LINE, pairs)  17.6 us
    pallas_call x13, Pallas kernels, call(): pl.pallas_call(body, out_shape=shapes, in_specs=[spec(i, x, far) for i, x...  10.4 us
    ppermute x3, starting transfers between devices, swap_halves(): return lax.ppermute(value, 'sub', [(0, 1), (1, 0)])  4.65 us
    ppermute x8, waiting for transfers between devices, moved(): return lax.ppermute(value, LINE, pairs)  4.48 us
    ppermute x3, waiting for transfers between devices, swap_halves(): return lax.ppermute(value, 'sub', [(0, 1), (1, 0)])  3.48 us
  transfers between devices with their start and end apart: 13, of which 5 were waited for; matrix products, arithmetic and copies ran while one was open for 0% of the time, Pallas kernels for 16%

profile of v5, /device:TPU:0, one launch (start us, length us, event | category | flops | bytes accessed | tf_op | source)
XLA Modules:
  0.0 41.6 jit_solution(9594295757913189173)
XLA Ops:
  0.6 1.2 %shard_map.103.wd_ref.own_wd_ref.refs_1_ = f32[64,1024]{1,0:T(8,128)S(1)} custom-call(f32[64,1024]{1,0:T(8,128)} %bitcast.14, s32[64,1024]{1,0:T(8,128)} %bitcast.15), custom_call_target="tpu_custom_call" | custom-call | bytes 262144 | tf_op jit(solution)/shard_map/pallas_call | solution.py:42
  1.8 3.0 %collective-permute-start.1 = (f32[64,1024]{1,0:T(8,128)S(1)}, f32[64,1024]{1,0:T(8,128)S(1)}, u32[]{:S(2)}, u32[]{:S(2)}) collective-permute-start(f32[64,1024]{1,0:T(8,128)S(1)} %shard_map.103.wd_ref.own_wd_ref.refs_1_), channel_id=1, source_target_pairs={{0,1},{1,0},{2,3},{3,2},{4,5},{5,4},{6,7},{7,6},{8,9},{9,8},{10,11... | collective-permute-start | bytes 786440 | tf_op jit(solution)/shard_map/ppermute | solution.py:26
  4.8 0.0 copy-start
  4.8 1.5 %shard_map.104 = (f32[72,1024]{1,0:T(8,128)S(1)}, f32[4,1024]{1,0:T(4,128)S(1)}, f32[64,1024]{1,0:T(8,128)S(1)}, f32[64,1024]{1,0:T(8,128)S(1)}) custom-call(f32[64,1024]{1,0:T(8,128)} %bitcast.16, f32[64,1024]{1,0:T(8,128)} %bitcast.17, f32[64,1024]{1,0:T(8,128)} %bitcast.18, f32[64,1024]{1,0:T(8,128)S(1)} %shard_map.103.wd_ref.own_wd_ref.refs_1_), custom_call_target="tpu_custom_call" | custom-call | bytes 1097728 | tf_op jit(solution)/shard_map/pallas_call | solution.py:42
  6.3 0.1 collective-permute-start
  6.4 1.3 %collective-permute-start.3 = (f32[4,1024]{1,0:T(4,128)S(1)}, f32[4,1024]{1,0:T(4,128)S(1)}, u32[]{:S(2)}, u32[]{:S(2)}) collective-permute-start(f32[4,1024]{1,0:T(4,128)S(1)} %get-tuple-element.30), channel_id=1, source_target_pairs={{1,3},{2,0},{3,5},{4,2},{5,7},{6,4},{7,9},{8,6},{9,11},{10,8},{11,... | collective-permute-start | bytes 49160 | tf_op jit(solution)/shard_map/ppermute | solution.py:22
  7.7 0.7 %collective-permute-start.2 = (f32[4,1024]{1,0:T(4,128)S(1)}, f32[4,1024]{1,0:T(4,128)S(1)}, u32[]{:S(2)}, u32[]{:S(2)}) collective-permute-start(f32[4,1024]{1,0:T(4,128)S(1)} %get-tuple-element.30), channel_id=1, source_target_pairs={{1,2},{2,1},{3,4},{4,3},{5,6},{6,5},{7,8},{8,7},{9,10},{10,9},{11,... | collective-permute-start | bytes 49160 | tf_op jit(solution)/shard_map/ppermute | solution.py:22
  8.4 3.7 %collective-permute-done.3.along_ref.refs_5_ = f32[4,1024]{1,0:T(4,128)S(1)} collective-permute-done((f32[4,1024]{1,0:T(4,128)S(1)}, f32[4,1024]{1,0:T(4,128)S(1)}, u32[]{:S(2)}, u32[]{:S(2)}) %collective-permute-start.3) | collective-permute-done | bytes 16416 | tf_op jit(solution)/shard_map/ppermute | solution.py:22
  12.0 0.0 copy-done
  12.0 1.7 %shard_map.105 = (f32[64,1024]{1,0:T(8,128)S(1)}, f32[64,1024]{1,0:T(8,128)S(1)}, f32[128,128]{1,0:T(8,128)S(1)}, f32[16,128]{1,0:T(8,128)S(1)}) custom-call(f32[64,1024]{1,0:T(8,128)S(1)} %get-tuple-element.31.h_ref, f32[64,1024]{1,0:T(8,128)S(1)} %get-tuple-element.32.mx_ref, f32[64,1024]{1,0:T(8,128)S(1)} %shard_map.103.wd_ref.own_wd_ref.refs_1_, ...), custom_call_target="tpu_custom_call" | custom-call | flops 67108864 | bytes 1925120 | tf_op jit(solution)/shard_map/pallas_call | solution.py:42
  13.7 0.0 collective-permute-done.1.other_wd_ref.refs_3_
  13.7 0.3 shard_map.106.refs_8_
  14.0 0.0 collective-permute-done.2.refs_4_.cross_ref
  14.0 3.5 %collective-permute-done.refs_2_ = f32[72,1024]{1,0:T(8,128)S(1)} collective-permute-done((f32[72,1024]{1,0:T(8,128)S(1)}, f32[72,1024]{1,0:T(8,128)S(1)}, u32[]{:S(2)}, u32[]{:S(2)}) %collective-permute-start) | collective-permute-done | bytes 294944 | tf_op jit(solution)/shard_map/ppermute | solution.py:26
  17.5 0.7 %shard_map.107 = (f32[128,1024]{1,0:T(8,128)S(1)}, f32[128,1024]{1,0:T(8,128)S(1)}, f32[4,1024]{1,0:T(4,128)S(1)}, f32[8,1024]{1,0:T(8,128)S(1)}, f32[8,1024]{1,0:T(8,128)S(1)}) custom-call(f32[72,1024]{1,0:T(8,128)S(1)} %get-tuple-element.29.refs_0_, f32[64,1024]{1,0:T(8,128)S(1)} %shard_map.103.wd_ref.own_wd_ref.refs_1_, ...), custom_call_target="tpu_custom_call" | custom-call | flops 67108864 | bytes 2875392 | tf_op jit(solution)/shard_map/pallas_call | solution.py:42
  18.2 2.1 %collective-permute-start.4 = (f32[4,1024]{1,0:T(4,128)S(1)}, f32[4,1024]{1,0:T(4,128)S(1)}, u32[]{:S(2)}, u32[]{:S(2)}) collective-permute-start(f32[4,1024]{1,0:T(4,128)S(1)} %get-tuple-element.37.msg_ref.refs_2_), channel_id=1, source_target_pairs={{0,2},{1,3},{2,0},{3,1},{4,6},{5,7},{6,4},{7,5},{8,10},{9,11},{10,... | collective-permute-start | bytes 49160 | tf_op jit(solution)/shard_map/ppermute | solution.py:22
  20.3 0.0 copy-start.1
  20.3 1.5 %collective-permute-start.7 = (f32[64,1024]{1,0:T(8,128)S(1)}, f32[64,1024]{1,0:T(8,128)S(1)}, u32[]{:S(2)}, u32[]{:S(2)}) collective-permute-start(f32[64,1024]{1,0:T(8,128)S(1)} %get-tuple-element.41.hx_ref.refs_8_), channel_id=1, source_target_pairs={{0,1},{1,0},{2,3},{3,2},{4,5},{5,4},{6,7},{7,6},{8,9},{9,8},{10,11... | collective-permute-start | bytes 786440 | tf_op jit(solution)/shard_map/ppermute | solution.py:26
  21.9 0.2 collective-permute-done.4.even_ref.refs_5_
  22.1 0.7 %collective-permute-start.5 = (f32[4,1024]{1,0:T(4,128)S(1)}, f32[4,1024]{1,0:T(4,128)S(1)}, u32[]{:S(2)}, u32[]{:S(2)}) collective-permute-start(f32[4,1024]{1,0:T(4,128)S(1)} %shard_map.108), channel_id=1, source_target_pairs={{4,8},{5,9},{6,10},{7,11},{8,4},{9,5},{10,6},{11,7},{20,24},{21,25... | collective-permute-start | bytes 49160 | tf_op jit(solution)/shard_map/ppermute | solution.py:22
  22.7 5.0 %collective-permute-start.6 = (f32[4,1024]{1,0:T(4,128)S(1)}, f32[4,1024]{1,0:T(4,128)S(1)}, u32[]{:S(2)}, u32[]{:S(2)}) collective-permute-start(f32[4,1024]{1,0:T(4,128)S(1)} %shard_map.108), channel_id=1, source_target_pairs={{0,4},{1,5},{2,6},{3,7},{4,0},{5,1},{6,2},{7,3},{8,12},{9,13},{10,... | collective-permute-start | bytes 49160 | tf_op jit(solution)/shard_map/ppermute | solution.py:22
  27.7 0.0 collective-permute-done.7.other_ref.refs_9_
  27.7 0.0 copy-done.1
  27.7 0.3 shard_map.110
  28.1 0.1 collective-permute-start.8
  28.2 0.7 %shard_map.109.refs_10_ = f32[8,1024]{1,0:T(8,128)S(1)} custom-call(f32[4,1024]{1,0:T(4,128)S(1)} %collective-permute-done.2.refs_4_.cross_ref, f32[4,1024]{1,0:T(4,128)S(1)} %collective-permute-done.3.along_ref.refs_5_, f32[8,128,128]{2,1,0:T(8,128)S(1)} %bitcast.11), custom_call_target="tpu_custom_call" | custom-call | bytes 589824 | tf_op jit(solution)/shard_map/pallas_call | solution.py:42
  28.8 0.0 collective-permute-done.5.refs_6_
  28.8 0.6 %collective-permute-done.6.refs_7_ = f32[4,1024]{1,0:T(4,128)S(1)} collective-permute-done((f32[4,1024]{1,0:T(4,128)S(1)}, f32[4,1024]{1,0:T(4,128)S(1)}, u32[]{:S(2)}, u32[]{:S(2)}) %collective-permute-start.6) | collective-permute-done | bytes 16416 | tf_op jit(solution)/shard_map/ppermute | solution.py:22
  29.5 0.0 collective-permute-done.8.refs_11_
  29.5 1.1 %shard_map.111 = (f32[64,1024]{1,0:T(8,128)S(1)}, f32[128,1024]{1,0:T(8,128)S(1)}, f32[4,1024]{1,0:T(4,128)S(1)}, f32[8,1024]{1,0:T(8,128)S(1)}, f32[1,1024]{1,0:T(1,128)S(1)}) custom-call(f32[128,1024]{1,0:T(8,128)S(1)} %get-tuple-element.35.refs_0_, f32[128,1024]{1,0:T(8,128)S(1)} %get-tuple-element.36.refs_1_.face_ref, ...), custom_call_target="tpu_custom_call" | custom-call | flops 67108864 | bytes 2646016 | tf_op jit(solution)/shard_map/pallas_call | solution.py:42
  30.6 0.7 %collective-permute-start.10 = (f32[4,1024]{1,0:T(4,128)S(1)}, f32[4,1024]{1,0:T(4,128)S(1)}, u32[]{:S(2)}, u32[]{:S(2)}) collective-permute-start(f32[4,1024]{1,0:T(4,128)S(1)} %get-tuple-element.43.msg_ref), channel_id=1, source_target_pairs={{2,4},{3,5},{4,2},{5,3},{6,8},{7,9},{8,6},{9,7},{10,12},{11,13},{1... | collective-permute-start | bytes 49160 | tf_op jit(solution)/shard_map/ppermute | solution.py:22
  31.2 4.8 %collective-permute-start.9 = (f32[4,1024]{1,0:T(4,128)S(1)}, f32[4,1024]{1,0:T(4,128)S(1)}, u32[]{:S(2)}, u32[]{:S(2)}) collective-permute-start(f32[4,1024]{1,0:T(4,128)S(1)} %get-tuple-element.43.msg_ref), channel_id=1, source_target_pairs={{0,2},{1,3},{2,0},{3,1},{4,6},{5,7},{6,4},{7,5},{8,10},{9,11},{10,... | collective-permute-start | bytes 49160 | tf_op jit(solution)/shard_map/ppermute | solution.py:22
  36.0 2.4 %collective-permute-start.11 = (f32[1,1024]{1,0:T(1,128)S(1)}, f32[1,1024]{1,0:T(1,128)S(1)}, u32[]{:S(2)}, u32[]{:S(2)}) collective-permute-start(f32[1,1024]{1,0:T(1,128)S(1)} %get-tuple-element.51), channel_id=1, source_target_pairs={{0,4},{2,6},{4,8},{6,10},{8,12},{10,14},{16,20},{18,22},{20,24},{2... | collective-permute-start | bytes 12296 | tf_op jit(solution)/shard_map/ppermute | solution.py:22
  38.4 0.9 %shard_map.112 = (f32[64,1024]{1,0:T(8,128)S(1)}, f32[64,1024]{1,0:T(8,128)S(1)}) custom-call(f32[64,1024]{1,0:T(8,128)S(1)} %get-tuple-element.44.h_ref, f32[64,1024]{1,0:T(8,128)S(1)} %get-tuple-element.45.mx_ref, f32[64,1024]{1,0:T(8,128)S(1)} %shard_map.103.wd_ref.own_wd_ref.refs_1_, f32[8,128,128]{2,1,0:T(8,128)S(1)} %bitcast.12), custom_call_target="tpu_custom_call" | custom-call | flops 67108864 | bytes 1835008 | tf_op jit(solution)/shard_map/pallas_call | solution.py:42
  39.3 0.0 collective-permute-done.10.odd_ref.other_ref
  39.3 0.0 collective-permute-done.9.even_ref
  39.3 0.3 shard_map.114
  39.7 0.1 collective-permute-start.12
  39.7 1.0 %shard_map.113 = (f32[64,1024]{1,0:T(8,128)}, f32[64,1024]{1,0:T(8,128)}, f32[64,1024]{1,0:T(8,128)}, f32[16,1024]{1,0:T(8,128)S(1)}, f32[8,1024]{1,0:T(8,128)S(1)}) custom-call(f32[128,1024]{1,0:T(8,128)S(1)} %get-tuple-element.42.flow_ref, f32[4,1024]{1,0:T(4,128)S(1)} %collective-permute-done.9.even_ref, ...), custom_call_target="tpu_custom_call" | custom-call | bytes 2555904 | tf_op jit(solution)/shard_map/pallas_call | solution.py:42
  40.8 0.0 collective-permute-done.11.above2_ref
  40.8 0.1 collective-permute-done.12.packet_ref
  40.9 0.7 %shard_map.115 = f32[64,1024]{1,0:T(8,128)} custom-call(f32[64,1024]{1,0:T(8,128)} %get-tuple-element.48.h_in, f32[16,1024]{1,0:T(8,128)S(1)} %get-tuple-element.49.edge_ref, f32[8,1024]{1,0:T(8,128)S(1)} %get-tuple-element.50.before_ref, f32[4,1024]{1,0:T(4,128)S(1)} %get-tuple-element.43.msg_ref, ...), custom_call_target="tpu_custom_call", output_to_operand_aliasing={{}: (0, {})} | custom-call | bytes 417792 | tf_op jit(solution)/shard_map/pallas_call | solution.py:42
  (1 shorter events, 0.0 us)
Async XLA Ops:
  1.8 11.9 %collective-permute-start.1 = (f32[64,1024]{1,0:T(8,128)S(1)}, f32[64,1024]{1,0:T(8,128)S(1)}, u32[]{:S(2)}, u32[]{:S(2)}) collective-permute-start(f32[64,1024]{1,0:T(8,128)S(1)} %shard_map.103.wd_ref.own_wd_ref.refs_1_), channel_id=1, source_target_pairs={{0,1},{1,0},{2,3},{3,2},{4,5},{5,4},{6,7},{7,6},{8,9},{9,8},{10,11... | collective-permute-start | bytes 786440 | tf_op jit(solution)/shard_map/ppermute | solution.py:26
  4.8 7.2 %copy-start = (f32[1,8,128,128]{3,2,1,0:T(8,128)S(1)}, f32[1,8,128,128]{3,2,1,0:T(8,128)}, u32[]{:S(2)}) copy-start(f32[1,8,128,128]{3,2,1,0:T(8,128)} %param.13) | copy-start | bytes 1572868
  6.3 11.1 %collective-permute-start = (f32[72,1024]{1,0:T(8,128)S(1)}, f32[72,1024]{1,0:T(8,128)S(1)}, u32[]{:S(2)}, u32[]{:S(2)}) collective-permute-start(f32[72,1024]{1,0:T(8,128)S(1)} %get-tuple-element.29.refs_0_), channel_id=1, source_target_pairs={{0,1},{1,0},{2,3},{3,2},{4,5},{5,4},{6,7},{7,6},{8,9},{9,8},{10,11... | collective-permute-start | bytes 884744 | tf_op jit(solution)/shard_map/ppermute | solution.py:26
  6.4 5.6 %collective-permute-start.3 = (f32[4,1024]{1,0:T(4,128)S(1)}, f32[4,1024]{1,0:T(4,128)S(1)}, u32[]{:S(2)}, u32[]{:S(2)}) collective-permute-start(f32[4,1024]{1,0:T(4,128)S(1)} %get-tuple-element.30), channel_id=1, source_target_pairs={{1,3},{2,0},{3,5},{4,2},{5,7},{6,4},{7,9},{8,6},{9,11},{10,8},{11,... | collective-permute-start | bytes 49160 | tf_op jit(solution)/shard_map/ppermute | solution.py:22
  7.7 6.3 %collective-permute-start.2 = (f32[4,1024]{1,0:T(4,128)S(1)}, f32[4,1024]{1,0:T(4,128)S(1)}, u32[]{:S(2)}, u32[]{:S(2)}) collective-permute-start(f32[4,1024]{1,0:T(4,128)S(1)} %get-tuple-element.30), channel_id=1, source_target_pairs={{1,2},{2,1},{3,4},{4,3},{5,6},{6,5},{7,8},{8,7},{9,10},{10,9},{11,... | collective-permute-start | bytes 49160 | tf_op jit(solution)/shard_map/ppermute | solution.py:22
  18.2 3.8 %collective-permute-start.4 = (f32[4,1024]{1,0:T(4,128)S(1)}, f32[4,1024]{1,0:T(4,128)S(1)}, u32[]{:S(2)}, u32[]{:S(2)}) collective-permute-start(f32[4,1024]{1,0:T(4,128)S(1)} %get-tuple-element.37.msg_ref.refs_2_), channel_id=1, source_target_pairs={{0,2},{1,3},{2,0},{3,1},{4,6},{5,7},{6,4},{7,5},{8,10},{9,11},{10,... | collective-permute-start | bytes 49160 | tf_op jit(solution)/shard_map/ppermute | solution.py:22
  20.3 7.4 %copy-start.1 = (s32[2,2,1024]{2,1,0:T(2,128)S(1)}, s32[2,2,1024]{2,1,0:T(2,128)}, u32[]{:S(2)}) copy-start(s32[2,2,1024]{2,1,0:T(2,128)} %map_ref.3) | copy-start | bytes 49156
  20.3 7.4 %collective-permute-start.7 = (f32[64,1024]{1,0:T(8,128)S(1)}, f32[64,1024]{1,0:T(8,128)S(1)}, u32[]{:S(2)}, u32[]{:S(2)}) collective-permute-start(f32[64,1024]{1,0:T(8,128)S(1)} %get-tuple-element.41.hx_ref.refs_8_), channel_id=1, source_target_pairs={{0,1},{1,0},{2,3},{3,2},{4,5},{5,4},{6,7},{7,6},{8,9},{9,8},{10,11... | collective-permute-start | bytes 786440 | tf_op jit(solution)/shard_map/ppermute | solution.py:26
  22.1 6.8 %collective-permute-start.5 = (f32[4,1024]{1,0:T(4,128)S(1)}, f32[4,1024]{1,0:T(4,128)S(1)}, u32[]{:S(2)}, u32[]{:S(2)}) collective-permute-start(f32[4,1024]{1,0:T(4,128)S(1)} %shard_map.108), channel_id=1, source_target_pairs={{4,8},{5,9},{6,10},{7,11},{8,4},{9,5},{10,6},{11,7},{20,24},{21,25... | collective-permute-start | bytes 49160 | tf_op jit(solution)/shard_map/ppermute | solution.py:22
  22.7 6.7 %collective-permute-start.6 = (f32[4,1024]{1,0:T(4,128)S(1)}, f32[4,1024]{1,0:T(4,128)S(1)}, u32[]{:S(2)}, u32[]{:S(2)}) collective-permute-start(f32[4,1024]{1,0:T(4,128)S(1)} %shard_map.108), channel_id=1, source_target_pairs={{0,4},{1,5},{2,6},{3,7},{4,0},{5,1},{6,2},{7,3},{8,12},{9,13},{10,... | collective-permute-start | bytes 49160 | tf_op jit(solution)/shard_map/ppermute | solution.py:22
  28.1 1.4 %collective-permute-start.8 = (f32[1,1024]{1,0:T(1,128)S(1)}, f32[1,1024]{1,0:T(1,128)S(1)}, u32[]{:S(2)}, u32[]{:S(2)}) collective-permute-start(f32[1,1024]{1,0:T(1,128)S(1)} %shard_map.110), channel_id=1, source_target_pairs={{0,16},{16,0},{1,17},{17,1},{2,18},{18,2},{3,19},{19,3},{4,20},{20... | collective-permute-start | bytes 12296 | tf_op jit(solution)/shard_map/ppermute | solution.py:30
  30.6 8.7 %collective-permute-start.10 = (f32[4,1024]{1,0:T(4,128)S(1)}, f32[4,1024]{1,0:T(4,128)S(1)}, u32[]{:S(2)}, u32[]{:S(2)}) collective-permute-start(f32[4,1024]{1,0:T(4,128)S(1)} %get-tuple-element.43.msg_ref), channel_id=1, source_target_pairs={{2,4},{3,5},{4,2},{5,3},{6,8},{7,9},{8,6},{9,7},{10,12},{11,13},{1... | collective-permute-start | bytes 49160 | tf_op jit(solution)/shard_map/ppermute | solution.py:22
  31.2 8.1 %collective-permute-start.9 = (f32[4,1024]{1,0:T(4,128)S(1)}, f32[4,1024]{1,0:T(4,128)S(1)}, u32[]{:S(2)}, u32[]{:S(2)}) collective-permute-start(f32[4,1024]{1,0:T(4,128)S(1)} %get-tuple-element.43.msg_ref), channel_id=1, source_target_pairs={{0,2},{1,3},{2,0},{3,1},{4,6},{5,7},{6,4},{7,5},{8,10},{9,11},{10,... | collective-permute-start | bytes 49160 | tf_op jit(solution)/shard_map/ppermute | solution.py:22
  36.0 4.8 %collective-permute-start.11 = (f32[1,1024]{1,0:T(1,128)S(1)}, f32[1,1024]{1,0:T(1,128)S(1)}, u32[]{:S(2)}, u32[]{:S(2)}) collective-permute-start(f32[1,1024]{1,0:T(1,128)S(1)} %get-tuple-element.51), channel_id=1, source_target_pairs={{0,4},{2,6},{4,8},{6,10},{8,12},{10,14},{16,20},{18,22},{20,24},{2... | collective-permute-start | bytes 12296 | tf_op jit(solution)/shard_map/ppermute | solution.py:22
  39.7 1.2 %collective-permute-start.12 = (f32[1,1024]{1,0:T(1,128)S(1)}, f32[1,1024]{1,0:T(1,128)S(1)}, u32[]{:S(2)}, u32[]{:S(2)}) collective-permute-start(f32[1,1024]{1,0:T(1,128)S(1)} %shard_map.114), channel_id=1, source_target_pairs={{0,16},{16,0},{1,17},{17,1},{2,18},{18,2},{3,19},{19,3},{4,20},{20... | collective-permute-start | bytes 12296 | tf_op jit(solution)/shard_map/ppermute | solution.py:30

commit v6 on v5

--- a/solution.py
+++ b/solution.py
@@ -484,7 +484,7 @@
     odd = moved(msg, lambda k, s: (((k + 1) ^ 1) - 1, s))
     above2 = moved(u_down, lambda k, s: (k + 2, s) if s == 0 else None)
     flow_x, hx = call(across, [(n, width), (n, width)], [height, flow_x, wd, table_x], [part, part], solve_flops)
-    (packet,) = call(packet_body, [(1, width)], [nest, even, nest_map, hx, odd])
+    (packet,) = call(packet_body, [(1, width)], [nest, even, nest_map, hx, even])
     packet = swap_nest(packet)
     flow_y, flow_x, height, edge, before = call(
         finish_body, [(n, width), (n, width), (n, width), (16, width), (8, width)],

time: 41.9 us -> 41.4 us (0.988)
  starting transfers between devices: 22.4 us -> 21.9 us
    ppermute x8, starting transfers between devices: 17.6 us -> 17.1 us  [moved(): return lax.ppermute(value, LINE, pairs)]
where the time goes in v6:
time: 41.4 us; the launch traced here: 41.1 us
  starting transfers between devices  21.9 us (53%)
  Pallas kernels  10.4 us (25%)
  waiting for transfers between devices  8.03 us (19%)
  between operations  0.8 us (2%)
    ppermute x8, starting transfers between devices, moved(): return lax.ppermute(value, LINE, pairs)  17.1 us
    pallas_call x13, Pallas kernels, call(): pl.pallas_call(body, out_shape=shapes, in_specs=[spec(i, x, far) for i, x...  10.4 us
    ppermute x3, starting transfers between devices, swap_halves(): return lax.ppermute(value, 'sub', [(0, 1), (1, 0)])  4.65 us
    ppermute x8, waiting for transfers between devices, moved(): return lax.ppermute(value, LINE, pairs)  4.48 us
    ppermute x3, waiting for transfers between devices, swap_halves(): return lax.ppermute(value, 'sub', [(0, 1), (1, 0)])  3.48 us
  transfers between devices with their start and end apart: 13, of which 5 were waited for; matrix products, arithmetic and copies ran while one was open for 0% of the time, Pallas kernels for 16%

profile of v6, /device:TPU:0, one launch (start us, length us, event | category | flops | bytes accessed | tf_op | source)
XLA Modules:
  0.0 41.1 jit_solution(12859982882023327298)
XLA Ops:
  0.6 1.2 %shard_map.103.wd_ref.own_wd_ref.refs_1_ = f32[64,1024]{1,0:T(8,128)S(1)} custom-call(f32[64,1024]{1,0:T(8,128)} %bitcast.14, s32[64,1024]{1,0:T(8,128)} %bitcast.15), custom_call_target="tpu_custom_call" | custom-call | bytes 262144 | tf_op jit(solution)/shard_map/pallas_call | solution.py:42
  1.8 3.0 %collective-permute-start.1 = (f32[64,1024]{1,0:T(8,128)S(1)}, f32[64,1024]{1,0:T(8,128)S(1)}, u32[]{:S(2)}, u32[]{:S(2)}) collective-permute-start(f32[64,1024]{1,0:T(8,128)S(1)} %shard_map.103.wd_ref.own_wd_ref.refs_1_), channel_id=1, source_target_pairs={{0,1},{1,0},{2,3},{3,2},{4,5},{5,4},{6,7},{7,6},{8,9},{9,8},{10,11... | collective-permute-start | bytes 786440 | tf_op jit(solution)/shard_map/ppermute | solution.py:26
  4.8 0.0 copy-start
  4.8 1.5 %shard_map.104 = (f32[72,1024]{1,0:T(8,128)S(1)}, f32[4,1024]{1,0:T(4,128)S(1)}, f32[64,1024]{1,0:T(8,128)S(1)}, f32[64,1024]{1,0:T(8,128)S(1)}) custom-call(f32[64,1024]{1,0:T(8,128)} %bitcast.16, f32[64,1024]{1,0:T(8,128)} %bitcast.17, f32[64,1024]{1,0:T(8,128)} %bitcast.18, f32[64,1024]{1,0:T(8,128)S(1)} %shard_map.103.wd_ref.own_wd_ref.refs_1_), custom_call_target="tpu_custom_call" | custom-call | bytes 1097728 | tf_op jit(solution)/shard_map/pallas_call | solution.py:42
  6.3 0.1 collective-permute-start
  6.4 1.3 %collective-permute-start.3 = (f32[4,1024]{1,0:T(4,128)S(1)}, f32[4,1024]{1,0:T(4,128)S(1)}, u32[]{:S(2)}, u32[]{:S(2)}) collective-permute-start(f32[4,1024]{1,0:T(4,128)S(1)} %get-tuple-element.30), channel_id=1, source_target_pairs={{1,3},{2,0},{3,5},{4,2},{5,7},{6,4},{7,9},{8,6},{9,11},{10,8},{11,... | collective-permute-start | bytes 49160 | tf_op jit(solution)/shard_map/ppermute | solution.py:22
  7.7 0.7 %collective-permute-start.2 = (f32[4,1024]{1,0:T(4,128)S(1)}, f32[4,1024]{1,0:T(4,128)S(1)}, u32[]{:S(2)}, u32[]{:S(2)}) collective-permute-start(f32[4,1024]{1,0:T(4,128)S(1)} %get-tuple-element.30), channel_id=1, source_target_pairs={{1,2},{2,1},{3,4},{4,3},{5,6},{6,5},{7,8},{8,7},{9,10},{10,9},{11,... | collective-permute-start | bytes 49160 | tf_op jit(solution)/shard_map/ppermute | solution.py:22
  8.4 3.7 %collective-permute-done.3.along_ref.refs_5_ = f32[4,1024]{1,0:T(4,128)S(1)} collective-permute-done((f32[4,1024]{1,0:T(4,128)S(1)}, f32[4,1024]{1,0:T(4,128)S(1)}, u32[]{:S(2)}, u32[]{:S(2)}) %collective-permute-start.3) | collective-permute-done | bytes 16416 | tf_op jit(solution)/shard_map/ppermute | solution.py:22
  12.0 0.0 copy-done
  12.0 1.7 %shard_map.105 = (f32[64,1024]{1,0:T(8,128)S(1)}, f32[64,1024]{1,0:T(8,128)S(1)}, f32[128,128]{1,0:T(8,128)S(1)}, f32[16,128]{1,0:T(8,128)S(1)}) custom-call(f32[64,1024]{1,0:T(8,128)S(1)} %get-tuple-element.31.h_ref, f32[64,1024]{1,0:T(8,128)S(1)} %get-tuple-element.32.mx_ref, f32[64,1024]{1,0:T(8,128)S(1)} %shard_map.103.wd_ref.own_wd_ref.refs_1_, ...), custom_call_target="tpu_custom_call" | custom-call | flops 67108864 | bytes 1925120 | tf_op jit(solution)/shard_map/pallas_call | solution.py:42
  13.7 0.0 collective-permute-done.1.other_wd_ref.refs_3_
  13.7 0.3 shard_map.106.refs_8_
  14.0 0.0 collective-permute-done.2.refs_4_.cross_ref
  14.0 3.5 %collective-permute-done.refs_2_ = f32[72,1024]{1,0:T(8,128)S(1)} collective-permute-done((f32[72,1024]{1,0:T(8,128)S(1)}, f32[72,1024]{1,0:T(8,128)S(1)}, u32[]{:S(2)}, u32[]{:S(2)}) %collective-permute-start) | collective-permute-done | bytes 294944 | tf_op jit(solution)/shard_map/ppermute | solution.py:26
  17.5 0.7 %shard_map.107 = (f32[128,1024]{1,0:T(8,128)S(1)}, f32[128,1024]{1,0:T(8,128)S(1)}, f32[4,1024]{1,0:T(4,128)S(1)}, f32[8,1024]{1,0:T(8,128)S(1)}, f32[8,1024]{1,0:T(8,128)S(1)}) custom-call(f32[72,1024]{1,0:T(8,128)S(1)} %get-tuple-element.29.refs_0_, f32[64,1024]{1,0:T(8,128)S(1)} %shard_map.103.wd_ref.own_wd_ref.refs_1_, ...), custom_call_target="tpu_custom_call" | custom-call | flops 67108864 | bytes 2875392 | tf_op jit(solution)/shard_map/pallas_call | solution.py:42
  18.2 2.1 %collective-permute-start.4 = (f32[4,1024]{1,0:T(4,128)S(1)}, f32[4,1024]{1,0:T(4,128)S(1)}, u32[]{:S(2)}, u32[]{:S(2)}) collective-permute-start(f32[4,1024]{1,0:T(4,128)S(1)} %get-tuple-element.37.msg_ref.refs_2_), channel_id=1, source_target_pairs={{0,2},{1,3},{2,0},{3,1},{4,6},{5,7},{6,4},{7,5},{8,10},{9,11},{10,... | collective-permute-start | bytes 49160 | tf_op jit(solution)/shard_map/ppermute | solution.py:22
  20.3 0.0 copy-start.1
  20.3 1.5 %collective-permute-start.7 = (f32[64,1024]{1,0:T(8,128)S(1)}, f32[64,1024]{1,0:T(8,128)S(1)}, u32[]{:S(2)}, u32[]{:S(2)}) collective-permute-start(f32[64,1024]{1,0:T(8,128)S(1)} %get-tuple-element.41.hx_ref.refs_8_), channel_id=1, source_target_pairs={{0,1},{1,0},{2,3},{3,2},{4,5},{5,4},{6,7},{7,6},{8,9},{9,8},{10,11... | collective-permute-start | bytes 786440 | tf_op jit(solution)/shard_map/ppermute | solution.py:26
  21.9 0.2 collective-permute-done.4.even_ref.refs_5_
  22.1 0.7 %collective-permute-start.5 = (f32[4,1024]{1,0:T(4,128)S(1)}, f32[4,1024]{1,0:T(4,128)S(1)}, u32[]{:S(2)}, u32[]{:S(2)}) collective-permute-start(f32[4,1024]{1,0:T(4,128)S(1)} %shard_map.108), channel_id=1, source_target_pairs={{4,8},{5,9},{6,10},{7,11},{8,4},{9,5},{10,6},{11,7},{20,24},{21,25... | collective-permute-start | bytes 49160 | tf_op jit(solution)/shard_map/ppermute | solution.py:22
  22.7 5.0 %collective-permute-start.6 = (f32[4,1024]{1,0:T(4,128)S(1)}, f32[4,1024]{1,0:T(4,128)S(1)}, u32[]{:S(2)}, u32[]{:S(2)}) collective-permute-start(f32[4,1024]{1,0:T(4,128)S(1)} %shard_map.108), channel_id=1, source_target_pairs={{0,4},{1,5},{2,6},{3,7},{4,0},{5,1},{6,2},{7,3},{8,12},{9,13},{10,... | collective-permute-start | bytes 49160 | tf_op jit(solution)/shard_map/ppermute | solution.py:22
  27.7 0.0 collective-permute-done.7.other_ref.refs_9_
  27.7 0.0 copy-done.1
  27.7 0.3 shard_map.110
  28.1 0.1 collective-permute-start.8
  28.2 0.7 %shard_map.109.refs_10_ = f32[8,1024]{1,0:T(8,128)S(1)} custom-call(f32[4,1024]{1,0:T(4,128)S(1)} %collective-permute-done.2.refs_4_.cross_ref, f32[4,1024]{1,0:T(4,128)S(1)} %collective-permute-done.3.along_ref.refs_5_, f32[8,128,128]{2,1,0:T(8,128)S(1)} %bitcast.11), custom_call_target="tpu_custom_call" | custom-call | bytes 589824 | tf_op jit(solution)/shard_map/pallas_call | solution.py:42
  28.8 0.0 collective-permute-done.5.refs_6_
  28.8 0.6 %collective-permute-done.6.refs_7_ = f32[4,1024]{1,0:T(4,128)S(1)} collective-permute-done((f32[4,1024]{1,0:T(4,128)S(1)}, f32[4,1024]{1,0:T(4,128)S(1)}, u32[]{:S(2)}, u32[]{:S(2)}) %collective-permute-start.6) | collective-permute-done | bytes 16416 | tf_op jit(solution)/shard_map/ppermute | solution.py:22
  29.5 0.0 collective-permute-done.8.refs_11_
  29.5 1.1 %shard_map.111 = (f32[64,1024]{1,0:T(8,128)S(1)}, f32[128,1024]{1,0:T(8,128)S(1)}, f32[4,1024]{1,0:T(4,128)S(1)}, f32[8,1024]{1,0:T(8,128)S(1)}, f32[1,1024]{1,0:T(1,128)S(1)}) custom-call(f32[128,1024]{1,0:T(8,128)S(1)} %get-tuple-element.35.refs_0_, f32[128,1024]{1,0:T(8,128)S(1)} %get-tuple-element.36.refs_1_.face_ref, ...), custom_call_target="tpu_custom_call" | custom-call | flops 67108864 | bytes 2646016 | tf_op jit(solution)/shard_map/pallas_call | solution.py:42
  30.6 1.6 %collective-permute-start.9 = (f32[4,1024]{1,0:T(4,128)S(1)}, f32[4,1024]{1,0:T(4,128)S(1)}, u32[]{:S(2)}, u32[]{:S(2)}) collective-permute-start(f32[4,1024]{1,0:T(4,128)S(1)} %get-tuple-element.43.msg_ref), channel_id=1, source_target_pairs={{0,2},{1,3},{2,0},{3,1},{4,6},{5,7},{6,4},{7,5},{8,10},{9,11},{10,... | collective-permute-start | bytes 49160 | tf_op jit(solution)/shard_map/ppermute | solution.py:22
  32.1 0.7 %collective-permute-start.10 = (f32[4,1024]{1,0:T(4,128)S(1)}, f32[4,1024]{1,0:T(4,128)S(1)}, u32[]{:S(2)}, u32[]{:S(2)}) collective-permute-start(f32[4,1024]{1,0:T(4,128)S(1)} %get-tuple-element.43.msg_ref), channel_id=1, source_target_pairs={{2,4},{3,5},{4,2},{5,3},{6,8},{7,9},{8,6},{9,7},{10,12},{11,13},{1... | collective-permute-start | bytes 49160 | tf_op jit(solution)/shard_map/ppermute | solution.py:22
  32.8 5.2 %collective-permute-start.11 = (f32[1,1024]{1,0:T(1,128)S(1)}, f32[1,1024]{1,0:T(1,128)S(1)}, u32[]{:S(2)}, u32[]{:S(2)}) collective-permute-start(f32[1,1024]{1,0:T(1,128)S(1)} %get-tuple-element.51), channel_id=1, source_target_pairs={{0,4},{2,6},{4,8},{6,10},{8,12},{10,14},{16,20},{18,22},{20,24},{2... | collective-permute-start | bytes 12296 | tf_op jit(solution)/shard_map/ppermute | solution.py:22
  38.0 0.9 %shard_map.112 = (f32[64,1024]{1,0:T(8,128)S(1)}, f32[64,1024]{1,0:T(8,128)S(1)}) custom-call(f32[64,1024]{1,0:T(8,128)S(1)} %get-tuple-element.44.h_ref, f32[64,1024]{1,0:T(8,128)S(1)} %get-tuple-element.45.mx_ref, f32[64,1024]{1,0:T(8,128)S(1)} %shard_map.103.wd_ref.own_wd_ref.refs_1_, f32[8,128,128]{2,1,0:T(8,128)S(1)} %bitcast.12), custom_call_target="tpu_custom_call" | custom-call | flops 67108864 | bytes 1835008 | tf_op jit(solution)/shard_map/pallas_call | solution.py:42
  38.8 0.0 collective-permute-done.9.even_ref.other_ref
  38.9 0.3 shard_map.114
  39.2 0.1 collective-permute-start.12
  39.3 0.0 collective-permute-done.10.odd_ref
  39.3 1.0 %shard_map.113 = (f32[64,1024]{1,0:T(8,128)}, f32[64,1024]{1,0:T(8,128)}, f32[64,1024]{1,0:T(8,128)}, f32[16,1024]{1,0:T(8,128)S(1)}, f32[8,1024]{1,0:T(8,128)S(1)}) custom-call(f32[128,1024]{1,0:T(8,128)S(1)} %get-tuple-element.42.flow_ref, f32[4,1024]{1,0:T(4,128)S(1)} %collective-permute-done.9.even_ref.other_ref, ...), custom_call_target="tpu_custom_call" | custom-call | bytes 2555904 | tf_op jit(solution)/shard_map/pallas_call | solution.py:42
  40.3 0.0 collective-permute-done.11.above2_ref
  40.4 0.1 collective-permute-done.12.packet_ref
  40.4 0.7 %shard_map.115 = f32[64,1024]{1,0:T(8,128)} custom-call(f32[64,1024]{1,0:T(8,128)} %get-tuple-element.48.h_in, f32[16,1024]{1,0:T(8,128)S(1)} %get-tuple-element.49.edge_ref, f32[8,1024]{1,0:T(8,128)S(1)} %get-tuple-element.50.before_ref, f32[4,1024]{1,0:T(4,128)S(1)} %get-tuple-element.43.msg_ref, ...), custom_call_target="tpu_custom_call", output_to_operand_aliasing={{}: (0, {})} | custom-call | bytes 417792 | tf_op jit(solution)/shard_map/pallas_call | solution.py:42
  (1 shorter events, 0.0 us)
Async XLA Ops:
  1.8 11.9 %collective-permute-start.1 = (f32[64,1024]{1,0:T(8,128)S(1)}, f32[64,1024]{1,0:T(8,128)S(1)}, u32[]{:S(2)}, u32[]{:S(2)}) collective-permute-start(f32[64,1024]{1,0:T(8,128)S(1)} %shard_map.103.wd_ref.own_wd_ref.refs_1_), channel_id=1, source_target_pairs={{0,1},{1,0},{2,3},{3,2},{4,5},{5,4},{6,7},{7,6},{8,9},{9,8},{10,11... | collective-permute-start | bytes 786440 | tf_op jit(solution)/shard_map/ppermute | solution.py:26
  4.8 7.2 %copy-start = (f32[1,8,128,128]{3,2,1,0:T(8,128)S(1)}, f32[1,8,128,128]{3,2,1,0:T(8,128)}, u32[]{:S(2)}) copy-start(f32[1,8,128,128]{3,2,1,0:T(8,128)} %param.13) | copy-start | bytes 1572868
  6.3 11.1 %collective-permute-start = (f32[72,1024]{1,0:T(8,128)S(1)}, f32[72,1024]{1,0:T(8,128)S(1)}, u32[]{:S(2)}, u32[]{:S(2)}) collective-permute-start(f32[72,1024]{1,0:T(8,128)S(1)} %get-tuple-element.29.refs_0_), channel_id=1, source_target_pairs={{0,1},{1,0},{2,3},{3,2},{4,5},{5,4},{6,7},{7,6},{8,9},{9,8},{10,11... | collective-permute-start | bytes 884744 | tf_op jit(solution)/shard_map/ppermute | solution.py:26
  6.4 5.6 %collective-permute-start.3 = (f32[4,1024]{1,0:T(4,128)S(1)}, f32[4,1024]{1,0:T(4,128)S(1)}, u32[]{:S(2)}, u32[]{:S(2)}) collective-permute-start(f32[4,1024]{1,0:T(4,128)S(1)} %get-tuple-element.30), channel_id=1, source_target_pairs={{1,3},{2,0},{3,5},{4,2},{5,7},{6,4},{7,9},{8,6},{9,11},{10,8},{11,... | collective-permute-start | bytes 49160 | tf_op jit(solution)/shard_map/ppermute | solution.py:22
  7.7 6.3 %collective-permute-start.2 = (f32[4,1024]{1,0:T(4,128)S(1)}, f32[4,1024]{1,0:T(4,128)S(1)}, u32[]{:S(2)}, u32[]{:S(2)}) collective-permute-start(f32[4,1024]{1,0:T(4,128)S(1)} %get-tuple-element.30), channel_id=1, source_target_pairs={{1,2},{2,1},{3,4},{4,3},{5,6},{6,5},{7,8},{8,7},{9,10},{10,9},{11,... | collective-permute-start | bytes 49160 | tf_op jit(solution)/shard_map/ppermute | solution.py:22
  18.2 3.8 %collective-permute-start.4 = (f32[4,1024]{1,0:T(4,128)S(1)}, f32[4,1024]{1,0:T(4,128)S(1)}, u32[]{:S(2)}, u32[]{:S(2)}) collective-permute-start(f32[4,1024]{1,0:T(4,128)S(1)} %get-tuple-element.37.msg_ref.refs_2_), channel_id=1, source_target_pairs={{0,2},{1,3},{2,0},{3,1},{4,6},{5,7},{6,4},{7,5},{8,10},{9,11},{10,... | collective-permute-start | bytes 49160 | tf_op jit(solution)/shard_map/ppermute | solution.py:22
  20.3 7.4 %copy-start.1 = (s32[2,2,1024]{2,1,0:T(2,128)S(1)}, s32[2,2,1024]{2,1,0:T(2,128)}, u32[]{:S(2)}) copy-start(s32[2,2,1024]{2,1,0:T(2,128)} %map_ref.3) | copy-start | bytes 49156
  20.3 7.4 %collective-permute-start.7 = (f32[64,1024]{1,0:T(8,128)S(1)}, f32[64,1024]{1,0:T(8,128)S(1)}, u32[]{:S(2)}, u32[]{:S(2)}) collective-permute-start(f32[64,1024]{1,0:T(8,128)S(1)} %get-tuple-element.41.hx_ref.refs_8_), channel_id=1, source_target_pairs={{0,1},{1,0},{2,3},{3,2},{4,5},{5,4},{6,7},{7,6},{8,9},{9,8},{10,11... | collective-permute-start | bytes 786440 | tf_op jit(solution)/shard_map/ppermute | solution.py:26
  22.1 6.8 %collective-permute-start.5 = (f32[4,1024]{1,0:T(4,128)S(1)}, f32[4,1024]{1,0:T(4,128)S(1)}, u32[]{:S(2)}, u32[]{:S(2)}) collective-permute-start(f32[4,1024]{1,0:T(4,128)S(1)} %shard_map.108), channel_id=1, source_target_pairs={{4,8},{5,9},{6,10},{7,11},{8,4},{9,5},{10,6},{11,7},{20,24},{21,25... | collective-permute-start | bytes 49160 | tf_op jit(solution)/shard_map/ppermute | solution.py:22
  22.7 6.7 %collective-permute-start.6 = (f32[4,1024]{1,0:T(4,128)S(1)}, f32[4,1024]{1,0:T(4,128)S(1)}, u32[]{:S(2)}, u32[]{:S(2)}) collective-permute-start(f32[4,1024]{1,0:T(4,128)S(1)} %shard_map.108), channel_id=1, source_target_pairs={{0,4},{1,5},{2,6},{3,7},{4,0},{5,1},{6,2},{7,3},{8,12},{9,13},{10,... | collective-permute-start | bytes 49160 | tf_op jit(solution)/shard_map/ppermute | solution.py:22
  28.1 1.4 %collective-permute-start.8 = (f32[1,1024]{1,0:T(1,128)S(1)}, f32[1,1024]{1,0:T(1,128)S(1)}, u32[]{:S(2)}, u32[]{:S(2)}) collective-permute-start(f32[1,1024]{1,0:T(1,128)S(1)} %shard_map.110), channel_id=1, source_target_pairs={{0,16},{16,0},{1,17},{17,1},{2,18},{18,2},{3,19},{19,3},{4,20},{20... | collective-permute-start | bytes 12296 | tf_op jit(solution)/shard_map/ppermute | solution.py:30
  30.6 8.3 %collective-permute-start.9 = (f32[4,1024]{1,0:T(4,128)S(1)}, f32[4,1024]{1,0:T(4,128)S(1)}, u32[]{:S(2)}, u32[]{:S(2)}) collective-permute-start(f32[4,1024]{1,0:T(4,128)S(1)} %get-tuple-element.43.msg_ref), channel_id=1, source_target_pairs={{0,2},{1,3},{2,0},{3,1},{4,6},{5,7},{6,4},{7,5},{8,10},{9,11},{10,... | collective-permute-start | bytes 49160 | tf_op jit(solution)/shard_map/ppermute | solution.py:22
  32.1 7.1 %collective-permute-start.10 = (f32[4,1024]{1,0:T(4,128)S(1)}, f32[4,1024]{1,0:T(4,128)S(1)}, u32[]{:S(2)}, u32[]{:S(2)}) collective-permute-start(f32[4,1024]{1,0:T(4,128)S(1)} %get-tuple-element.43.msg_ref), channel_id=1, source_target_pairs={{2,4},{3,5},{4,2},{5,3},{6,8},{7,9},{8,6},{9,7},{10,12},{11,13},{1... | collective-permute-start | bytes 49160 | tf_op jit(solution)/shard_map/ppermute | solution.py:22
  32.8 7.6 %collective-permute-start.11 = (f32[1,1024]{1,0:T(1,128)S(1)}, f32[1,1024]{1,0:T(1,128)S(1)}, u32[]{:S(2)}, u32[]{:S(2)}) collective-permute-start(f32[1,1024]{1,0:T(1,128)S(1)} %get-tuple-element.51), channel_id=1, source_target_pairs={{0,4},{2,6},{4,8},{6,10},{8,12},{10,14},{16,20},{18,22},{20,24},{2... | collective-permute-start | bytes 12296 | tf_op jit(solution)/shard_map/ppermute | solution.py:22
  39.2 1.2 %collective-permute-start.12 = (f32[1,1024]{1,0:T(1,128)S(1)}, f32[1,1024]{1,0:T(1,128)S(1)}, u32[]{:S(2)}, u32[]{:S(2)}) collective-permute-start(f32[1,1024]{1,0:T(1,128)S(1)} %shard_map.114), channel_id=1, source_target_pairs={{0,16},{16,0},{1,17},{17,1},{2,18},{18,2},{3,19},{19,3},{4,20},{20... | collective-permute-start | bytes 12296 | tf_op jit(solution)/shard_map/ppermute | solution.py:30
